TPU v7x, 128 devices: a whole 4x4x4 slice. The times are simulated.
128 devices in a mesh: gx: 8 (over x, y_hi), gy: 16 (over z, y_lo, core).
Axes of the slice: x: 4, y: 4 (y_hi: 2, y_lo: 2; y = y_hi * 2 + y_lo), z: 4, core: 2. Of those that a mesh axis runs over, the one named last changes fastest.
Arguments:
- features: bfloat16 [16, 256, 256, 128], P(None, 'gx', 'gy'), may hold values from -24 to 24
- w_first: bfloat16 [27, 16, 16], replicated, may hold values from -0.3125 to 0.3125
- w_second: bfloat16 [27, 16, 16], replicated, may hold values from -0.3125 to 0.3125
- w_lift: bfloat16 [512, 16], replicated, may hold values from -1.5 to 1.5
- w_coarse: bfloat16 [512, 27, 512], P('gy'), may hold values from -0.0546875 to 0.0546875
- w_decode: bfloat16 [16, 512], replicated, may hold values from -0.25 to 0.25
- w_joining: bfloat16 [16, 32], replicated, may hold values from -1 to 1
Outputs:
- joined: bfloat16 [16, 256, 256, 128], P(None, 'gx', 'gy')
All inputs are finite; a program needn't handle non-finite values.
Results may differ from a plain program's by a relative error of at most 0.0065.
Values may be sent and summed in bfloat16 or wider, within the bound.
No kernel may reach another device: no remote copies, remote signals or barrier semaphores. Data moves between devices by JAX's collectives and lax.ppermute only.
A program may use at most 192 MiB of HBM per device.

v0:
```python
import jax
import jax.numpy as jnp
from jax import lax
from jax.experimental import pallas as pl
from jax.experimental.pallas import tpu as pltpu
from jax.sharding import PartitionSpec as P

POOL = 16
F32 = jnp.float32
BF16 = jnp.bfloat16
VMEM = pl.BlockSpec(memory_space=pltpu.VMEM)
LIMIT = 12 << 20


def iota(shape, dim):
    return lax.broadcasted_iota(jnp.int32, shape, dim)


def dot(a, b):
    return jnp.dot(a, b, preferred_element_type=F32)


def shape(*dims, dtype=BF16):
    return jax.ShapeDtypeStruct(dims, dtype)


def vmem_call(kernel, out_shape, args, scratch=(), flops=0, nbytes=0, aliases={}):
    single = not isinstance(out_shape, (list, tuple))
    return pl.pallas_call(
        kernel,
        out_shape=out_shape,
        in_specs=[VMEM for _ in args],
        out_specs=VMEM if single else [VMEM for _ in out_shape],
        scratch_shapes=list(scratch),
        input_output_aliases=aliases,
        compiler_params=pltpu.CompilerParams(vmem_limit_bytes=LIMIT),
        cost_estimate=pl.CostEstimate(flops=flops, bytes_accessed=nbytes, transcendentals=0),
    )(*args)


def side_flags(axis):
    at, count = lax.axis_index(axis), lax.axis_size(axis)
    even = lax.rem(at, 2) == 0

    def number(flag):
        return jnp.where(flag, 1.0, 0.0).astype(F32)

    inner_left, inner_right = at > 0, at < count - 1
    left = number(jnp.logical_not(even)), number(jnp.logical_and(even, inner_left))
    right = number(even), number(jnp.logical_and(jnp.logical_not(even), inner_right))
    return left, right


def mix(a, b, flags):
    return (a.astype(F32) * flags[0] + b.astype(F32) * flags[1]).astype(BF16)


def scaled(v, m):
    return (v.astype(F32) * m).astype(BF16)


def is_even(axis):
    return jnp.where(lax.rem(lax.axis_index(axis), 2) == 0, 1, 0)


def pack_kernel(feat, planes, gy_a, gy_b, held, sems):
    chunks, _, count = held.shape[:3]

    def copy(i):
        return pltpu.make_async_copy(
            feat.at[:, i * count : (i + 1) * count], held.at[i], sems.at[i]
        )

    for i in range(chunks):
        copy(i).start()
    row, col = iota((256, 256), 0), iota((256, 256), 1)
    match = ((row >> 4) == (col & 15)) & ((row & 15) == (col >> 4))
    swap = jnp.where(match, 1.0, 0.0).astype(BF16)
    even = is_even("gy")
    rows_a = pl.multiple_of(even * 224, 32)
    rows_b = pl.multiple_of((1 - even) * 224, 32)
    for i in range(chunks):
        copy(i).wait()
        for x in range(0, count, 2):
            both = jnp.concatenate(
                [held[i, :, x].reshape(256, 128), held[i, :, x + 1].reshape(256, 128)], axis=1
            )
            moved = dot(swap, both).astype(BF16)
            planes[i * count + x] = moved[:, :128]
            planes[i * count + x + 1] = moved[:, 128:]
    gy_a[...] = planes[:, pl.ds(rows_a, 32), :]
    gy_b[...] = planes[:, pl.ds(rows_b, 32), :]


def pack(features):
    size_x = features.shape[1]
    step = 8
    return pl.pallas_call(
        pack_kernel,
        in_specs=[pl.BlockSpec(memory_space=pltpu.HBM)],
        out_specs=[VMEM] * 3,
        out_shape=[shape(size_x, 256, 128), shape(size_x, 32, 128), shape(size_x, 32, 128)],
        scratch_shapes=[
            pltpu.VMEM((size_x // step, 16, step, 16, 128), BF16),
            pltpu.SemaphoreType.DMA((size_x // step,)),
        ],
        compiler_params=pltpu.CompilerParams(vmem_limit_bytes=LIMIT),
        cost_estimate=pl.CostEstimate(
            flops=2 * 256 * 256 * 128 * size_x, bytes_accessed=5 << 20, transcendentals=0
        ),
    )(features)


def band(wide, t_ref, block):
    cols = t_ref.shape[1]
    group = iota((16, cols), 1) >> 4
    for c in range(3):
        for y in range(block):
            total = jnp.zeros((16, cols), F32)
            for a in range(3):
                for b in range(3):
                    k = 9 * a + 3 * b + c
                    here = group == a * (block + 2) + y + b
                    total = jnp.where(here, wide[16 * k : 16 * k + 16, :cols], total)
            at = 16 * (c * block + y)
            t_ref[at : at + 16, :] = total.astype(BF16)


def spread_channels(w):
    copies = jnp.where((iota((16, 240), 1) & 15) == iota((16, 240), 0), 1.0, 0.0).astype(BF16)
    return dot(w, copies)


def shifted_sum(acc, rows, half):
    lanes = slice(half * 128, half * 128 + 128)
    lane = iota((rows, 128), 1)
    before = pltpu.roll(acc[0:rows, lanes], 1, 1)
    after = pltpu.roll(acc[2 * rows : 3 * rows, lanes], 127, 1)
    total = acc[rows : 2 * rows, lanes]
    total = total + jnp.where(lane > 0, before, 0.0)
    total = total + jnp.where(lane < 127, after, 0.0)
    return jnp.maximum(total, 0.0)


def side_by_side(parts):
    halves = [jnp.concatenate([parts(h + a) for a in range(3)], axis=0) for h in range(2)]
    return jnp.concatenate(halves, axis=1)


def conv_block(matrix, rhs):
    acc = dot(matrix, rhs)
    rows = matrix.shape[0] // 3
    return [shifted_sum(acc, rows, h) for h in range(2)]


def interior_kernel(planes, w, f1, t1, t2, t2_last):
    size_x = planes.shape[0]
    wide = spread_channels(w[0:432, :])
    band(wide, t1, 3)
    wide = spread_channels(w[432:864, :])
    band(wide, t2, 3)
    band(wide, t2_last, 1)

    def step(p, carry):
        for j in range(1, 5):
            row = 16 * (3 * j - 2)
            rhs = side_by_side(lambda x: planes[2 * p - 2 + x, row : row + 80])
            for h, value in enumerate(conv_block(t1[...], rhs)):
                f1[2 * p + h, 48 * j : 48 * j + 48] = value.astype(BF16)
        return carry

    lax.fori_loop(1, size_x // 2, step, 0)


def face_kernel(planes, gy_a, gy_b, faces, send_a, send_b):
    size_x = planes.shape[0]
    left, right = side_flags("gy")
    for side in range(2):
        for j in range(2):
            x = side * (size_x - 2) + j
            faces[side, j, 0:32] = mix(gy_a[x], gy_b[x], left)
            faces[side, j, 32:288] = planes[x]
            faces[side, j, 288:320] = mix(gy_a[x], gy_b[x], right)
    even = is_even("gx")
    send_a[...] = faces[even]
    send_b[...] = faces[1 - even]


def conv_two_pair(f1_of, t2, t2_last, store):
    summed = jnp.zeros((16, 128), F32)
    for j in range(6):
        rows = 48 if j < 5 else 16
        size = 80 if j < 5 else 48
        rhs = side_by_side(lambda x: f1_of(x, 48 * j, size))
        for h, value in enumerate(conv_block(t2[...] if j < 5 else t2_last[...], rhs)):
            value = value.astype(BF16)
            store(h, 48 * j, rows, value)
            summed = summed + jnp.sum(value.astype(F32).reshape(rows // 16, 16, 128), axis=0)
    return summed


def middle_kernel(f1_in, planes, gy_a, gy_b, t1, t2, t2_last, f1, second, psum, hl, hr):
    size_x = planes.shape[0]
    left, right = side_flags("gy")
    y_left, y_right = left[0] + left[1], right[0] + right[1]

    def fill(x, carry):
        hl[x] = mix(gy_a[x], gy_b[x], left)
        hr[x] = mix(gy_a[x], gy_b[x], right)
        return carry

    lax.fori_loop(0, size_x, fill, 0, unroll=4)

    def rim(p, carry):
        at = 2 * p - 2
        low = side_by_side(
            lambda x: jnp.concatenate([hl[at + x], planes[at + x, 0:48]], axis=0)
        )
        high = side_by_side(
            lambda x: jnp.concatenate([planes[at + x, 208:256], hr[at + x]], axis=0)
        )
        for h, value in enumerate(conv_block(t1[...], low)):
            f1[2 * p + h, 0:16] = (value[:16] * y_left).astype(BF16)
            f1[2 * p + h, 16:48] = value[16:].astype(BF16)
        for h, value in enumerate(conv_block(t1[...], high)):
            f1[2 * p + h, 240:272] = value[:32].astype(BF16)
            f1[2 * p + h, 272:288] = (value[32:] * y_right).astype(BF16)
        return carry

    lax.fori_loop(1, size_x // 2, rim, 0)
    psum[...] = jnp.zeros(psum.shape, F32)

    def step(q, carry):
        def store(h, row, rows, value):
            second[2 * q + h, row : row + rows] = value

        psum[q // (POOL // 2)] += conv_two_pair(
            lambda x, row, size: f1[2 * q + x, row : row + size], t2, t2_last, store
        )
        return carry

    lax.fori_loop(1, size_x // 2 - 1, step, 0)


def edge_kernel(
    second_in, f1, faces, got_a, got_b, psum_in, t1, t2, t2_last, second, pooled, fe, fx
):
    size_x = second.shape[0]
    x_left, x_right = side_flags("gx")
    y_left, y_right = side_flags("gy")
    y_left, y_right = y_left[0] + y_left[1], y_right[0] + y_right[1]
    for j in range(2):
        fe[0, j] = mix(got_a[j], got_b[j], x_left)
        fe[0, 2 + j] = faces[0, j]
        fe[1, j] = faces[1, j]
        fe[1, 2 + j] = mix(got_a[j], got_b[j], x_right)
    keeps = ((x_left[0] + x_left[1], 1.0), (1.0, x_right[0] + x_right[1]))

    def rim(side, keep_of):
        for j in range(6):
            rhs = side_by_side(lambda x: fe[side, x, 48 * j : 48 * j + 80])
            for h, value in enumerate(conv_block(t1[...], rhs)):
                keep = keep_of[h]
                low, mid, high = value[:16], value[16:32], value[32:]
                if j == 0:
                    low = low * y_left
                if j == 5:
                    high = high * y_right
                value = jnp.concatenate([low, mid, high], axis=0) * keep
                fx[side, h, 48 * j : 48 * j + 48] = value.astype(BF16)

    for side in range(2):
        rim(side, keeps[side])

    z, lane = iota((128, 128), 0), iota((128, 128), 1)
    gather = jnp.where((z >> 4) == (lane & 7), 1.0, 0.0).astype(F32)
    keep = (iota((16, 128), 1) >> 3) == iota((16, 128), 0)
    results = []
    for side in range(2):
        base = side * (size_x - 2)

        def f1_of(x, row, size):
            if side == 0:
                return fx[0, x, row : row + size] if x < 2 else f1[x, row : row + size]
            if x < 2:
                return f1[size_x - 2 + x, row : row + size]
            return fx[1, x - 2, row : row + size]

        def store(h, row, rows, value):
            second[base + h, row : row + rows] = value

        summed = psum_in[side] + conv_two_pair(f1_of, t2, t2_last, store)
        cells = jnp.dot(
            summed, gather, preferred_element_type=F32, precision=lax.Precision.HIGHEST
        )
        row = jnp.sum(jnp.where(keep, cells, 0.0), axis=0, keepdims=True) * (1.0 / POOL**3)
        results.append(row)
    both = jnp.concatenate(results, axis=0)
    for d in range(16):
        pooled[d] = both


def split3(v):
    a = v.astype(BF16)
    v = v - a.astype(F32)
    b = v.astype(BF16)
    c = (v - b.astype(F32)).astype(BF16)
    return a, b, c


def swap_groups(rows):
    lane = iota((256, 128), 1)
    major, minor = iota((256, 128), 0) >> 4, iota((256, 128), 0) & 15
    spread = jnp.broadcast_to(rows[:, None, :], (16, 16, 128)).reshape(256, 128)
    spread = jnp.where((lane >> 3) == minor, spread, 0.0)
    l0, l1 = iota((128, 128), 0), iota((128, 128), 1)
    fold = jnp.where((l0 & 7) == (l1 & 7), 1.0, 0.0).astype(BF16)
    out = []
    for piece in split3(spread):
        moved = jnp.where((lane >> 3) == major, dot(piece, fold), 0.0)
        out.append(jnp.sum(moved.reshape(16, 16, 128), axis=0))
    return out


def lift_slabs(slabs, w_lift):
    columns = []
    for slab in slabs:
        pieces = [v.astype(BF16) for v in swap_groups(slab)]
        columns.append(jnp.concatenate(pieces, axis=0))
    stacked = jnp.concatenate(columns, axis=1)
    lift3 = jnp.concatenate([w_lift] * 3, axis=1)
    return jnp.maximum(dot(lift3, stacked), 0.0).astype(BF16)


def taps(partial, count):
    lane = iota((count, 128), 1)
    y, z = lane >> 3, lane & 7
    total = jnp.zeros((count, 128), F32)
    for k in range(9):
        b, c = k // 3 - 1, k % 3 - 1
        piece = partial[k * count : (k + 1) * count, :]
        step = 8 * b + c
        if step:
            piece = pltpu.roll(piece, (-step) % 128, 1)
        good = None
        if b:
            good = (y < 15) if b > 0 else (y > 0)
        if c:
            inside = (z < 7) if c > 0 else (z > 0)
            good = inside if good is None else good & inside
        total = total + (piece if good is None else jnp.where(good, piece, 0.0))
    return total


def own_kernel(own, w_lift, w_coarse, out):
    count = w_coarse.shape[0] // 27
    lifted = lift_slabs([own[:, 0, :], own[:, 1, :]], w_lift[...])
    partial = dot(w_coarse[...], lifted)
    for x in range(2):
        total = jnp.zeros((count, 128), F32)
        for slab in range(2):
            a = slab - x + 1
            piece = partial[9 * a * count : 9 * (a + 1) * count, slab * 128 : slab * 128 + 128]
            total = total + taps(piece, count)
        out[x] = total


def beside_kernel(mine, gl, gr, w_lift, w_coarse, w_dec, out):
    count = w_coarse.shape[0] // 27
    at, last = lax.axis_index("gx"), lax.axis_size("gx") - 1
    m_left = jnp.where(at > 0, 1.0, 0.0).astype(F32)
    m_right = jnp.where(at < last, 1.0, 0.0).astype(F32)
    lifted = lift_slabs([gl[...] * m_left, gr[...] * m_right], w_lift[...])
    for x in range(2):
        a = 2 * x
        rows = w_coarse[9 * a * count : 9 * (a + 1) * count, :]
        total = mine[x] + taps(dot(rows, lifted[:, x * 128 : x * 128 + 128]), count)
        coarse = jnp.maximum(total, 0.0).astype(BF16)
        pieces = swap_groups(dot(w_dec[...], coarse))
        out[:, x, :] = pieces[0] + pieces[1] + pieces[2]


def skip_kernel(second, w_join, out):
    size_x = second.shape[0]
    r, c = iota((256, 16), 0), iota((256, 16), 1)
    rows = jnp.where((r >> 4) == c, 1.0, 0.0).astype(BF16)
    mixed = dot(rows, w_join[:, 0:16]).astype(BF16)
    r, c = iota((16, 256), 0), iota((16, 256), 1)
    cols = jnp.where((c & 15) == r, 1.0, 0.0).astype(BF16)
    r, c = iota((256, 256), 0), iota((256, 256), 1)
    matrix = jnp.where((r & 15) == (c >> 4), dot(mixed, cols), 0.0).astype(BF16)

    def step(q, carry):
        both = jnp.concatenate([second[2 * q], second[2 * q + 1]], axis=1)
        result = dot(matrix, both)
        out[2 * q] = result[:, :128]
        out[2 * q + 1] = result[:, 128:]
        return carry

    lax.fori_loop(0, size_x // 2, step, 0, unroll=4)


def join_kernel(skip, parts, w_join, out, held, sems):
    size_x = skip.shape[0]
    r, c = iota((256, 16), 0), iota((256, 16), 1)
    rows = jnp.where((r >> 4) == c, 1.0, 0.0).astype(BF16)
    up = dot(rows, w_join[:, 16:32]).astype(BF16)
    keep = (iota((16, 128), 1) >> 3) == iota((16, 128), 0)
    l0, l1 = iota((128, 128), 0), iota((128, 128), 1)
    widen = jnp.where((l0 & 7) == (l1 >> 4), 1.0, 0.0).astype(BF16)
    total = parts[0]
    for d in range(1, 16):
        total = total + parts[d]
    terms = []
    for block in range(2):
        decoded = jnp.broadcast_to(total[block : block + 1, :], (16, 128))
        decoded = jnp.where(keep, decoded, 0.0).astype(BF16)
        terms.append(dot(up, dot(decoded, widen).astype(BF16)))
    chunks, _, count = held.shape[:3]

    def copy(i):
        return pltpu.make_async_copy(
            held.at[i], out.at[:, i * count : (i + 1) * count], sems.at[i]
        )

    for i in range(chunks):
        for x in range(count):
            at = i * count + x
            value = (skip[at] + terms[at // POOL]).astype(BF16)
            held[i, :, x] = value.reshape(16, 16, 128)
        copy(i).start()
    for i in range(chunks):
        copy(i).wait()


def join(skip, parts, w_join):
    size_x = skip.shape[0]
    step = 4
    return pl.pallas_call(
        join_kernel,
        in_specs=[VMEM] * 3,
        out_specs=pl.BlockSpec(memory_space=pltpu.HBM),
        out_shape=shape(16, size_x, 16, 128),
        scratch_shapes=[
            pltpu.VMEM((size_x // step, 16, step, 16, 128), BF16),
            pltpu.SemaphoreType.DMA((size_x // step,)),
        ],
        compiler_params=pltpu.CompilerParams(vmem_limit_bytes=LIMIT),
        cost_estimate=pl.CostEstimate(flops=1 << 22, bytes_accessed=4 << 20, transcendentals=0),
    )(skip, parts, w_join)


def local(features, w_first, w_second, w_lift, w_coarse, w_decode, w_joining):
    size_x = features.shape[1]
    nx, ny = lax.axis_size("gx"), lax.axis_size("gy")
    gy = lax.axis_index("gy")

    def ring(count, step):
        return [(i, (i + step) % count) for i in range(count)]

    def swap(count, odd):
        return [(i, (((i + odd) ^ 1) - odd) % count) for i in range(count)]

    planes, gy_a, gy_b = pack(features)
    gy_a = lax.ppermute(gy_a, "gy", swap(ny, 0))
    gy_b = lax.ppermute(gy_b, "gy", swap(ny, 1))

    w_fine = jnp.concatenate([w_first, w_second], axis=0).reshape(864, 16)
    f1, t1, t2, t2_last = vmem_call(
        interior_kernel,
        [shape(size_x + 2, 288, 128), shape(144, 240), shape(144, 240), shape(48, 144)],
        (planes, w_fine),
        flops=2 * 1152 * 256 * 128 * size_x,
        nbytes=4 << 20,
    )
    faces, send_a, send_b = vmem_call(
        face_kernel,
        [shape(2, 2, 320, 128), shape(2, 320, 128), shape(2, 320, 128)],
        (planes, gy_a, gy_b),
        nbytes=1 << 19,
    )
    got_a = lax.ppermute(send_a, "gx", swap(nx, 0))
    got_b = lax.ppermute(send_b, "gx", swap(nx, 1))
    f1, second, psum = vmem_call(
        middle_kernel,
        [shape(size_x + 2, 288, 128), shape(size_x, 256, 128), shape(2, 16, 128, dtype=F32)],
        (f1, planes, gy_a, gy_b, t1, t2, t2_last),
        scratch=[pltpu.VMEM((size_x, 32, 128), BF16), pltpu.VMEM((size_x, 32, 128), BF16)],
        flops=2 * 2 * 1152 * 256 * 128 * size_x,
        nbytes=6 << 20,
        aliases={0: 0},
    )
    second, pooled = vmem_call(
        edge_kernel,
        [shape(size_x, 256, 128), shape(16, 2, 128, dtype=F32)],
        (second, f1, faces, got_a, got_b, psum, t1, t2, t2_last),
        scratch=[pltpu.VMEM((2, 4, 320, 128), BF16), pltpu.VMEM((2, 2, 288, 128), BF16)],
        flops=1 << 29,
        nbytes=1 << 20,
        aliases={0: 0},
    )

    count = w_coarse.shape[0]
    w_rows = jnp.transpose(w_coarse, (1, 0, 2)).reshape(27 * count, w_coarse.shape[2])
    w_dec = lax.dynamic_slice_in_dim(w_decode, gy * count, count, axis=1)
    own = lax.all_to_all(pooled, "gy", 0, 0)
    skip = vmem_call(
        skip_kernel,
        shape(size_x, 256, 128, dtype=F32),
        (second, w_joining),
        flops=2 * 256 * 256 * 128 * size_x,
        nbytes=6 << 20,
    )
    gl = lax.ppermute(own[:, 1, :], "gx", ring(nx, 1))
    gr = lax.ppermute(own[:, 0, :], "gx", ring(nx, -1))
    mine = vmem_call(
        own_kernel,
        shape(2, count, 128, dtype=F32),
        (own, w_lift, w_rows),
        flops=2 * 864 * 512 * 512,
        nbytes=2 << 20,
    )
    parts = vmem_call(
        beside_kernel,
        shape(16, 2, 128, dtype=F32),
        (mine, gl, gr, w_lift, w_rows, w_dec),
        flops=2 * 864 * 512 * 256,
        nbytes=2 << 20,
    )
    parts = lax.all_to_all(parts, "gy", 0, 0)
    return join(skip, parts, w_joining)


def solution(mesh):
    in_specs = (P(None, "gx", "gy", None), P(), P(), P(), P("gy", None, None), P(), P())
    out_specs = P(None, "gx", "gy", None)
    return jax.shard_map(local, mesh=mesh, in_specs=in_specs, out_specs=out_specs, check_vma=False)
```

profile of v0, /device:TPU:1, one launch (start us, length us, event | category | flops | bytes accessed | tf_op | source)
XLA Modules:
  0.0 67.9 jit_solution(2301470111940648874)
XLA Ops:
  0.0 0.0 copy-start
  0.0 0.0 copy-start.5
  0.0 1.6 %copy-done.5 = bf16[16,32,16,128]{3,2,1,0:T(8,128)(2,1)S(1)} copy-done((bf16[16,32,16,128]{3,2,1,0:T(8,128)(2,1)S(1)}, bf16[16,32,16,128]{3,2,1,0:T(8,128)(2,1)}, u32[]{:S(2)}) %copy-start.5) | copy-done | bytes 2097176
  1.6 0.0 copy-start.8
  1.6 0.0 copy-start.9
  1.6 1.5 %shard_map.73 = (bf16[32,256,128]{2,1,0:T(8,128)(2,1)S(1)}, bf16[32,32,128]{2,1,0:T(8,128)(2,1)S(1)}, bf16[32,32,128]{2,1,0:T(8,128)(2,1)S(1)}) custom-call(bf16[16,32,16,128]{3,2,1,0:T(8,128)(2,1)S(1)} %copy-done.5), custom_call_target="tpu_custom_call" | custom-call | flops 536870912 | bytes 5242880 | tf_op jit(solution)/shard_map/pallas_call | solution.py:98
  3.1 0.0 copy-start.3
  3.1 1.5 %collective-permute-start = (bf16[32,32,128]{2,1,0:T(8,128)(2,1)S(1)}, bf16[32,32,128]{2,1,0:T(8,128)(2,1)S(1)}, u32[]{:S(2)}, u32[]{:S(2)}) collective-permute-start(bf16[32,32,128]{2,1,0:T(8,128)(2,1)S(1)} %get-tuple-element.22), channel_id=1, source_target_pairs={{0,1},{1,0},{2,3},{3,2},{4,5},{5,4},{6,7},{7,6},{8,9},{9,8},{10,11... | collective-permute-start | bytes 786440 | tf_op jit(solution)/shard_map/ppermute | solution.py:465
  4.6 1.4 %collective-permute-start.1 = (bf16[32,32,128]{2,1,0:T(8,128)(2,1)S(1)}, bf16[32,32,128]{2,1,0:T(8,128)(2,1)S(1)}, u32[]{:S(2)}, u32[]{:S(2)}) collective-permute-start(bf16[32,32,128]{2,1,0:T(8,128)(2,1)S(1)} %get-tuple-element.23), channel_id=1, source_target_pairs={{0,15},{1,2},{2,1},{3,4},{4,3},{5,6},{6,5},{7,8},{8,7},{9,10},{10,... | collective-permute-start | bytes 786440 | tf_op jit(solution)/shard_map/ppermute | solution.py:466
  6.0 0.0 copy-done.8
  6.0 0.0 copy-done.9
  6.0 0.1 pad_maximum_fusion
  6.1 0.3 copy.15
  6.3 5.3 %shard_map.74 = (bf16[34,288,128]{2,1,0:T(8,128)(2,1)S(1)}, bf16[144,240]{1,0:T(8,128)(2,1)S(1)}, bf16[144,240]{1,0:T(8,128)(2,1)S(1)}, bf16[48,144]{1,0:T(8,128)(2,1)S(1)}) custom-call(bf16[32,256,128]{2,1,0:T(8,128)(2,1)S(1)} %get-tuple-element.20.planes, bf16[864,16]{1,0:T(8,128)(2,1)S(1)} %bitcast.12), custom_call_target="tpu_custom_call" | custom-call | flops 2415919104 | bytes 4194304 | tf_op jit(solution)/shard_map/pallas_call | solution.py:29
  11.7 0.0 collective-permute-done.gy_a
  11.7 0.9 %collective-permute-done.1.gy_b = bf16[32,32,128]{2,1,0:T(8,128)(2,1)S(1)} collective-permute-done((bf16[32,32,128]{2,1,0:T(8,128)(2,1)S(1)}, bf16[32,32,128]{2,1,0:T(8,128)(2,1)S(1)}, u32[]{:S(2)}, u32[]{:S(2)}) %collective-permute-start.1) | collective-permute-done | bytes 262176 | tf_op jit(solution)/shard_map/ppermute | solution.py:466
  12.6 0.0 copy-done.3
  12.6 0.1 shard_map.76
  12.7 3.2 %collective-permute-start.2 = (bf16[2,320,128]{2,1,0:T(8,128)(2,1)S(1)}, bf16[2,320,128]{2,1,0:T(8,128)(2,1)S(1)}, u32[]{:S(2)}, u32[]{:S(2)}) collective-permute-start(bf16[2,320,128]{2,1,0:T(8,128)(2,1)S(1)} %get-tuple-element.30), channel_id=1, source_target_pairs={{0,16},{16,0},{32,48},{48,32},{64,80},{80,64},{96,112},{112,96},{1... | collective-permute-start | bytes 491528 | tf_op jit(solution)/shard_map/ppermute | solution.py:482
  15.9 2.3 %collective-permute-start.3 = (bf16[2,320,128]{2,1,0:T(8,128)(2,1)S(1)}, bf16[2,320,128]{2,1,0:T(8,128)(2,1)S(1)}, u32[]{:S(2)}, u32[]{:S(2)}) collective-permute-start(bf16[2,320,128]{2,1,0:T(8,128)(2,1)S(1)} %get-tuple-element.31), channel_id=1, source_target_pairs={{0,112},{16,32},{32,16},{48,64},{64,48},{80,96},{96,80},{112,0},{1... | collective-permute-start | bytes 491528 | tf_op jit(solution)/shard_map/ppermute | solution.py:483
  18.2 0.0 copy-start.4
  18.2 1.6 %copy-done.4 = bf16[32,256,128]{2,1,0:T(8,128)(2,1)S(1)} copy-done((bf16[32,256,128]{2,1,0:T(8,128)(2,1)S(1)}, bf16[32,256,128]{2,1,0:T(8,128)(2,1)}, u32[]{:S(2)}) %copy-start.4) | copy-done | bytes 2097176
  19.8 9.7 %shard_map.75 = (bf16[34,288,128]{2,1,0:T(8,128)(2,1)S(1)}, bf16[32,256,128]{2,1,0:T(8,128)(2,1)S(1)}, f32[2,16,128]{2,1,0:T(8,128)S(1)}) custom-call(bf16[34,288,128]{2,1,0:T(8,128)(2,1)S(1)} %get-tuple-element.21.f1_in, bf16[32,256,128]{2,1,0:T(8,128)(2,1)S(1)} %copy-done.4, ...), custom_call_target="tpu_custom_call", output_to_operand_aliasing={{0}: (0, {})} | custom-call | flops 4831838208 | bytes 6291456 | tf_op jit(solution)/shard_map/pallas_call | solution.py:29
  29.5 0.0 collective-permute-done.2.got_a
  29.5 0.0 collective-permute-done.3.got_b
  29.5 0.0 copy-start.10
  29.5 0.0 copy-start.6
  29.5 1.9 %shard_map.77 = (bf16[32,256,128]{2,1,0:T(8,128)(2,1)S(1)}, f32[16,2,128]{2,1,0:T(2,128)}) custom-call(bf16[32,256,128]{2,1,0:T(8,128)(2,1)S(1)} %get-tuple-element.27.second_in, bf16[34,288,128]{2,1,0:T(8,128)(2,1)S(1)} %get-tuple-element.28.f1, bf16[2,2,320,128]{3,2,1,0:T(8,128)(2,1)S(1)} %get-tuple-element.29.faces, ...), custom_call_target="tpu_custom_call", output_to_operand_aliasing={{0}: (0, {})} | custom-call | flops 536870912 | bytes 1048576 | tf_op jit(solution)/shard_map/pallas_call | solution.py:29
  31.4 0.0 copy-start.7
  31.4 7.3 %all-to-all-start = ((f32[16,2,128]{2,1,0:T(2,128)}), f32[16,2,128]{2,1,0:T(2,128)S(1)}, u32[]{:S(2)}, u32[]{:S(2)}) async-start(f32[16,2,128]{2,1,0:T(2,128)} %get-tuple-element.34), calls=%async_computation | async-start | bytes 32768 | tf_op jit(solution)/shard_map/all_to_all | solution.py:506
  38.7 0.0 copy-done
  38.7 0.1 constant_dynamic-slice_fusion.w_dec
  38.8 0.0 copy-done.10
  38.8 0.1 copy.16.w_lift
  38.9 5.6 %all-to-all-done.own = f32[16,2,128]{2,1,0:T(2,128)S(1)} async-done(((f32[16,2,128]{2,1,0:T(2,128)}), f32[16,2,128]{2,1,0:T(2,128)S(1)}, u32[]{:S(2)}, u32[]{:S(2)}) %all-to-all-start) | async-done | bytes 16416 | tf_op jit(solution)/shard_map/all_to_all | solution.py:506
  44.5 1.4 %collective-permute-start.4 = (f32[16,128]{1,0:T(8,128)S(1)}, f32[16,128]{1,0:T(8,128)S(1)}, u32[]{:S(2)}, u32[]{:S(2)}) collective-permute-start(f32[16,128]{1,0:T(8,128)S(1)} %bitcast.14), channel_id=1, source_target_pairs={{0,16},{16,32},{32,48},{48,64},{64,80},{80,96},{96,112},{112,0},{1... | collective-permute-start | bytes 24584 | tf_op jit(solution)/shard_map/ppermute | solution.py:514
  46.0 3.7 %collective-permute-start.5 = (f32[16,128]{1,0:T(8,128)S(1)}, f32[16,128]{1,0:T(8,128)S(1)}, u32[]{:S(2)}, u32[]{:S(2)}) collective-permute-start(f32[16,128]{1,0:T(8,128)S(1)} %bitcast.13), channel_id=1, source_target_pairs={{0,112},{16,0},{32,16},{48,32},{64,48},{80,64},{96,80},{112,96},{1... | collective-permute-start | bytes 24584 | tf_op jit(solution)/shard_map/ppermute | solution.py:515
  49.7 0.0 copy-done.6
  49.7 1.0 %shard_map.79.mine = f32[2,32,128]{2,1,0:T(8,128)S(1)} custom-call(f32[16,2,128]{2,1,0:T(2,128)S(1)} %all-to-all-done.own, bf16[512,16]{1,0:T(8,128)(2,1)S(1)} %copy.16.w_lift, bf16[864,512]{1,0:T(8,128)(2,1)S(1)} %bitcast.10), custom_call_target="tpu_custom_call" | custom-call | flops 452984832 | bytes 2097152 | tf_op jit(solution)/shard_map/pallas_call | solution.py:29
  50.7 0.1 collective-permute-done.4.gl
  50.7 0.0 collective-permute-done.5.gr
  50.7 2.3 %shard_map.80 = f32[16,2,128]{2,1,0:T(2,128)} custom-call(f32[2,32,128]{2,1,0:T(8,128)S(1)} %shard_map.79.mine, f32[16,128]{1,0:T(8,128)S(1)} %collective-permute-done.4.gl, f32[16,128]{1,0:T(8,128)S(1)} %collective-permute-done.5.gr, bf16[512,16]{1,0:T(8,128)(2,1)S(1)} %copy.16.w_lift, bf16[864,512]{1,0:T(8,128)(2,1)S(1)} %bitcast.11, ...), custom_call_target="tpu_custom_call" | custom-call | flops 226492416 | bytes 2097152 | tf_op jit(solution)/shard_map/pallas_call | solution.py:29
  53.0 4.8 %all-to-all-start.1 = ((f32[16,2,128]{2,1,0:T(2,128)}), f32[16,2,128]{2,1,0:T(2,128)S(1)}, u32[]{:S(2)}, u32[]{:S(2)}) async-start(f32[16,2,128]{2,1,0:T(2,128)} %shard_map.80), calls=%async_computation.1 | async-start | bytes 32768 | tf_op jit(solution)/shard_map/all_to_all | solution.py:530
  57.8 0.0 copy-done.7
  57.8 1.5 %shard_map.78.skip = f32[32,256,128]{2,1,0:T(8,128)S(1)} custom-call(bf16[32,256,128]{2,1,0:T(8,128)(2,1)S(1)} %get-tuple-element.33.second, bf16[16,32]{1,0:T(8,128)(2,1)S(1)} %copy-done.7), custom_call_target="tpu_custom_call" | custom-call | flops 536870912 | bytes 6291456 | tf_op jit(solution)/shard_map/pallas_call | solution.py:29
  59.4 0.0 copy-start.1
  59.4 1.9 %copy-done.1 = f32[32,256,128]{2,1,0:T(8,128)} copy-done((f32[32,256,128]{2,1,0:T(8,128)}, f32[32,256,128]{2,1,0:T(8,128)S(1)}, u32[]{:S(2)}) %copy-start.1) | copy-done | bytes 4194328
  61.3 2.3 %all-to-all-done.1.parts = f32[16,2,128]{2,1,0:T(2,128)S(1)} async-done(((f32[16,2,128]{2,1,0:T(2,128)}), f32[16,2,128]{2,1,0:T(2,128)S(1)}, u32[]{:S(2)}, u32[]{:S(2)}) %all-to-all-start.1) | async-done | bytes 16416 | tf_op jit(solution)/shard_map/all_to_all | solution.py:530
  63.7 0.0 copy-start.2
  63.7 2.2 %copy-done.2 = f32[32,256,128]{2,1,0:T(8,128)S(1)} copy-done((f32[32,256,128]{2,1,0:T(8,128)S(1)}, f32[32,256,128]{2,1,0:T(8,128)}, u32[]{:S(2)}) %copy-start.2) | copy-done | bytes 4194328
  65.8 2.0 %shard_map.81 = bf16[16,32,16,128]{3,2,1,0:T(8,128)(2,1)} custom-call(f32[32,256,128]{2,1,0:T(8,128)S(1)} %copy-done.2, f32[16,2,128]{2,1,0:T(2,128)S(1)} %all-to-all-done.1.parts, bf16[16,32]{1,0:T(8,128)(2,1)S(1)} %copy-done.7), custom_call_target="tpu_custom_call" | custom-call | flops 4194304 | bytes 4194304 | tf_op jit(solution)/shard_map/pallas_call | solution.py:439
  (1 shorter events, 0.0 us)
Async XLA Ops:
  0.0 38.7 %copy-start = (bf16[16,512]{1,0:T(8,128)(2,1)S(1)}, bf16[16,512]{1,0:T(8,128)(2,1)}, u32[]{:S(2)}) copy-start(bf16[16,512]{1,0:T(8,128)(2,1)} %param.12) | copy-start | bytes 49156
  0.0 1.6 %copy-start.5 = (bf16[16,32,16,128]{3,2,1,0:T(8,128)(2,1)S(1)}, bf16[16,32,16,128]{3,2,1,0:T(8,128)(2,1)}, u32[]{:S(2)}) copy-start(bf16[16,32,16,128]{3,2,1,0:T(8,128)(2,1)} %feat.1) | copy-start | bytes 6291460
  1.6 4.4 %copy-start.8 = (bf16[27,16,16]{0,2,1:T(8,128)(2,1)S(1)}, bf16[27,16,16]{0,2,1:T(8,128)(2,1)}, u32[]{:S(2)}) copy-start(bf16[27,16,16]{0,2,1:T(8,128)(2,1)} %param.9) | copy-start | bytes 41476
  1.6 4.4 %copy-start.9 = (bf16[27,16,16]{0,2,1:T(8,128)(2,1)S(1)}, bf16[27,16,16]{0,2,1:T(8,128)(2,1)}, u32[]{:S(2)}) copy-start(bf16[27,16,16]{0,2,1:T(8,128)(2,1)} %param.8) | copy-start | bytes 41476
  3.1 9.5 %copy-start.3 = (bf16[32,256,128]{2,1,0:T(8,128)(2,1)}, bf16[32,256,128]{2,1,0:T(8,128)(2,1)S(1)}, u32[]{:S(2)}) copy-start(bf16[32,256,128]{2,1,0:T(8,128)(2,1)S(1)} %get-tuple-element.20.planes) | copy-start | bytes 6291460
  3.1 8.6 %collective-permute-start = (bf16[32,32,128]{2,1,0:T(8,128)(2,1)S(1)}, bf16[32,32,128]{2,1,0:T(8,128)(2,1)S(1)}, u32[]{:S(2)}, u32[]{:S(2)}) collective-permute-start(bf16[32,32,128]{2,1,0:T(8,128)(2,1)S(1)} %get-tuple-element.22), channel_id=1, source_target_pairs={{0,1},{1,0},{2,3},{3,2},{4,5},{5,4},{6,7},{7,6},{8,9},{9,8},{10,11... | collective-permute-start | bytes 786440 | tf_op jit(solution)/shard_map/ppermute | solution.py:465
  4.6 8.0 %collective-permute-start.1 = (bf16[32,32,128]{2,1,0:T(8,128)(2,1)S(1)}, bf16[32,32,128]{2,1,0:T(8,128)(2,1)S(1)}, u32[]{:S(2)}, u32[]{:S(2)}) collective-permute-start(bf16[32,32,128]{2,1,0:T(8,128)(2,1)S(1)} %get-tuple-element.23), channel_id=1, source_target_pairs={{0,15},{1,2},{2,1},{3,4},{4,3},{5,6},{6,5},{7,8},{8,7},{9,10},{10,... | collective-permute-start | bytes 786440 | tf_op jit(solution)/shard_map/ppermute | solution.py:466
  12.7 16.8 %collective-permute-start.2 = (bf16[2,320,128]{2,1,0:T(8,128)(2,1)S(1)}, bf16[2,320,128]{2,1,0:T(8,128)(2,1)S(1)}, u32[]{:S(2)}, u32[]{:S(2)}) collective-permute-start(bf16[2,320,128]{2,1,0:T(8,128)(2,1)S(1)} %get-tuple-element.30), channel_id=1, source_target_pairs={{0,16},{16,0},{32,48},{48,32},{64,80},{80,64},{96,112},{112,96},{1... | collective-permute-start | bytes 491528 | tf_op jit(solution)/shard_map/ppermute | solution.py:482
  15.9 13.6 %collective-permute-start.3 = (bf16[2,320,128]{2,1,0:T(8,128)(2,1)S(1)}, bf16[2,320,128]{2,1,0:T(8,128)(2,1)S(1)}, u32[]{:S(2)}, u32[]{:S(2)}) collective-permute-start(bf16[2,320,128]{2,1,0:T(8,128)(2,1)S(1)} %get-tuple-element.31), channel_id=1, source_target_pairs={{0,112},{16,32},{32,16},{48,64},{64,48},{80,96},{96,80},{112,0},{1... | collective-permute-start | bytes 491528 | tf_op jit(solution)/shard_map/ppermute | solution.py:483
  18.2 1.6 %copy-start.4 = (bf16[32,256,128]{2,1,0:T(8,128)(2,1)S(1)}, bf16[32,256,128]{2,1,0:T(8,128)(2,1)}, u32[]{:S(2)}) copy-start(bf16[32,256,128]{2,1,0:T(8,128)(2,1)} %copy-done.3) | copy-start | bytes 6291460
  29.5 9.3 %copy-start.10 = (bf16[512,16]{0,1:T(8,128)(2,1)S(1)}, bf16[512,16]{0,1:T(8,128)(2,1)}, u32[]{:S(2)}) copy-start(bf16[512,16]{0,1:T(8,128)(2,1)} %param.10) | copy-start | bytes 49156
  29.5 20.2 %copy-start.6 = (bf16[32,27,512]{2,0,1:T(8,128)(2,1)S(1)}, bf16[32,27,512]{2,0,1:T(8,128)(2,1)}, u32[]{:S(2)}) copy-start(bf16[32,27,512]{2,0,1:T(8,128)(2,1)} %param.11) | copy-start | bytes 2654212
  31.4 26.4 %copy-start.7 = (bf16[16,32]{1,0:T(8,128)(2,1)S(1)}, bf16[16,32]{1,0:T(8,128)(2,1)}, u32[]{:S(2)}) copy-start(bf16[16,32]{1,0:T(8,128)(2,1)} %w_join.3) | copy-start | bytes 3076
  31.4 13.1 %all-to-all-start = ((f32[16,2,128]{2,1,0:T(2,128)}), f32[16,2,128]{2,1,0:T(2,128)S(1)}, u32[]{:S(2)}, u32[]{:S(2)}) async-start(f32[16,2,128]{2,1,0:T(2,128)} %get-tuple-element.34), calls=%async_computation | async-start | bytes 32768 | tf_op jit(solution)/shard_map/all_to_all | solution.py:506
  44.5 6.2 %collective-permute-start.4 = (f32[16,128]{1,0:T(8,128)S(1)}, f32[16,128]{1,0:T(8,128)S(1)}, u32[]{:S(2)}, u32[]{:S(2)}) collective-permute-start(f32[16,128]{1,0:T(8,128)S(1)} %bitcast.14), channel_id=1, source_target_pairs={{0,16},{16,32},{32,48},{48,64},{64,80},{80,96},{96,112},{112,0},{1... | collective-permute-start | bytes 24584 | tf_op jit(solution)/shard_map/ppermute | solution.py:514
  46.0 4.8 %collective-permute-start.5 = (f32[16,128]{1,0:T(8,128)S(1)}, f32[16,128]{1,0:T(8,128)S(1)}, u32[]{:S(2)}, u32[]{:S(2)}) collective-permute-start(f32[16,128]{1,0:T(8,128)S(1)} %bitcast.13), channel_id=1, source_target_pairs={{0,112},{16,0},{32,16},{48,32},{64,48},{80,64},{96,80},{112,96},{1... | collective-permute-start | bytes 24584 | tf_op jit(solution)/shard_map/ppermute | solution.py:515
  53.0 10.7 %all-to-all-start.1 = ((f32[16,2,128]{2,1,0:T(2,128)}), f32[16,2,128]{2,1,0:T(2,128)S(1)}, u32[]{:S(2)}, u32[]{:S(2)}) async-start(f32[16,2,128]{2,1,0:T(2,128)} %shard_map.80), calls=%async_computation.1 | async-start | bytes 32768 | tf_op jit(solution)/shard_map/all_to_all | solution.py:530
  59.4 1.9 %copy-start.1 = (f32[32,256,128]{2,1,0:T(8,128)}, f32[32,256,128]{2,1,0:T(8,128)S(1)}, u32[]{:S(2)}) copy-start(f32[32,256,128]{2,1,0:T(8,128)S(1)} %shard_map.78.skip) | copy-start | bytes 12582916
  63.7 2.2 %copy-start.2 = (f32[32,256,128]{2,1,0:T(8,128)S(1)}, f32[32,256,128]{2,1,0:T(8,128)}, u32[]{:S(2)}) copy-start(f32[32,256,128]{2,1,0:T(8,128)} %copy-done.1) | copy-start | bytes 12582916
where the time goes:
time: 68.2 us; the launch traced here: 67.9 us
  starting transfers between devices  25.7 us (38%)
  Pallas kernels  25.2 us (37%)
  waiting for transfers between devices  8.94 us (13%)
  local copies, waits for them, and re-layouts  7.82 us (11%)
    pallas_call x7, Pallas kernels, vmem_call(): pl.pallas_call(kernel, out_shape=out_shape, in_specs=[VMEM for _ in args]...  21.7 us
    unnamed x23, local copies, waits for them, and re-layouts  7.47 us
    all_to_all x1, starting transfers between devices, local(): own = lax.all_to_all(pooled, 'gy', 0, 0)  7.33 us
    all_to_all x1, waiting for transfers between devices, local(): own = lax.all_to_all(pooled, 'gy', 0, 0)  5.58 us
    all_to_all x1, starting transfers between devices, local(): parts = lax.all_to_all(parts, 'gy', 0, 0)  4.83 us
    ppermute x1, starting transfers between devices, local(): gr = lax.ppermute(own[:, 0, :], 'gx', ring(nx, -1))  3.73 us
    ppermute x1, starting transfers between devices, local(): got_a = lax.ppermute(send_a, 'gx', swap(nx, 0))  3.21 us
    all_to_all x1, waiting for transfers between devices, local(): parts = lax.all_to_all(parts, 'gy', 0, 0)  2.35 us
  transfers between devices with their start and end apart: 8, of which 4 were waited for; matrix products, arithmetic and copies ran while one was open for 1% of the time, Pallas kernels for 26%

commit v1 on v0

v1 whole, which is shorter than its diff:
```python
import jax
import jax.numpy as jnp
from jax import lax
from jax.experimental import pallas as pl
from jax.experimental.pallas import tpu as pltpu
from jax.sharding import PartitionSpec as P

POOL = 16
F32 = jnp.float32
BF16 = jnp.bfloat16
VMEM = pl.BlockSpec(memory_space=pltpu.VMEM)
LIMIT = 12 << 20


def iota(shape, dim):
    return lax.broadcasted_iota(jnp.int32, shape, dim)


def dot(a, b):
    return jnp.dot(a, b, preferred_element_type=F32)


def shape(*dims, dtype=BF16):
    return jax.ShapeDtypeStruct(dims, dtype)


def vmem_call(kernel, out_shape, args, scratch=(), flops=0, nbytes=0, far=()):
    args = [
        pltpu.with_memory_space_constraint(arg, pltpu.HBM) if i in far else arg
        for i, arg in enumerate(args)
    ]
    single = not isinstance(out_shape, (list, tuple))
    return pl.pallas_call(
        kernel,
        out_shape=out_shape,
        in_specs=[
            pl.BlockSpec(memory_space=pltpu.HBM) if i in far else VMEM for i in range(len(args))
        ],
        out_specs=VMEM if single else [VMEM for _ in out_shape],
        scratch_shapes=list(scratch),
        compiler_params=pltpu.CompilerParams(vmem_limit_bytes=LIMIT),
        cost_estimate=pl.CostEstimate(flops=flops, bytes_accessed=nbytes, transcendentals=0),
    )(*args)


def side_flags(axis):
    at, count = lax.axis_index(axis), lax.axis_size(axis)
    even = lax.rem(at, 2) == 0

    def number(flag):
        return jnp.where(flag, 1.0, 0.0).astype(F32)

    inner_left, inner_right = at > 0, at < count - 1
    left = number(jnp.logical_not(even)), number(jnp.logical_and(even, inner_left))
    right = number(even), number(jnp.logical_and(jnp.logical_not(even), inner_right))
    return left, right


def mix(a, b, flags):
    return (a.astype(F32) * flags[0] + b.astype(F32) * flags[1]).astype(BF16)


def scaled(v, m):
    return (v.astype(F32) * m).astype(BF16)


def is_even(axis):
    return jnp.where(lax.rem(lax.axis_index(axis), 2) == 0, 1, 0)


def pack_kernel(feat, planes, gy_a, gy_b, held, sems):
    chunks, _, count = held.shape[:3]

    def copy(i):
        return pltpu.make_async_copy(
            feat.at[:, i * count : (i + 1) * count], held.at[i], sems.at[i]
        )

    for i in range(chunks):
        copy(i).start()
    row, col = iota((256, 256), 0), iota((256, 256), 1)
    match = ((row >> 4) == (col & 15)) & ((row & 15) == (col >> 4))
    swap = jnp.where(match, 1.0, 0.0).astype(BF16)
    even = is_even("gy")
    rows_a = pl.multiple_of(even * 224, 32)
    rows_b = pl.multiple_of((1 - even) * 224, 32)
    for i in range(chunks):
        copy(i).wait()
        for x in range(0, count, 2):
            both = jnp.concatenate(
                [held[i, :, x].reshape(256, 128), held[i, :, x + 1].reshape(256, 128)], axis=1
            )
            moved = dot(swap, both).astype(BF16)
            planes[i * count + x] = moved[:, :128]
            planes[i * count + x + 1] = moved[:, 128:]
    gy_a[...] = planes[:, pl.ds(rows_a, 32), :]
    gy_b[...] = planes[:, pl.ds(rows_b, 32), :]


def pack(features):
    size_x = features.shape[1]
    step = 8
    return pl.pallas_call(
        pack_kernel,
        in_specs=[pl.BlockSpec(memory_space=pltpu.HBM)],
        out_specs=[VMEM] * 3,
        out_shape=[shape(size_x, 256, 128), shape(size_x, 32, 128), shape(size_x, 32, 128)],
        scratch_shapes=[
            pltpu.VMEM((size_x // step, 16, step, 16, 128), BF16),
            pltpu.SemaphoreType.DMA((size_x // step,)),
        ],
        compiler_params=pltpu.CompilerParams(vmem_limit_bytes=LIMIT),
        cost_estimate=pl.CostEstimate(
            flops=2 * 256 * 256 * 128 * size_x, bytes_accessed=5 << 20, transcendentals=0
        ),
    )(features)


def band(w, t_ref):
    copies = jnp.where((iota((16, 256), 1) & 15) == iota((16, 256), 0), 1.0, 0.0).astype(BF16)
    wide = dot(w, copies)
    group = iota((16, 256), 1) >> 4
    for c in range(3):
        for x in range(2):
            for y in range(2):
                total = jnp.zeros((16, 256), F32)
                for a in range(3):
                    for b in range(3):
                        k = 9 * a + 3 * b + c
                        here = group == 4 * (x + a) + y + b
                        total = jnp.where(here, wide[16 * k : 16 * k + 16], total)
                at = 16 * (4 * c + 2 * x + y)
                t_ref[at : at + 16, :] = total.astype(BF16)


def shifted_sum(acc, rows, half):
    lanes = slice(half * 128, half * 128 + 128)
    lane = iota((rows, 128), 1)
    before = pltpu.roll(acc[0:rows, lanes], 1, 1)
    after = pltpu.roll(acc[2 * rows : 3 * rows, lanes], 127, 1)
    total = acc[rows : 2 * rows, lanes]
    total = total + jnp.where(lane > 0, before, 0.0)
    total = total + jnp.where(lane < 127, after, 0.0)
    return jnp.maximum(total, 0.0)


def window(rows_of):
    return jnp.concatenate([rows_of(x) for x in range(4)], axis=0)


def conv_pair(t, first, second):
    acc = dot(t[...], jnp.concatenate([first, second], axis=1))
    return shifted_sum(acc, 64, 0), shifted_sum(acc, 64, 1)


def interior_kernel(planes, w, f1, rims, faces, t1, t2):
    size_x = planes.shape[0]
    rims[0] = planes[:, 0:32]
    rims[1] = planes[:, 224:256]
    faces[0] = planes[0:2]
    faces[1] = planes[size_x - 2 : size_x]
    band(w[0:432, :], t1)
    band(w[432:864, :], t2)

    def piece(at, j):
        return window(lambda x: planes[at + x, 32 * j : 32 * j + 64])

    def store(at, j, value):
        for x in range(2):
            f1[at + x, 32 * j + 32 : 32 * j + 64] = value[32 * x : 32 * x + 32].astype(BF16)

    def step(p, carry):
        at = 4 * p
        for j in range(7):
            for h, value in enumerate(conv_pair(t1, piece(at, j), piece(at + 2, j))):
                store(at + 2 * h, j, value)
        return carry

    lax.fori_loop(0, (size_x - 2) // 4, step, 0, unroll=7)
    at = size_x - 4
    for pair in ((0, 1), (2, 3), (4, 5), (5, 6)):
        for j, value in zip(pair, conv_pair(t1, piece(at, pair[0]), piece(at, pair[1]))):
            store(at, j, value)


def rim_kernel(inner, rims, faces, gy_a, gy_b, t1, f1, send_a, send_b, halo):
    size_x = rims.shape[1]
    left, right = side_flags("gy")
    y_left, y_right = left[0] + left[1], right[0] + right[1]

    def fill(x, carry):
        halo[0, x] = mix(gy_a[x], gy_b[x], left)
        halo[1, x] = mix(gy_a[x], gy_b[x], right)
        return carry

    lax.fori_loop(0, size_x, fill, 0, unroll=4)
    even = is_even("gx")
    for send, side in ((send_a, even), (send_b, 1 - even)):
        for j in range(2):
            x = side * (size_x - 2) + j
            send[j, 0:32] = halo[0, x]
            send[j, 32:288] = faces[side, j]
            send[j, 288:320] = halo[1, x]

    def step(p, carry):
        at = 2 * p
        low = window(lambda x: jnp.concatenate([halo[0, at + x], rims[0, at + x]], axis=0))
        high = window(lambda x: jnp.concatenate([rims[1, at + x], halo[1, at + x]], axis=0))
        low, high = conv_pair(t1, low, high)
        for x in range(2):
            cut = slice(32 * x, 32 * x + 16), slice(32 * x + 16, 32 * x + 32)
            f1[at + x, 0:16] = (low[cut[0]] * y_left).astype(BF16)
            f1[at + x, 16:32] = low[cut[1]].astype(BF16)
            f1[at + x, 32:256] = inner[at + x, 32:256]
            f1[at + x, 256:272] = high[cut[0]].astype(BF16)
            f1[at + x, 272:288] = (high[cut[1]] * y_right).astype(BF16)
        return carry

    lax.fori_loop(0, (size_x - 2) // 2, step, 0, unroll=15)


def fold_rows(value):
    return jnp.sum(value.astype(F32).reshape(4, 16, 128), axis=0)


def middle_kernel(f1, t2, second, f1_ends, psum):
    size_x = f1.shape[0] + 2
    f1_ends[0:2] = f1[0:2]
    f1_ends[2:4] = f1[size_x - 4 : size_x - 2]
    psum[...] = jnp.zeros(psum.shape, F32)

    def step(q, carry):
        at = 2 * q - 2
        summed = jnp.zeros((16, 128), F32)

        def piece(j):
            return window(lambda x: f1[at + x, 32 * j : 32 * j + 64])

        for j in range(0, 8, 2):
            for h, value in enumerate(conv_pair(t2, piece(j), piece(j + 1))):
                value = value.astype(BF16)
                row = 32 * (j + h)
                for x in range(2):
                    second[at + x, row : row + 32] = value[32 * x : 32 * x + 32]
                summed = summed + fold_rows(value)
        psum[q // (POOL // 2)] += summed
        return carry

    lax.fori_loop(1, size_x // 2 - 1, step, 0, unroll=14)


def edge_kernel(
    inner, f1_ends, send_a, send_b, far_a, far_b, psum_in, t1, t2, left_out, right_out,
    pooled, fe, fx, got_a, got_b, sems,
):
    fetches = [
        pltpu.make_async_copy(far_a, got_a, sems.at[0]),
        pltpu.make_async_copy(far_b, got_b, sems.at[1]),
    ]
    for fetch in fetches:
        fetch.start()
    half = left_out.shape[0]
    size_x = 2 * half
    moved = iter(range(size_x - 4))

    def put(x, rows, value):
        if x < half:
            left_out[x, rows] = value
        else:
            right_out[x - half, rows] = value

    def carry_over():
        for at in (next(moved, None), next(moved, None)):
            if at is not None:
                put(at + 2, slice(0, 256), inner[at])

    x_left, x_right = side_flags("gx")
    y_left, y_right = side_flags("gy")
    y_left, y_right = y_left[0] + y_left[1], y_right[0] + y_right[1]
    even = is_even("gx").astype(F32)
    for fetch in fetches:
        fetch.wait()
    for j in range(2):
        fe[0, j] = mix(got_a[j], got_b[j], x_left)
        fe[0, 2 + j] = mix(send_a[j], send_b[j], (1.0 - even, even))
        fe[1, j] = mix(send_a[j], send_b[j], (even, 1.0 - even))
        fe[1, 2 + j] = mix(got_a[j], got_b[j], x_right)
    keeps = ((x_left[0] + x_left[1], 1.0), (1.0, x_right[0] + x_right[1]))
    for j in range(9):
        carry_over()
        pieces = [window(lambda x: fe[s, x, 32 * j : 32 * j + 64]) for s in range(2)]
        for s, value in enumerate(conv_pair(t1, *pieces)):
            for x in range(2):
                for y in range(2):
                    part = value[32 * x + 16 * y : 32 * x + 16 * y + 16] * keeps[s][x]
                    if j == 0 and y == 0:
                        part = part * y_left
                    if j == 8 and y == 1:
                        part = part * y_right
                    row = 32 * j + 16 * y
                    fx[s, x, row : row + 16] = part.astype(BF16)

    def left(j):
        cut = slice(32 * j, 32 * j + 64)
        return window(lambda x: fx[0, x, cut] if x < 2 else f1_ends[x - 2, cut])

    def right(j):
        cut = slice(32 * j, 32 * j + 64)
        return window(lambda x: f1_ends[2 + x, cut] if x < 2 else fx[1, x - 2, cut])

    sums = [psum_in[0], psum_in[1]]
    for j in range(8):
        carry_over()
        for s, value in enumerate(conv_pair(t2, left(j), right(j))):
            value = value.astype(BF16)
            for x in range(2):
                cut = slice(32 * j, 32 * j + 32)
                put(s * (size_x - 2) + x, cut, value[32 * x : 32 * x + 32])
            sums[s] = sums[s] + fold_rows(value)

    z, lane = iota((128, 128), 0), iota((128, 128), 1)
    gather = jnp.where((z >> 4) == (lane & 7), 1.0, 0.0).astype(F32)
    keep = (iota((16, 128), 1) >> 3) == iota((16, 128), 0)
    results = []
    for s in range(2):
        cells = jnp.dot(
            sums[s], gather, preferred_element_type=F32, precision=lax.Precision.HIGHEST
        )
        row = jnp.sum(jnp.where(keep, cells, 0.0), axis=0, keepdims=True) * (1.0 / POOL**3)
        results.append(row)
    both = jnp.concatenate(results, axis=0)
    for d in range(16):
        pooled[d] = both


def split3(v):
    a = v.astype(BF16)
    v = v - a.astype(F32)
    b = v.astype(BF16)
    c = (v - b.astype(F32)).astype(BF16)
    return a, b, c


def swap_groups(rows):
    lane = iota((256, 128), 1)
    major, minor = iota((256, 128), 0) >> 4, iota((256, 128), 0) & 15
    spread = jnp.broadcast_to(rows[:, None, :], (16, 16, 128)).reshape(256, 128)
    spread = jnp.where((lane >> 3) == minor, spread, 0.0)
    l0, l1 = iota((128, 128), 0), iota((128, 128), 1)
    fold = jnp.where((l0 & 7) == (l1 & 7), 1.0, 0.0).astype(BF16)
    out = []
    for piece in split3(spread):
        moved = jnp.where((lane >> 3) == major, dot(piece, fold), 0.0)
        out.append(jnp.sum(moved.reshape(16, 16, 128), axis=0))
    return out


def lift_slabs(slabs, w_lift):
    columns = []
    for slab in slabs:
        pieces = [v.astype(BF16) for v in swap_groups(slab)]
        columns.append(jnp.concatenate(pieces, axis=0))
    stacked = jnp.concatenate(columns, axis=1)
    lift3 = jnp.concatenate([w_lift] * 3, axis=1)
    return jnp.maximum(dot(lift3, stacked), 0.0).astype(BF16)


def taps(partial, count):
    lane = iota((count, 128), 1)
    y, z = lane >> 3, lane & 7
    total = jnp.zeros((count, 128), F32)
    for k in range(9):
        b, c = k // 3 - 1, k % 3 - 1
        piece = partial[k * count : (k + 1) * count, :]
        step = 8 * b + c
        if step:
            piece = pltpu.roll(piece, (-step) % 128, 1)
        good = None
        if b:
            good = (y < 15) if b > 0 else (y > 0)
        if c:
            inside = (z < 7) if c > 0 else (z > 0)
            good = inside if good is None else good & inside
        total = total + (piece if good is None else jnp.where(good, piece, 0.0))
    return total


def own_kernel(own, w_lift, w_coarse, out):
    count = w_coarse.shape[0] // 27
    lifted = lift_slabs([own[:, 0, :], own[:, 1, :]], w_lift[...])
    partial = dot(w_coarse[...], lifted)
    for x in range(2):
        total = jnp.zeros((count, 128), F32)
        for slab in range(2):
            a = slab - x + 1
            piece = partial[9 * a * count : 9 * (a + 1) * count, slab * 128 : slab * 128 + 128]
            total = total + taps(piece, count)
        out[x] = total


def beside_kernel(mine, gl, gr, w_lift, w_coarse, w_dec, out):
    count = w_coarse.shape[0] // 27
    at, last = lax.axis_index("gx"), lax.axis_size("gx") - 1
    m_left = jnp.where(at > 0, 1.0, 0.0).astype(F32)
    m_right = jnp.where(at < last, 1.0, 0.0).astype(F32)
    lifted = lift_slabs([gl[...] * m_left, gr[...] * m_right], w_lift[...])
    for x in range(2):
        a = 2 * x
        rows = w_coarse[9 * a * count : 9 * (a + 1) * count, :]
        total = mine[x] + taps(dot(rows, lifted[:, x * 128 : x * 128 + 128]), count)
        coarse = jnp.maximum(total, 0.0).astype(BF16)
        pieces = swap_groups(dot(w_dec[...], coarse))
        out[:, x, :] = pieces[0] + pieces[1] + pieces[2]


def skip_planes(matrix, second, at):
    both = jnp.concatenate([second[at], second[at + 1]], axis=1)
    result = dot(matrix[...], both)
    return result[:, :128], result[:, 128:]


def skip_kernel(second, w_join, matrix, up, ahead):
    r, c = iota((256, 16), 0), iota((256, 16), 1)
    rows = jnp.where((r >> 4) == c, 1.0, 0.0).astype(BF16)
    mixed = dot(rows, w_join[...]).astype(BF16)
    up[...] = mixed[:, 16:32]
    r, c = iota((16, 256), 0), iota((16, 256), 1)
    cols = jnp.where((c & 15) == r, 1.0, 0.0).astype(BF16)
    r, c = iota((256, 256), 0), iota((256, 256), 1)
    match = (r & 15) == (c >> 4)
    matrix[...] = jnp.where(match, dot(mixed[:, 0:16], cols), 0.0).astype(BF16)
    for at in range(0, ahead.shape[0], 2):
        ahead[at], ahead[at + 1] = skip_planes(matrix, second, at)


def join_kernel(left, right, ahead, matrix, up, parts, out, held, sems):
    half = left.shape[0]
    keep = (iota((16, 128), 1) >> 3) == iota((16, 128), 0)
    l0, l1 = iota((128, 128), 0), iota((128, 128), 1)
    widen = jnp.where((l0 & 7) == (l1 >> 4), 1.0, 0.0).astype(BF16)
    total = parts[0]
    for d in range(1, 16):
        total = total + parts[d]
    terms = []
    for block in range(2):
        decoded = jnp.broadcast_to(total[block : block + 1, :], (16, 128))
        decoded = jnp.where(keep, decoded, 0.0).astype(BF16)
        terms.append(dot(up[...], dot(decoded, widen).astype(BF16)))
    chunks, _, count = held.shape[:3]

    def copy(i):
        return pltpu.make_async_copy(
            held.at[i], out.at[:, i * count : (i + 1) * count], sems.at[i]
        )

    for i in range(chunks):
        for x in range(0, count, 2):
            at = i * count + x
            if at < ahead.shape[0]:
                skips = ahead[at], ahead[at + 1]
            else:
                skips = skip_planes(matrix, (left, right)[at // half], at % half)
            for h in range(2):
                value = (skips[h] + terms[at // POOL]).astype(BF16)
                held[i, :, x + h] = value.reshape(16, 16, 128)
        copy(i).start()
    for i in range(chunks):
        copy(i).wait()


def join(left, right, ahead, matrix, up, parts):
    size_x = 2 * left.shape[0]
    step = 4
    return pl.pallas_call(
        join_kernel,
        in_specs=[VMEM] * 6,
        out_specs=pl.BlockSpec(memory_space=pltpu.HBM),
        out_shape=shape(16, size_x, 16, 128),
        scratch_shapes=[
            pltpu.VMEM((size_x // step, 16, step, 16, 128), BF16),
            pltpu.SemaphoreType.DMA((size_x // step,)),
        ],
        compiler_params=pltpu.CompilerParams(vmem_limit_bytes=LIMIT),
        cost_estimate=pl.CostEstimate(
            flops=2 * 256 * 256 * 128 * size_x, bytes_accessed=4 << 20, transcendentals=0
        ),
    )(left, right, ahead, matrix, up, parts)


def local(features, w_first, w_second, w_lift, w_coarse, w_decode, w_joining):
    size_x = features.shape[1]
    nx, ny = lax.axis_size("gx"), lax.axis_size("gy")
    gy = lax.axis_index("gy")

    def ring(count, step):
        return [(i, (i + step) % count) for i in range(count)]

    def swap(count, odd):
        return [(i, (((i + odd) ^ 1) - odd) % count) for i in range(count)]

    planes, gy_a, gy_b = pack(pltpu.with_memory_space_constraint(features, pltpu.HBM))
    gy_a = lax.ppermute(gy_a, "gy", swap(ny, 0))
    gy_b = lax.ppermute(gy_b, "gy", swap(ny, 1))

    w_fine = jnp.concatenate([w_first, w_second], axis=0).reshape(864, 16)
    first = shape(size_x - 2, 288, 128)
    f1, rims, faces, t1, t2 = vmem_call(
        interior_kernel,
        [
            first,
            shape(2, size_x, 32, 128),
            shape(2, 2, 256, 128),
            shape(192, 256),
            shape(192, 256),
        ],
        (planes, w_fine),
        flops=2 * 192 * 256 * 256 * 53,
        nbytes=4 << 20,
    )
    f1, send_a, send_b = vmem_call(
        rim_kernel,
        [first, shape(2, 320, 128), shape(2, 320, 128)],
        (f1, rims, faces, gy_a, gy_b, t1),
        scratch=[pltpu.VMEM((2, size_x, 32, 128), BF16)],
        flops=2 * 192 * 256 * 256 * 15,
        nbytes=1 << 20,
    )
    got_a = lax.ppermute(send_a, "gx", swap(nx, 0))
    got_b = lax.ppermute(send_b, "gx", swap(nx, 1))
    second, f1_ends, psum = vmem_call(
        middle_kernel,
        [shape(size_x - 4, 256, 128), shape(4, 288, 128), shape(2, 16, 128, dtype=F32)],
        (f1, t2),
        flops=2 * 192 * 256 * 256 * 56,
        nbytes=6 << 20,
    )
    half = shape(size_x // 2, 256, 128)
    *seconds, pooled = vmem_call(
        edge_kernel,
        [half, half, shape(16, 2, 128, dtype=F32)],
        (second, f1_ends, send_a, send_b, got_a, got_b, psum, t1, t2),
        scratch=[
            pltpu.VMEM((2, 4, 320, 128), BF16),
            pltpu.VMEM((2, 2, 288, 128), BF16),
            pltpu.VMEM((2, 320, 128), BF16),
            pltpu.VMEM((2, 320, 128), BF16),
            pltpu.SemaphoreType.DMA((2,)),
        ],
        far=(4, 5),
        flops=2 * 192 * 256 * 256 * 17,
        nbytes=1 << 20,
    )

    count = w_coarse.shape[0]
    w_rows = jnp.transpose(w_coarse, (1, 0, 2)).reshape(27 * count, w_coarse.shape[2])
    w_dec = lax.dynamic_slice_in_dim(w_decode, gy * count, count, axis=1)
    own = lax.all_to_all(pooled, "gy", 0, 0)
    gl = lax.ppermute(own[:, 1, :], "gx", ring(nx, 1))
    gr = lax.ppermute(own[:, 0, :], "gx", ring(nx, -1))
    mine = vmem_call(
        own_kernel,
        shape(2, count, 128, dtype=F32),
        (own, w_lift, w_rows),
        flops=2 * 864 * 512 * 512,
        nbytes=2 << 20,
    )
    parts = vmem_call(
        beside_kernel,
        shape(16, 2, 128, dtype=F32),
        (mine, gl, gr, w_lift, w_rows, w_dec),
        flops=2 * 864 * 512 * 256,
        nbytes=2 << 20,
    )
    parts = lax.all_to_all(parts, "gy", 0, 0)
    matrix, up, ahead = vmem_call(
        skip_kernel,
        [shape(256, 256), shape(256, 16), shape(8, 256, 128, dtype=F32)],
        (seconds[0], w_joining),
        flops=2 * 256 * 256 * 128 * 8,
        nbytes=2 << 20,
    )
    return join(*seconds, ahead, matrix, up, parts)


def solution(mesh):
    in_specs = (P(None, "gx", "gy", None), P(), P(), P(), P("gy", None, None), P(), P())
    out_specs = P(None, "gx", "gy", None)
    return jax.shard_map(local, mesh=mesh, in_specs=in_specs, out_specs=out_specs, check_vma=False)
```

time: 68.2 us -> 63.9 us (0.937)
  waiting for transfers between devices: 8.94 us -> 18.1 us
  Pallas kernels: 25.2 us -> 17.3 us
  local copies, waits for them, and re-layouts: 7.82 us -> 1.17 us
  starting transfers between devices: 25.7 us -> 26.9 us
    pallas_call x8, Pallas kernels: 23.7 us -> 14.2 us  [the longest x7 12.5 us: vmem_call(): pl.pallas_call(kernel, out_shape=out_shape, in_specs=[pl.BlockSpec(memory...]
    unnamed x23 -> x17, local copies, waits for them, and re-layouts: 7.47 us -> 0.82 us
    ppermute x1, waiting for transfers between devices: 0.01 us -> 3.16 us  [local(): got_b = lax.ppermute(send_b, 'gx', swap(nx, 1))]
    all_to_all x1, waiting for transfers between devices: 2.35 us -> 5.3 us  [local(): parts = lax.all_to_all(parts, 'gy', 0, 0)]
    ppermute x1, waiting for transfers between devices: 0.94 us -> 3.82 us  [local(): gy_b = lax.ppermute(gy_b, 'gy', swap(ny, 1))]
    pallas_call x1, Pallas kernels: 1.47 us -> 3.07 us  [pack(): pl.pallas_call(pack_kernel, in_specs=[pl.BlockSpec(memory_space=pltpu.HBM...]
    all_to_all x1, starting transfers between devices: 7.33 us -> 8.57 us  [local(): own = lax.all_to_all(pooled, 'gy', 0, 0)]
  transfers between devices with their start and end apart: 8 -> 8, of which waited for: 4 -> 6; matrix products, arithmetic and copies ran while one was open for 1% -> 1% of each run, Pallas kernels for 26% -> 10%
where the time goes in v1:
time: 63.9 us; the launch traced here: 63.6 us
  starting transfers between devices  26.9 us (42%)
  waiting for transfers between devices  18.1 us (28%)
  Pallas kernels  17.3 us (27%)
  local copies, waits for them, and re-layouts  1.17 us (2%)
    pallas_call x7, Pallas kernels, vmem_call(): pl.pallas_call(kernel, out_shape=out_shape, in_specs=[pl.BlockSpec(memory...  12.5 us
    all_to_all x1, starting transfers between devices, local(): own = lax.all_to_all(pooled, 'gy', 0, 0)  8.57 us
    all_to_all x1, waiting for transfers between devices, local(): own = lax.all_to_all(pooled, 'gy', 0, 0)  5.58 us
    all_to_all x1, waiting for transfers between devices, local(): parts = lax.all_to_all(parts, 'gy', 0, 0)  5.3 us
    all_to_all x1, starting transfers between devices, local(): parts = lax.all_to_all(parts, 'gy', 0, 0)  4.81 us
    ppermute x1, waiting for transfers between devices, local(): gy_b = lax.ppermute(gy_b, 'gy', swap(ny, 1))  3.82 us
    ppermute x1, starting transfers between devices, local(): got_a = lax.ppermute(send_a, 'gx', swap(nx, 0))  3.22 us
    ppermute x1, waiting for transfers between devices, local(): got_b = lax.ppermute(send_b, 'gx', swap(nx, 1))  3.16 us
  transfers between devices with their start and end apart: 8, of which 6 were waited for; matrix products, arithmetic and copies ran while one was open for 1% of the time, Pallas kernels for 10%

profile of v1, /device:TPU:1, one launch (start us, length us, event | category | flops | bytes accessed | tf_op | source)
XLA Modules:
  0.0 63.6 jit_solution(17570408970748244271)
XLA Ops:
  0.0 0.0 copy-start
  0.0 0.0 copy-start.6
  0.0 0.0 copy-start.5
  0.0 3.1 %shard_map.73 = (bf16[32,256,128]{2,1,0:T(8,128)(2,1)S(1)}, bf16[32,32,128]{2,1,0:T(8,128)(2,1)}, bf16[32,32,128]{2,1,0:T(8,128)(2,1)S(1)}) custom-call(bf16[16,32,16,128]{3,2,1,0:T(8,128)(2,1)} %feat.1), custom_call_target="tpu_custom_call" | custom-call | flops 536870912 | bytes 5242880 | tf_op jit(solution)/shard_map/pallas_call | solution.py:103
  3.1 1.5 %collective-permute-start = (bf16[32,32,128]{2,1,0:T(8,128)(2,1)}, bf16[32,32,128]{2,1,0:T(8,128)(2,1)S(1)}, u32[]{:S(2)}, u32[]{:S(2)}) collective-permute-start(bf16[32,32,128]{2,1,0:T(8,128)(2,1)} %get-tuple-element.29), channel_id=1, source_target_pairs={{0,1},{1,0},{2,3},{3,2},{4,5},{5,4},{6,7},{7,6},{8,9},{9,8},{10,11... | collective-permute-start | bytes 786440 | tf_op jit(solution)/shard_map/ppermute | solution.py:502
  4.5 1.4 %collective-permute-start.1 = (bf16[32,32,128]{2,1,0:T(8,128)(2,1)S(1)}, bf16[32,32,128]{2,1,0:T(8,128)(2,1)S(1)}, u32[]{:S(2)}, u32[]{:S(2)}) collective-permute-start(bf16[32,32,128]{2,1,0:T(8,128)(2,1)S(1)} %get-tuple-element.30), channel_id=1, source_target_pairs={{0,15},{1,2},{2,1},{3,4},{4,3},{5,6},{6,5},{7,8},{8,7},{9,10},{10,... | collective-permute-start | bytes 786440 | tf_op jit(solution)/shard_map/ppermute | solution.py:503
  5.9 0.0 copy-done.6
  5.9 0.0 copy-done.5
  5.9 0.1 pad_maximum_fusion
  6.0 0.3 copy.13
  6.3 2.4 %shard_map.74 = (bf16[30,288,128]{2,1,0:T(8,128)(2,1)S(1)}, bf16[2,32,32,128]{3,2,1,0:T(8,128)(2,1)S(1)}, bf16[2,2,256,128]{3,2,1,0:T(8,128)(2,1)S(1)}, bf16[192,256]{1,0:T(8,128)(2,1)S(1)}, bf16[192,256]{1,0:T(8,128)(2,1)S(1)}) custom-call(bf16[32,256,128]{2,1,0:T(8,128)(2,1)S(1)} %get-tuple-element.25.planes, bf16[864,16]{1,0:T(8,128)(2,1)S(1)} %bitcast.12), custom_call_target="tpu_custom_call" | custom-call | flops 1333788672 | bytes 4194304 | tf_op jit(solution)/shard_map/pallas_call | solution.py:33
  8.7 0.0 collective-permute-done.gy_a
  8.7 3.8 %collective-permute-done.1.gy_b = bf16[32,32,128]{2,1,0:T(8,128)(2,1)S(1)} collective-permute-done((bf16[32,32,128]{2,1,0:T(8,128)(2,1)S(1)}, bf16[32,32,128]{2,1,0:T(8,128)(2,1)S(1)}, u32[]{:S(2)}, u32[]{:S(2)}) %collective-permute-start.1) | collective-permute-done | bytes 262176 | tf_op jit(solution)/shard_map/ppermute | solution.py:503
  12.6 1.0 %shard_map.75 = (bf16[30,288,128]{2,1,0:T(8,128)(2,1)S(1)}, bf16[2,320,128]{2,1,0:T(8,128)(2,1)S(1)}, bf16[2,320,128]{2,1,0:T(8,128)(2,1)S(1)}) custom-call(bf16[30,288,128]{2,1,0:T(8,128)(2,1)S(1)} %get-tuple-element.26.inner, bf16[2,32,32,128]{3,2,1,0:T(8,128)(2,1)S(1)} %get-tuple-element.27.rims, bf16[2,2,256,128]{3,2,1,0:T(8,128)(2,1)S(1)} %get-tuple-element.28.faces, ...), custom_call_target="tpu_custom_call" | custom-call | flops 377487360 | bytes 1048576 | tf_op jit(solution)/shard_map/pallas_call | solution.py:33
  13.6 3.2 %collective-permute-start.2 = (bf16[2,320,128]{2,1,0:T(8,128)(2,1)S(1)}, bf16[2,320,128]{2,1,0:T(8,128)(2,1)S(1)}, u32[]{:S(2)}, u32[]{:S(2)}) collective-permute-start(bf16[2,320,128]{2,1,0:T(8,128)(2,1)S(1)} %get-tuple-element.36.send_a), channel_id=1, source_target_pairs={{0,16},{16,0},{32,48},{48,32},{64,80},{80,64},{96,112},{112,96},{1... | collective-permute-start | bytes 491528 | tf_op jit(solution)/shard_map/ppermute | solution.py:528
  16.8 2.3 %collective-permute-start.3 = (bf16[2,320,128]{2,1,0:T(8,128)(2,1)S(1)}, bf16[2,320,128]{2,1,0:T(8,128)(2,1)S(1)}, u32[]{:S(2)}, u32[]{:S(2)}) collective-permute-start(bf16[2,320,128]{2,1,0:T(8,128)(2,1)S(1)} %get-tuple-element.37.send_b), channel_id=1, source_target_pairs={{0,112},{16,32},{32,16},{48,64},{64,48},{80,96},{96,80},{112,0},{1... | collective-permute-start | bytes 491528 | tf_op jit(solution)/shard_map/ppermute | solution.py:529
  19.1 2.4 %shard_map.76 = (bf16[28,256,128]{2,1,0:T(8,128)(2,1)S(1)}, bf16[4,288,128]{2,1,0:T(8,128)(2,1)S(1)}, f32[2,16,128]{2,1,0:T(8,128)S(1)}) custom-call(bf16[30,288,128]{2,1,0:T(8,128)(2,1)S(1)} %get-tuple-element.32.f1, bf16[192,256]{1,0:T(8,128)(2,1)S(1)} %get-tuple-element.33.t2), custom_call_target="tpu_custom_call" | custom-call | flops 1409286144 | bytes 6291456 | tf_op jit(solution)/shard_map/pallas_call | solution.py:33
  21.5 0.0 copy-start.7
  21.5 0.0 copy-start.1
  21.5 0.0 collective-permute-done.2.far_a
  21.5 0.0 copy-start.3
  21.5 3.2 %collective-permute-done.3.far_b = bf16[2,320,128]{2,1,0:T(8,128)(2,1)S(1)} collective-permute-done((bf16[2,320,128]{2,1,0:T(8,128)(2,1)S(1)}, bf16[2,320,128]{2,1,0:T(8,128)(2,1)S(1)}, u32[]{:S(2)}, u32[]{:S(2)}) %collective-permute-start.3) | collective-permute-done | bytes 163872 | tf_op jit(solution)/shard_map/ppermute | solution.py:529
  24.7 0.0 copy-start.4
  24.7 0.0 copy-done.3
  24.7 0.7 %copy-done.4 = bf16[2,320,128]{2,1,0:T(8,128)(2,1)} copy-done((bf16[2,320,128]{2,1,0:T(8,128)(2,1)}, bf16[2,320,128]{2,1,0:T(8,128)(2,1)S(1)}, u32[]{:S(2)}) %copy-start.4) | copy-done | bytes 163864
  25.3 2.9 %shard_map.77 = (bf16[16,256,128]{2,1,0:T(8,128)(2,1)S(1)}, bf16[16,256,128]{2,1,0:T(8,128)(2,1)S(1)}, f32[16,2,128]{2,1,0:T(2,128)}) custom-call(bf16[28,256,128]{2,1,0:T(8,128)(2,1)S(1)} %get-tuple-element.34.inner, bf16[4,288,128]{2,1,0:T(8,128)(2,1)S(1)} %get-tuple-element.35.f1_ends, bf16[2,320,128]{2,1,0:T(8,128)(2,1)S(1)} %get-tuple-element.36.send_a, ...), custom_call_target="tpu_custom_call" | custom-call | flops 427819008 | bytes 1048576 | tf_op jit(solution)/shard_map/pallas_call | solution.py:33
  28.3 0.0 copy-start.2
  28.3 8.6 %all-to-all-start = ((f32[16,2,128]{2,1,0:T(2,128)}), f32[16,2,128]{2,1,0:T(2,128)S(1)}, u32[]{:S(2)}, u32[]{:S(2)}) async-start(f32[16,2,128]{2,1,0:T(2,128)} %get-tuple-element.44), calls=%async_computation | async-start | bytes 32768 | tf_op jit(solution)/shard_map/all_to_all | solution.py:557
  36.9 0.0 copy-done
  36.9 0.1 constant_dynamic-slice_fusion.w_dec
  37.0 0.0 copy-done.7
  37.0 0.1 copy.14.w_lift
  37.1 5.6 %all-to-all-done.own = f32[16,2,128]{2,1,0:T(2,128)S(1)} async-done(((f32[16,2,128]{2,1,0:T(2,128)}), f32[16,2,128]{2,1,0:T(2,128)S(1)}, u32[]{:S(2)}, u32[]{:S(2)}) %all-to-all-start) | async-done | bytes 16416 | tf_op jit(solution)/shard_map/all_to_all | solution.py:557
  42.7 2.0 %collective-permute-start.4 = (f32[16,128]{1,0:T(8,128)S(1)}, f32[16,128]{1,0:T(8,128)S(1)}, u32[]{:S(2)}, u32[]{:S(2)}) collective-permute-start(f32[16,128]{1,0:T(8,128)S(1)} %bitcast.14), channel_id=1, source_target_pairs={{0,16},{16,32},{32,48},{48,64},{64,80},{80,96},{96,112},{112,0},{1... | collective-permute-start | bytes 24584 | tf_op jit(solution)/shard_map/ppermute | solution.py:558
  44.7 3.1 %collective-permute-start.5 = (f32[16,128]{1,0:T(8,128)S(1)}, f32[16,128]{1,0:T(8,128)S(1)}, u32[]{:S(2)}, u32[]{:S(2)}) collective-permute-start(f32[16,128]{1,0:T(8,128)S(1)} %bitcast.13), channel_id=1, source_target_pairs={{0,112},{16,0},{32,16},{48,32},{64,48},{80,64},{96,80},{112,96},{1... | collective-permute-start | bytes 24584 | tf_op jit(solution)/shard_map/ppermute | solution.py:559
  47.8 0.0 copy-done.1
  47.8 1.0 %shard_map.79.mine = f32[2,32,128]{2,1,0:T(8,128)S(1)} custom-call(f32[16,2,128]{2,1,0:T(2,128)S(1)} %all-to-all-done.own, bf16[512,16]{1,0:T(8,128)(2,1)S(1)} %copy.14.w_lift, bf16[864,512]{1,0:T(8,128)(2,1)S(1)} %bitcast.10), custom_call_target="tpu_custom_call" | custom-call | flops 452984832 | bytes 2097152 | tf_op jit(solution)/shard_map/pallas_call | solution.py:33
  48.8 0.1 collective-permute-done.4.gl
  48.9 0.1 collective-permute-done.5.gr
  49.0 2.3 %shard_map.80 = f32[16,2,128]{2,1,0:T(2,128)} custom-call(f32[2,32,128]{2,1,0:T(8,128)S(1)} %shard_map.79.mine, f32[16,128]{1,0:T(8,128)S(1)} %collective-permute-done.4.gl, f32[16,128]{1,0:T(8,128)S(1)} %collective-permute-done.5.gr, bf16[512,16]{1,0:T(8,128)(2,1)S(1)} %copy.14.w_lift, bf16[864,512]{1,0:T(8,128)(2,1)S(1)} %bitcast.11, ...), custom_call_target="tpu_custom_call" | custom-call | flops 226492416 | bytes 2097152 | tf_op jit(solution)/shard_map/pallas_call | solution.py:33
  51.3 4.8 %all-to-all-start.1 = ((f32[16,2,128]{2,1,0:T(2,128)}), f32[16,2,128]{2,1,0:T(2,128)S(1)}, u32[]{:S(2)}, u32[]{:S(2)}) async-start(f32[16,2,128]{2,1,0:T(2,128)} %shard_map.80), calls=%async_computation.1 | async-start | bytes 32768 | tf_op jit(solution)/shard_map/all_to_all | solution.py:574
  56.1 0.0 copy-done.2
  56.1 0.5 shard_map.78
  56.6 5.3 %all-to-all-done.1.parts = f32[16,2,128]{2,1,0:T(2,128)S(1)} async-done(((f32[16,2,128]{2,1,0:T(2,128)}), f32[16,2,128]{2,1,0:T(2,128)S(1)}, u32[]{:S(2)}, u32[]{:S(2)}) %all-to-all-start.1) | async-done | bytes 16416 | tf_op jit(solution)/shard_map/all_to_all | solution.py:574
  61.9 1.7 %shard_map.81 = bf16[16,32,16,128]{3,2,1,0:T(8,128)(2,1)} custom-call(bf16[16,256,128]{2,1,0:T(8,128)(2,1)S(1)} %get-tuple-element.39.second.left, bf16[16,256,128]{2,1,0:T(8,128)(2,1)S(1)} %get-tuple-element.40.right, f32[8,256,128]{2,1,0:T(8,128)S(1)} %get-tuple-element.41.ahead, bf16[256,256]{1,0:T(8,128)(2,1)S(1)} %get-tuple-element.42.matrix, ...), custom_call_target="tpu_custom_call" | custom-call | flops 536870912 | bytes 4194304 | tf_op jit(solution)/shard_map/pallas_call | solution.py:474
  (1 shorter events, 0.0 us)
Async XLA Ops:
  0.0 36.9 %copy-start = (bf16[16,512]{1,0:T(8,128)(2,1)S(1)}, bf16[16,512]{1,0:T(8,128)(2,1)}, u32[]{:S(2)}) copy-start(bf16[16,512]{1,0:T(8,128)(2,1)} %param.12) | copy-start | bytes 49156
  0.0 5.9 %copy-start.6 = (bf16[27,16,16]{0,2,1:T(8,128)(2,1)S(1)}, bf16[27,16,16]{0,2,1:T(8,128)(2,1)}, u32[]{:S(2)}) copy-start(bf16[27,16,16]{0,2,1:T(8,128)(2,1)} %param.8) | copy-start | bytes 41476
  0.0 5.9 %copy-start.5 = (bf16[27,16,16]{0,2,1:T(8,128)(2,1)S(1)}, bf16[27,16,16]{0,2,1:T(8,128)(2,1)}, u32[]{:S(2)}) copy-start(bf16[27,16,16]{0,2,1:T(8,128)(2,1)} %param.9) | copy-start | bytes 41476
  3.1 5.6 %collective-permute-start = (bf16[32,32,128]{2,1,0:T(8,128)(2,1)}, bf16[32,32,128]{2,1,0:T(8,128)(2,1)S(1)}, u32[]{:S(2)}, u32[]{:S(2)}) collective-permute-start(bf16[32,32,128]{2,1,0:T(8,128)(2,1)} %get-tuple-element.29), channel_id=1, source_target_pairs={{0,1},{1,0},{2,3},{3,2},{4,5},{5,4},{6,7},{7,6},{8,9},{9,8},{10,11... | collective-permute-start | bytes 786440 | tf_op jit(solution)/shard_map/ppermute | solution.py:502
  4.5 8.0 %collective-permute-start.1 = (bf16[32,32,128]{2,1,0:T(8,128)(2,1)S(1)}, bf16[32,32,128]{2,1,0:T(8,128)(2,1)S(1)}, u32[]{:S(2)}, u32[]{:S(2)}) collective-permute-start(bf16[32,32,128]{2,1,0:T(8,128)(2,1)S(1)} %get-tuple-element.30), channel_id=1, source_target_pairs={{0,15},{1,2},{2,1},{3,4},{4,3},{5,6},{6,5},{7,8},{8,7},{9,10},{10,... | collective-permute-start | bytes 786440 | tf_op jit(solution)/shard_map/ppermute | solution.py:503
  13.6 7.9 %collective-permute-start.2 = (bf16[2,320,128]{2,1,0:T(8,128)(2,1)S(1)}, bf16[2,320,128]{2,1,0:T(8,128)(2,1)S(1)}, u32[]{:S(2)}, u32[]{:S(2)}) collective-permute-start(bf16[2,320,128]{2,1,0:T(8,128)(2,1)S(1)} %get-tuple-element.36.send_a), channel_id=1, source_target_pairs={{0,16},{16,0},{32,48},{48,32},{64,80},{80,64},{96,112},{112,96},{1... | collective-permute-start | bytes 491528 | tf_op jit(solution)/shard_map/ppermute | solution.py:528
  16.8 7.9 %collective-permute-start.3 = (bf16[2,320,128]{2,1,0:T(8,128)(2,1)S(1)}, bf16[2,320,128]{2,1,0:T(8,128)(2,1)S(1)}, u32[]{:S(2)}, u32[]{:S(2)}) collective-permute-start(bf16[2,320,128]{2,1,0:T(8,128)(2,1)S(1)} %get-tuple-element.37.send_b), channel_id=1, source_target_pairs={{0,112},{16,32},{32,16},{48,64},{64,48},{80,96},{96,80},{112,0},{1... | collective-permute-start | bytes 491528 | tf_op jit(solution)/shard_map/ppermute | solution.py:529
  21.5 15.5 %copy-start.7 = (bf16[512,16]{0,1:T(8,128)(2,1)S(1)}, bf16[512,16]{0,1:T(8,128)(2,1)}, u32[]{:S(2)}) copy-start(bf16[512,16]{0,1:T(8,128)(2,1)} %param.10) | copy-start | bytes 49156
  21.5 26.3 %copy-start.1 = (bf16[32,27,512]{2,0,1:T(8,128)(2,1)S(1)}, bf16[32,27,512]{2,0,1:T(8,128)(2,1)}, u32[]{:S(2)}) copy-start(bf16[32,27,512]{2,0,1:T(8,128)(2,1)} %param.11) | copy-start | bytes 2654212
  21.5 3.2 %copy-start.3 = (bf16[2,320,128]{2,1,0:T(8,128)(2,1)}, bf16[2,320,128]{2,1,0:T(8,128)(2,1)S(1)}, u32[]{:S(2)}) copy-start(bf16[2,320,128]{2,1,0:T(8,128)(2,1)S(1)} %collective-permute-done.2.far_a) | copy-start | bytes 491524
  24.7 0.7 %copy-start.4 = (bf16[2,320,128]{2,1,0:T(8,128)(2,1)}, bf16[2,320,128]{2,1,0:T(8,128)(2,1)S(1)}, u32[]{:S(2)}) copy-start(bf16[2,320,128]{2,1,0:T(8,128)(2,1)S(1)} %collective-permute-done.3.far_b) | copy-start | bytes 491524
  28.3 27.8 %copy-start.2 = (bf16[16,32]{1,0:T(8,128)(2,1)S(1)}, bf16[16,32]{1,0:T(8,128)(2,1)}, u32[]{:S(2)}) copy-start(bf16[16,32]{1,0:T(8,128)(2,1)} %w_join.1) | copy-start | bytes 3076
  28.3 14.4 %all-to-all-start = ((f32[16,2,128]{2,1,0:T(2,128)}), f32[16,2,128]{2,1,0:T(2,128)S(1)}, u32[]{:S(2)}, u32[]{:S(2)}) async-start(f32[16,2,128]{2,1,0:T(2,128)} %get-tuple-element.44), calls=%async_computation | async-start | bytes 32768 | tf_op jit(solution)/shard_map/all_to_all | solution.py:557
  42.7 6.2 %collective-permute-start.4 = (f32[16,128]{1,0:T(8,128)S(1)}, f32[16,128]{1,0:T(8,128)S(1)}, u32[]{:S(2)}, u32[]{:S(2)}) collective-permute-start(f32[16,128]{1,0:T(8,128)S(1)} %bitcast.14), channel_id=1, source_target_pairs={{0,16},{16,32},{32,48},{48,64},{64,80},{80,96},{96,112},{112,0},{1... | collective-permute-start | bytes 24584 | tf_op jit(solution)/shard_map/ppermute | solution.py:558
  44.7 4.3 %collective-permute-start.5 = (f32[16,128]{1,0:T(8,128)S(1)}, f32[16,128]{1,0:T(8,128)S(1)}, u32[]{:S(2)}, u32[]{:S(2)}) collective-permute-start(f32[16,128]{1,0:T(8,128)S(1)} %bitcast.13), channel_id=1, source_target_pairs={{0,112},{16,0},{32,16},{48,32},{64,48},{80,64},{96,80},{112,96},{1... | collective-permute-start | bytes 24584 | tf_op jit(solution)/shard_map/ppermute | solution.py:559
  51.3 10.7 %all-to-all-start.1 = ((f32[16,2,128]{2,1,0:T(2,128)}), f32[16,2,128]{2,1,0:T(2,128)S(1)}, u32[]{:S(2)}, u32[]{:S(2)}) async-start(f32[16,2,128]{2,1,0:T(2,128)} %shard_map.80), calls=%async_computation.1 | async-start | bytes 32768 | tf_op jit(solution)/shard_map/all_to_all | solution.py:574

commit v2 on v1

--- a/solution.py
+++ b/solution.py
@@ -24,19 +24,31 @@
     return jax.ShapeDtypeStruct(dims, dtype)
 
 
-def vmem_call(kernel, out_shape, args, scratch=(), flops=0, nbytes=0, far=()):
+def vmem_call(kernel, out_shape, args, scratch=(), flops=0, nbytes=0, far=(), far_out=()):
     args = [
         pltpu.with_memory_space_constraint(arg, pltpu.HBM) if i in far else arg
         for i, arg in enumerate(args)
     ]
     single = not isinstance(out_shape, (list, tuple))
+    if far_out:
+        out_shape = [
+            pltpu.HBM(out.shape, out.dtype) if i in far_out else out
+            for i, out in enumerate(out_shape)
+        ]
     return pl.pallas_call(
         kernel,
         out_shape=out_shape,
         in_specs=[
             pl.BlockSpec(memory_space=pltpu.HBM) if i in far else VMEM for i in range(len(args))
         ],
-        out_specs=VMEM if single else [VMEM for _ in out_shape],
+        out_specs=(
+            VMEM
+            if single
+            else [
+                pl.BlockSpec(memory_space=pltpu.HBM) if i in far_out else VMEM
+                for i in range(len(out_shape))
+            ]
+        ),
         scratch_shapes=list(scratch),
         compiler_params=pltpu.CompilerParams(vmem_limit_bytes=LIMIT),
         cost_estimate=pl.CostEstimate(flops=flops, bytes_accessed=nbytes, transcendentals=0),
@@ -68,52 +80,53 @@
     return jnp.where(lax.rem(lax.axis_index(axis), 2) == 0, 1, 0)
 
 
-def pack_kernel(feat, planes, gy_a, gy_b, held, sems):
-    chunks, _, count = held.shape[:3]
-
-    def copy(i):
-        return pltpu.make_async_copy(
-            feat.at[:, i * count : (i + 1) * count], held.at[i], sems.at[i]
+def fetch_planes(far, feat, sems):
+    parts = sems.shape[0]
+    count = far.shape[1] // parts
+    fetches = [
+        pltpu.make_async_copy(
+            far.at[:, i * count : (i + 1) * count],
+            feat.at[:, i * count : (i + 1) * count],
+            sems.at[i],
         )
-
-    for i in range(chunks):
-        copy(i).start()
+        for i in range(parts)
+    ]
+    for fetch in fetches:
+        fetch.start()
+    return fetches, count
+
+
+def rows_kernel(far, gy_a, gy_b, feat, sems):
+    fetches, count = fetch_planes(far, feat, sems)
+    size_x = feat.shape[1]
+    even = is_even("gy")
+    row, col = iota((64, 256), 0), iota((64, 256), 1)
+    upper = jnp.where(row < 32, even, 1 - even)
+    match = ((row & 15) == (col >> 4)) & ((col & 15) == ((row >> 4) & 1) + 14 * upper)
+    select = jnp.where(match, 1.0, 0.0).astype(BF16)
+    for x in range(0, size_x, 2):
+        if x % count == 0:
+            fetches[x // count].wait()
+        both = jnp.concatenate(
+            [feat[:, x].reshape(256, 128), feat[:, x + 1].reshape(256, 128)], axis=1
+        )
+        rows = dot(select, both).astype(BF16)
+        for h in range(2):
+            gy_a[x + h] = rows[0:32, 128 * h : 128 * h + 128]
+            gy_b[x + h] = rows[32:64, 128 * h : 128 * h + 128]
+
+
+def swap_rows(feat, planes):
     row, col = iota((256, 256), 0), iota((256, 256), 1)
     match = ((row >> 4) == (col & 15)) & ((row & 15) == (col >> 4))
     swap = jnp.where(match, 1.0, 0.0).astype(BF16)
-    even = is_even("gy")
-    rows_a = pl.multiple_of(even * 224, 32)
-    rows_b = pl.multiple_of((1 - even) * 224, 32)
-    for i in range(chunks):
-        copy(i).wait()
-        for x in range(0, count, 2):
-            both = jnp.concatenate(
-                [held[i, :, x].reshape(256, 128), held[i, :, x + 1].reshape(256, 128)], axis=1
-            )
-            moved = dot(swap, both).astype(BF16)
-            planes[i * count + x] = moved[:, :128]
-            planes[i * count + x + 1] = moved[:, 128:]
-    gy_a[...] = planes[:, pl.ds(rows_a, 32), :]
-    gy_b[...] = planes[:, pl.ds(rows_b, 32), :]
-
-
-def pack(features):
-    size_x = features.shape[1]
-    step = 8
-    return pl.pallas_call(
-        pack_kernel,
-        in_specs=[pl.BlockSpec(memory_space=pltpu.HBM)],
-        out_specs=[VMEM] * 3,
-        out_shape=[shape(size_x, 256, 128), shape(size_x, 32, 128), shape(size_x, 32, 128)],
-        scratch_shapes=[
-            pltpu.VMEM((size_x // step, 16, step, 16, 128), BF16),
-            pltpu.SemaphoreType.DMA((size_x // step,)),
-        ],
-        compiler_params=pltpu.CompilerParams(vmem_limit_bytes=LIMIT),
-        cost_estimate=pl.CostEstimate(
-            flops=2 * 256 * 256 * 128 * size_x, bytes_accessed=5 << 20, transcendentals=0
-        ),
-    )(features)
+    for x in range(0, feat.shape[1], 2):
+        both = jnp.concatenate(
+            [feat[:, x].reshape(256, 128), feat[:, x + 1].reshape(256, 128)], axis=1
+        )
+        moved = dot(swap, both).astype(BF16)
+        planes[x] = moved[:, :128]
+        planes[x + 1] = moved[:, 128:]
 
 
 def band(w, t_ref):
@@ -153,37 +166,55 @@
     return shifted_sum(acc, 64, 0), shifted_sum(acc, 64, 1)
 
 
-def interior_kernel(planes, w, f1, rims, faces, t1, t2):
+def plane_of(parts, x):
+    count = parts[0].shape[0]
+    return (parts[0], x) if x < count else (parts[1], x - count)
+
+
+def interior_kernel(far, w, low, high_far, rims, faces, t1, t2, planes, feat, high, sems, puts):
+    fetches, _ = fetch_planes(far, feat, sems)
     size_x = planes.shape[0]
+    band(w[0:432, :], t1)
+    band(w[432:864, :], t2)
+    for fetch in fetches:
+        fetch.wait()
+    swap_rows(feat, planes)
     rims[0] = planes[:, 0:32]
     rims[1] = planes[:, 224:256]
     faces[0] = planes[0:2]
     faces[1] = planes[size_x - 2 : size_x]
-    band(w[0:432, :], t1)
-    band(w[432:864, :], t2)
 
     def piece(at, j):
         return window(lambda x: planes[at + x, 32 * j : 32 * j + 64])
 
     def store(at, j, value):
         for x in range(2):
-            f1[at + x, 32 * j + 32 : 32 * j + 64] = value[32 * x : 32 * x + 32].astype(BF16)
-
-    def step(p, carry):
-        at = 4 * p
-        for j in range(7):
-            for h, value in enumerate(conv_pair(t1, piece(at, j), piece(at + 2, j))):
-                store(at + 2 * h, j, value)
-        return carry
-
-    lax.fori_loop(0, (size_x - 2) // 4, step, 0, unroll=7)
+            to, index = plane_of((low, high), at + x)
+            to[index, 32 * j : 32 * j + 32] = value[32 * x : 32 * x + 32].astype(BF16)
+
+    half = high.shape[0] // 2
+
+    def put(i):
+        span = pl.ds(i * half, half)
+        return pltpu.make_async_copy(high.at[span], high_far.at[span], puts.at[i])
+
     at = size_x - 4
     for pair in ((0, 1), (2, 3), (4, 5), (5, 6)):
         for j, value in zip(pair, conv_pair(t1, piece(at, pair[0]), piece(at, pair[1]))):
             store(at, j, value)
-
-
-def rim_kernel(inner, rims, faces, gy_a, gy_b, t1, f1, send_a, send_b, halo):
+    for at in range(size_x - 8, -1, -4):
+        for j in range(7):
+            for h, value in enumerate(conv_pair(t1, piece(at, j), piece(at + 2, j))):
+                store(at + 2 * h, j, value)
+        start = low.shape[0]
+        for i in (1, 0):
+            if at <= start + i * half < at + 4:
+                put(i).start()
+    for i in range(2):
+        put(i).wait()
+
+
+def rim_kernel(rims, faces, gy_a, gy_b, t1, rim_rows, send_a, send_b, halo):
     size_x = rims.shape[1]
     left, right = side_flags("gy")
     y_left, y_right = left[0] + left[1], right[0] + right[1]
@@ -202,39 +233,42 @@
             send[j, 32:288] = faces[side, j]
             send[j, 288:320] = halo[1, x]
 
-    def step(p, carry):
-        at = 2 * p
+    for at in range(0, size_x - 2, 2):
         low = window(lambda x: jnp.concatenate([halo[0, at + x], rims[0, at + x]], axis=0))
         high = window(lambda x: jnp.concatenate([rims[1, at + x], halo[1, at + x]], axis=0))
         low, high = conv_pair(t1, low, high)
         for x in range(2):
             cut = slice(32 * x, 32 * x + 16), slice(32 * x + 16, 32 * x + 32)
-            f1[at + x, 0:16] = (low[cut[0]] * y_left).astype(BF16)
-            f1[at + x, 16:32] = low[cut[1]].astype(BF16)
-            f1[at + x, 32:256] = inner[at + x, 32:256]
-            f1[at + x, 256:272] = high[cut[0]].astype(BF16)
-            f1[at + x, 272:288] = (high[cut[1]] * y_right).astype(BF16)
-        return carry
-
-    lax.fori_loop(0, (size_x - 2) // 2, step, 0, unroll=15)
+            rim_rows[at + x, 0:16] = (low[cut[0]] * y_left).astype(BF16)
+            rim_rows[at + x, 16:32] = low[cut[1]].astype(BF16)
+            rim_rows[at + x, 32:48] = high[cut[0]].astype(BF16)
+            rim_rows[at + x, 48:64] = (high[cut[1]] * y_right).astype(BF16)
 
 
 def fold_rows(value):
     return jnp.sum(value.astype(F32).reshape(4, 16, 128), axis=0)
 
 
-def middle_kernel(f1, t2, second, f1_ends, psum):
-    size_x = f1.shape[0] + 2
-    f1_ends[0:2] = f1[0:2]
-    f1_ends[2:4] = f1[size_x - 4 : size_x - 2]
-    psum[...] = jnp.zeros(psum.shape, F32)
-
-    def step(q, carry):
-        at = 2 * q - 2
-        summed = jnp.zeros((16, 128), F32)
+def middle_kernel(low, high_far, rim_rows, t2, second, f1_ends, psum, high, sem):
+    fetch = pltpu.make_async_copy(high_far, high, sem)
+    fetch.start()
+    size_x = low.shape[0] + high.shape[0] + 2
+
+    def rows(x, j):
+        inner, at = plane_of((low, high), x)
+        if j == 0:
+            return jnp.concatenate([rim_rows[x, 0:32], inner[at, 0:32]], axis=0)
+        if j == 7:
+            return jnp.concatenate([inner[at, 192:224], rim_rows[x, 32:64]], axis=0)
+        return inner[at, 32 * j - 32 : 32 * j + 32]
+
+    sums = [jnp.zeros((16, 128), F32) for _ in range(2)]
+    for at in range(0, size_x - 4, 2):
+        if at + 2 == low.shape[0]:
+            fetch.wait()
 
         def piece(j):
-            return window(lambda x: f1[at + x, 32 * j : 32 * j + 64])
+            return window(lambda x: rows(at + x, j))
 
         for j in range(0, 8, 2):
             for h, value in enumerate(conv_pair(t2, piece(j), piece(j + 1))):
@@ -242,23 +276,19 @@
                 row = 32 * (j + h)
                 for x in range(2):
                     second[at + x, row : row + 32] = value[32 * x : 32 * x + 32]
-                summed = summed + fold_rows(value)
-        psum[q // (POOL // 2)] += summed
-        return carry
-
-    lax.fori_loop(1, size_x // 2 - 1, step, 0, unroll=14)
+                sums[(at + 2) // POOL] += fold_rows(value)
+    psum[0], psum[1] = sums
+    for i, x in enumerate((0, 1, size_x - 4, size_x - 3)):
+        inner, at = plane_of((low, high), x)
+        f1_ends[i, 0:32] = rim_rows[x, 0:32]
+        f1_ends[i, 32:256] = inner[at]
+        f1_ends[i, 256:288] = rim_rows[x, 32:64]
 
 
 def edge_kernel(
-    inner, f1_ends, send_a, send_b, far_a, far_b, psum_in, t1, t2, left_out, right_out,
-    pooled, fe, fx, got_a, got_b, sems,
+    inner, f1_ends, send_a, send_b, got_a, got_b, psum_in, t1, t2, left_out, right_out,
+    pooled, fe, fx,
 ):
-    fetches = [
-        pltpu.make_async_copy(far_a, got_a, sems.at[0]),
-        pltpu.make_async_copy(far_b, got_b, sems.at[1]),
-    ]
-    for fetch in fetches:
-        fetch.start()
     half = left_out.shape[0]
     size_x = 2 * half
     moved = iter(range(size_x - 4))
@@ -278,8 +308,6 @@
     y_left, y_right = side_flags("gy")
     y_left, y_right = y_left[0] + y_left[1], y_right[0] + y_right[1]
     even = is_even("gx").astype(F32)
-    for fetch in fetches:
-        fetch.wait()
     for j in range(2):
         fe[0, j] = mix(got_a[j], got_b[j], x_left)
         fe[0, 2 + j] = mix(send_a[j], send_b[j], (1.0 - even, even))
@@ -338,28 +366,30 @@
     v = v - a.astype(F32)
     b = v.astype(BF16)
     c = (v - b.astype(F32)).astype(BF16)
-    return a, b, c
+    return [a, b, c]
 
 
 def swap_groups(rows):
-    lane = iota((256, 128), 1)
-    major, minor = iota((256, 128), 0) >> 4, iota((256, 128), 0) & 15
-    spread = jnp.broadcast_to(rows[:, None, :], (16, 16, 128)).reshape(256, 128)
-    spread = jnp.where((lane >> 3) == minor, spread, 0.0)
-    l0, l1 = iota((128, 128), 0), iota((128, 128), 1)
-    fold = jnp.where((l0 & 7) == (l1 & 7), 1.0, 0.0).astype(BF16)
-    out = []
-    for piece in split3(spread):
-        moved = jnp.where((lane >> 3) == major, dot(piece, fold), 0.0)
-        out.append(jnp.sum(moved.reshape(16, 16, 128), axis=0))
-    return out
+    lane = iota((16, 128), 1) >> 3
+    total = jnp.zeros((16, 128), F32)
+    rows = pltpu.roll(pltpu.roll(rows, 0, 1, stride=8, stride_axis=0), 8, 1)
+    for s in range(16):
+        spread = jnp.broadcast_to(rows[s : s + 1, :], (16, 128))
+        moved = pltpu.roll(spread, 0, 1, stride=8, stride_axis=0)
+        total = jnp.where(lane == s, moved, total)
+    return total
+
+
+def load_kernel(far, after, out, sem):
+    fetch = pltpu.make_async_copy(far, out, sem)
+    fetch.start()
+    fetch.wait()
 
 
 def lift_slabs(slabs, w_lift):
     columns = []
     for slab in slabs:
-        pieces = [v.astype(BF16) for v in swap_groups(slab)]
-        columns.append(jnp.concatenate(pieces, axis=0))
+        columns.append(jnp.concatenate(split3(swap_groups(slab)), axis=0))
     stacked = jnp.concatenate(columns, axis=1)
     lift3 = jnp.concatenate([w_lift] * 3, axis=1)
     return jnp.maximum(dot(lift3, stacked), 0.0).astype(BF16)
@@ -409,8 +439,9 @@
         rows = w_coarse[9 * a * count : 9 * (a + 1) * count, :]
         total = mine[x] + taps(dot(rows, lifted[:, x * 128 : x * 128 + 128]), count)
         coarse = jnp.maximum(total, 0.0).astype(BF16)
-        pieces = swap_groups(dot(w_dec[...], coarse))
-        out[:, x, :] = pieces[0] + pieces[1] + pieces[2]
+        rows = swap_groups(dot(w_dec[...], coarse))
+        for y in range(16):
+            out[y, x : x + 1, :] = rows[15 - y : 16 - y, :]
 
 
 def skip_planes(matrix, second, at):
@@ -498,29 +529,47 @@
     def swap(count, odd):
         return [(i, (((i + odd) ^ 1) - odd) % count) for i in range(count)]
 
-    planes, gy_a, gy_b = pack(pltpu.with_memory_space_constraint(features, pltpu.HBM))
+    gy_a, gy_b = vmem_call(
+        rows_kernel,
+        [shape(size_x, 32, 128), shape(size_x, 32, 128)],
+        (features,),
+        scratch=[pltpu.VMEM(features.shape, BF16), pltpu.SemaphoreType.DMA((1,))],
+        far=(0,),
+        flops=2 * 64 * 256 * 128 * size_x,
+        nbytes=3 << 20,
+    )
     gy_a = lax.ppermute(gy_a, "gy", swap(ny, 0))
     gy_b = lax.ppermute(gy_b, "gy", swap(ny, 1))
 
     w_fine = jnp.concatenate([w_first, w_second], axis=0).reshape(864, 16)
-    first = shape(size_x - 2, 288, 128)
-    f1, rims, faces, t1, t2 = vmem_call(
+    near, rest = size_x // 2 - 2, size_x // 2
+    low, high, rims, faces, t1, t2 = vmem_call(
         interior_kernel,
         [
-            first,
+            shape(near, 224, 128),
+            shape(rest, 224, 128),
             shape(2, size_x, 32, 128),
             shape(2, 2, 256, 128),
             shape(192, 256),
             shape(192, 256),
         ],
-        (planes, w_fine),
-        flops=2 * 192 * 256 * 256 * 53,
+        (features, w_fine),
+        scratch=[
+            pltpu.VMEM((size_x, 256, 128), BF16),
+            pltpu.VMEM(features.shape, BF16),
+            pltpu.VMEM((rest, 224, 128), BF16),
+            pltpu.SemaphoreType.DMA((1,)),
+            pltpu.SemaphoreType.DMA((2,)),
+        ],
+        far=(0,),
+        far_out=(1,),
+        flops=2 * 192 * 256 * 256 * 70,
         nbytes=4 << 20,
     )
-    f1, send_a, send_b = vmem_call(
+    rim_rows, send_a, send_b = vmem_call(
         rim_kernel,
-        [first, shape(2, 320, 128), shape(2, 320, 128)],
-        (f1, rims, faces, gy_a, gy_b, t1),
+        [shape(size_x - 2, 64, 128), shape(2, 320, 128), shape(2, 320, 128)],
+        (rims, faces, gy_a, gy_b, t1),
         scratch=[pltpu.VMEM((2, size_x, 32, 128), BF16)],
         flops=2 * 192 * 256 * 256 * 15,
         nbytes=1 << 20,
@@ -530,7 +579,9 @@
     second, f1_ends, psum = vmem_call(
         middle_kernel,
         [shape(size_x - 4, 256, 128), shape(4, 288, 128), shape(2, 16, 128, dtype=F32)],
-        (f1, t2),
+        (low, high, rim_rows, t2),
+        scratch=[pltpu.VMEM((rest, 224, 128), BF16), pltpu.SemaphoreType.DMA],
+        far=(1,),
         flops=2 * 192 * 256 * 256 * 56,
         nbytes=6 << 20,
     )
@@ -542,11 +593,7 @@
         scratch=[
             pltpu.VMEM((2, 4, 320, 128), BF16),
             pltpu.VMEM((2, 2, 288, 128), BF16),
-            pltpu.VMEM((2, 320, 128), BF16),
-            pltpu.VMEM((2, 320, 128), BF16),
-            pltpu.SemaphoreType.DMA((2,)),
         ],
-        far=(4, 5),
         flops=2 * 192 * 256 * 256 * 17,
         nbytes=1 << 20,
     )
@@ -554,7 +601,17 @@
     count = w_coarse.shape[0]
     w_rows = jnp.transpose(w_coarse, (1, 0, 2)).reshape(27 * count, w_coarse.shape[2])
     w_dec = lax.dynamic_slice_in_dim(w_decode, gy * count, count, axis=1)
+    w_lift = jnp.flip(w_lift, axis=1)
     own = lax.all_to_all(pooled, "gy", 0, 0)
+    w_rows = vmem_call(
+        load_kernel,
+        shape(*w_rows.shape),
+        (w_rows, pooled),
+        scratch=[pltpu.SemaphoreType.DMA],
+        far=(0,),
+        flops=1 << 28,
+        nbytes=4 << 20,
+    )
     gl = lax.ppermute(own[:, 1, :], "gx", ring(nx, 1))
     gr = lax.ppermute(own[:, 0, :], "gx", ring(nx, -1))
     mine = vmem_call(
@@ -574,7 +631,7 @@
     parts = lax.all_to_all(parts, "gy", 0, 0)
     matrix, up, ahead = vmem_call(
         skip_kernel,
-        [shape(256, 256), shape(256, 16), shape(8, 256, 128, dtype=F32)],
+        [shape(256, 256), shape(256, 16), shape(4, 256, 128, dtype=F32)],
         (seconds[0], w_joining),
         flops=2 * 256 * 256 * 128 * 8,
         nbytes=2 << 20,

time: 63.9 us -> 61.1 us (0.956)
  waiting for transfers between devices: 18.1 us -> 12.6 us
  Pallas kernels: 17.3 us -> 20 us
    pallas_call x7 -> x9, Pallas kernels: 12.5 us -> 18.3 us  [vmem_call(): pl.pallas_call(kernel, out_shape=out_shape, in_specs=[pl.BlockSpec(memory...]
    pallas_call x1 -> x0, Pallas kernels: 3.07 us -> none  [pack(): pl.pallas_call(pack_kernel, in_specs=[pl.BlockSpec(memory_space=pltpu.HBM...]
    ppermute x1, waiting for transfers between devices: 3.82 us -> 0.97 us  [local(): gy_b = lax.ppermute(gy_b, 'gy', swap(ny, 1))]
    all_to_all x1, waiting for transfers between devices: 5.58 us -> 3.86 us  [local(): own = lax.all_to_all(pooled, 'gy', 0, 0)]
    ppermute x1, waiting for transfers between devices: 3.16 us -> 2.34 us  [local(): got_b = lax.ppermute(send_b, 'gx', swap(nx, 1))]
    unnamed x17 -> x11, local copies, waits for them, and re-layouts: 0.82 us -> 0.14 us
  transfers between devices with their start and end apart: 8 -> 8, of which waited for: 6 -> 4; matrix products, arithmetic and copies ran while one was open for 1% -> 2% of each run, Pallas kernels for 10% -> 19%
where the time goes in v2:
time: 61.1 us; the launch traced here: 60.7 us
  starting transfers between devices  27 us (44%)
  Pallas kernels  20 us (33%)
  waiting for transfers between devices  12.6 us (21%)
  local copies, waits for them, and re-layouts  0.89 us (1%)
    pallas_call x9, Pallas kernels, vmem_call(): pl.pallas_call(kernel, out_shape=out_shape, in_specs=[pl.BlockSpec(memory...  18.3 us
    all_to_all x1, starting transfers between devices, local(): own = lax.all_to_all(pooled, 'gy', 0, 0)  8.55 us
    all_to_all x1, waiting for transfers between devices, local(): parts = lax.all_to_all(parts, 'gy', 0, 0)  5.38 us
    all_to_all x1, starting transfers between devices, local(): parts = lax.all_to_all(parts, 'gy', 0, 0)  4.91 us
    all_to_all x1, waiting for transfers between devices, local(): own = lax.all_to_all(pooled, 'gy', 0, 0)  3.86 us
    ppermute x1, starting transfers between devices, local(): got_a = lax.ppermute(send_a, 'gx', swap(nx, 0))  3.24 us
    ppermute x1, starting transfers between devices, local(): gr = lax.ppermute(own[:, 0, :], 'gx', ring(nx, -1))  3.19 us
    ppermute x1, waiting for transfers between devices, local(): got_b = lax.ppermute(send_b, 'gx', swap(nx, 1))  2.34 us
  transfers between devices with their start and end apart: 8, of which 4 were waited for; matrix products, arithmetic and copies ran while one was open for 2% of the time, Pallas kernels for 19%

profile of v2, /device:TPU:1, one launch (start us, length us, event | category | flops | bytes accessed | tf_op | source)
XLA Modules:
  0.0 60.7 jit_solution(11902300269583205838)
XLA Ops:
  0.0 0.0 copy-start
  0.0 0.0 copy-start.3
  0.0 0.0 copy-start.2
  0.0 2.1 %shard_map.74 = (bf16[32,32,128]{2,1,0:T(8,128)(2,1)S(1)}, bf16[32,32,128]{2,1,0:T(8,128)(2,1)S(1)}) custom-call(bf16[16,32,16,128]{3,2,1,0:T(8,128)(2,1)} %far.3), custom_call_target="tpu_custom_call" | custom-call | flops 134217728 | bytes 3145728 | tf_op jit(solution)/shard_map/pallas_call | solution.py:38
  2.1 1.5 %collective-permute-start = (bf16[32,32,128]{2,1,0:T(8,128)(2,1)S(1)}, bf16[32,32,128]{2,1,0:T(8,128)(2,1)S(1)}, u32[]{:S(2)}, u32[]{:S(2)}) collective-permute-start(bf16[32,32,128]{2,1,0:T(8,128)(2,1)S(1)} %get-tuple-element.29), channel_id=1, source_target_pairs={{0,1},{1,0},{2,3},{3,2},{4,5},{5,4},{6,7},{7,6},{8,9},{9,8},{10,11... | collective-permute-start | bytes 786440 | tf_op jit(solution)/shard_map/ppermute | solution.py:541
  3.6 1.4 %collective-permute-start.1 = (bf16[32,32,128]{2,1,0:T(8,128)(2,1)S(1)}, bf16[32,32,128]{2,1,0:T(8,128)(2,1)S(1)}, u32[]{:S(2)}, u32[]{:S(2)}) collective-permute-start(bf16[32,32,128]{2,1,0:T(8,128)(2,1)S(1)} %get-tuple-element.30), channel_id=1, source_target_pairs={{0,15},{1,2},{2,1},{3,4},{4,3},{5,6},{6,5},{7,8},{8,7},{9,10},{10,... | collective-permute-start | bytes 786440 | tf_op jit(solution)/shard_map/ppermute | solution.py:542
  5.0 0.0 copy-done.3
  5.0 0.0 copy-done.2
  5.0 0.1 pad_maximum_fusion
  5.1 0.3 copy.12
  5.3 0.0 copy-start.4
  5.4 5.3 %shard_map.73 = (bf16[14,224,128]{2,1,0:T(8,128)(2,1)S(1)}, bf16[16,224,128]{2,1,0:T(8,128)(2,1)}, bf16[2,32,32,128]{3,2,1,0:T(8,128)(2,1)S(1)}, bf16[2,2,256,12...) custom-call(bf16[16,32,16,128]{3,2,1,0:T(8,128)(2,1)} %far.3, ...), custom_call_target="tpu_custom_call" | custom-call | flops 1761607680 | bytes 4194304 | tf_op jit(solution)/shard_map/pallas_call | solution.py:38
  10.6 0.0 collective-permute-done.gy_a
  10.6 1.0 %collective-permute-done.1.gy_b = bf16[32,32,128]{2,1,0:T(8,128)(2,1)S(1)} collective-permute-done((bf16[32,32,128]{2,1,0:T(8,128)(2,1)S(1)}, bf16[32,32,128]{2,1,0:T(8,128)(2,1)S(1)}, u32[]{:S(2)}, u32[]{:S(2)}) %collective-permute-start.1) | collective-permute-done | bytes 262176 | tf_op jit(solution)/shard_map/ppermute | solution.py:542
  11.6 1.0 %shard_map.75 = (bf16[30,64,128]{2,1,0:T(8,128)(2,1)S(1)}, bf16[2,320,128]{2,1,0:T(8,128)(2,1)S(1)}, bf16[2,320,128]{2,1,0:T(8,128)(2,1)S(1)}) custom-call(bf16[2,32,32,128]{3,2,1,0:T(8,128)(2,1)S(1)} %get-tuple-element.27.rims, bf16[2,2,256,128]{3,2,1,0:T(8,128)(2,1)S(1)} %get-tuple-element.28.faces, bf16[32,32,128]{2,1,0:T(8,128)(2,1)S(1)} %collective-permute-done.gy_a, ...), custom_call_target="tpu_custom_call" | custom-call | flops 377487360 | bytes 1048576 | tf_op jit(solution)/shard_map/pallas_call | solution.py:38
  12.6 3.2 %collective-permute-start.2 = (bf16[2,320,128]{2,1,0:T(8,128)(2,1)S(1)}, bf16[2,320,128]{2,1,0:T(8,128)(2,1)S(1)}, u32[]{:S(2)}, u32[]{:S(2)}) collective-permute-start(bf16[2,320,128]{2,1,0:T(8,128)(2,1)S(1)} %get-tuple-element.36.send_a), channel_id=1, source_target_pairs={{0,16},{16,0},{32,48},{48,32},{64,80},{80,64},{96,112},{112,96},{1... | collective-permute-start | bytes 491528 | tf_op jit(solution)/shard_map/ppermute | solution.py:577
  15.8 2.3 %collective-permute-start.3 = (bf16[2,320,128]{2,1,0:T(8,128)(2,1)S(1)}, bf16[2,320,128]{2,1,0:T(8,128)(2,1)S(1)}, u32[]{:S(2)}, u32[]{:S(2)}) collective-permute-start(bf16[2,320,128]{2,1,0:T(8,128)(2,1)S(1)} %get-tuple-element.37.send_b), channel_id=1, source_target_pairs={{0,112},{16,32},{32,16},{48,64},{64,48},{80,96},{96,80},{112,0},{1... | collective-permute-start | bytes 491528 | tf_op jit(solution)/shard_map/ppermute | solution.py:578
  18.1 0.0 copy-done
  18.1 0.1 constant_dynamic-slice_fusion.w_dec
  18.2 0.0 copy-done.4
  18.2 0.1 copy.13
  18.3 0.4 rev.4.w_lift
  18.7 2.6 %shard_map.76 = (bf16[28,256,128]{2,1,0:T(8,128)(2,1)S(1)}, bf16[4,288,128]{2,1,0:T(8,128)(2,1)S(1)}, f32[2,16,128]{2,1,0:T(8,128)S(1)}) custom-call(bf16[14,224,128]{2,1,0:T(8,128)(2,1)S(1)} %get-tuple-element.25.low, bf16[16,224,128]{2,1,0:T(8,128)(2,1)} %get-tuple-element.26.high_far, bf16[30,64,128]{2,1,0:T(8,128)(2,1)S(1)} %get-tuple-element.32.rim_rows, ...), custom_call_target="tpu_custom_call" | custom-call | flops 1409286144 | bytes 6291456 | tf_op jit(solution)/shard_map/pallas_call | solution.py:38
  21.4 0.0 collective-permute-done.2.got_a
  21.4 2.3 %collective-permute-done.3.got_b = bf16[2,320,128]{2,1,0:T(8,128)(2,1)S(1)} collective-permute-done((bf16[2,320,128]{2,1,0:T(8,128)(2,1)S(1)}, bf16[2,320,128]{2,1,0:T(8,128)(2,1)S(1)}, u32[]{:S(2)}, u32[]{:S(2)}) %collective-permute-start.3) | collective-permute-done | bytes 163872 | tf_op jit(solution)/shard_map/ppermute | solution.py:578
  23.7 1.9 %shard_map.77 = (bf16[16,256,128]{2,1,0:T(8,128)(2,1)S(1)}, bf16[16,256,128]{2,1,0:T(8,128)(2,1)S(1)}, f32[16,2,128]{2,1,0:T(2,128)}) custom-call(bf16[28,256,128]{2,1,0:T(8,128)(2,1)S(1)} %get-tuple-element.34.inner, bf16[4,288,128]{2,1,0:T(8,128)(2,1)S(1)} %get-tuple-element.35.f1_ends, bf16[2,320,128]{2,1,0:T(8,128)(2,1)S(1)} %get-tuple-element.36.send_a, ...), custom_call_target="tpu_custom_call" | custom-call | flops 427819008 | bytes 1048576 | tf_op jit(solution)/shard_map/pallas_call | solution.py:38
  25.6 8.5 %all-to-all-start = ((f32[16,2,128]{2,1,0:T(2,128)}), f32[16,2,128]{2,1,0:T(2,128)S(1)}, u32[]{:S(2)}, u32[]{:S(2)}) async-start(f32[16,2,128]{2,1,0:T(2,128)} %get-tuple-element.44.after), calls=%async_computation | async-start | bytes 32768 | tf_op jit(solution)/shard_map/all_to_all | solution.py:605
  34.1 0.0 copy-start.1
  34.1 1.9 %shard_map.79.w_coarse = bf16[864,512]{1,0:T(8,128)(2,1)S(1)} custom-call(bf16[864,512]{1,0:T(8,128)(2,1)} %bitcast.11, f32[16,2,128]{2,1,0:T(2,128)} %get-tuple-element.44.after), custom_call_target="tpu_custom_call" | custom-call | flops 268435456 | bytes 4194304 | tf_op jit(solution)/shard_map/pallas_call | solution.py:38
  36.0 3.9 %all-to-all-done.own = f32[16,2,128]{2,1,0:T(2,128)S(1)} async-done(((f32[16,2,128]{2,1,0:T(2,128)}), f32[16,2,128]{2,1,0:T(2,128)S(1)}, u32[]{:S(2)}, u32[]{:S(2)}) %all-to-all-start) | async-done | bytes 16416 | tf_op jit(solution)/shard_map/all_to_all | solution.py:605
  39.9 2.0 %collective-permute-start.4 = (f32[16,128]{1,0:T(8,128)S(1)}, f32[16,128]{1,0:T(8,128)S(1)}, u32[]{:S(2)}, u32[]{:S(2)}) collective-permute-start(f32[16,128]{1,0:T(8,128)S(1)} %bitcast.13), channel_id=1, source_target_pairs={{0,16},{16,32},{32,48},{48,64},{64,80},{80,96},{96,112},{112,0},{1... | collective-permute-start | bytes 24584 | tf_op jit(solution)/shard_map/ppermute | solution.py:615
  41.9 3.2 %collective-permute-start.5 = (f32[16,128]{1,0:T(8,128)S(1)}, f32[16,128]{1,0:T(8,128)S(1)}, u32[]{:S(2)}, u32[]{:S(2)}) collective-permute-start(f32[16,128]{1,0:T(8,128)S(1)} %bitcast.12), channel_id=1, source_target_pairs={{0,112},{16,0},{32,16},{48,32},{64,48},{80,64},{96,80},{112,96},{1... | collective-permute-start | bytes 24584 | tf_op jit(solution)/shard_map/ppermute | solution.py:616
  45.1 1.0 %shard_map.80.mine = f32[2,32,128]{2,1,0:T(8,128)S(1)} custom-call(f32[16,2,128]{2,1,0:T(2,128)S(1)} %all-to-all-done.own, bf16[512,16]{1,0:T(8,128)(2,1)S(1)} %rev.4.w_lift, bf16[864,512]{1,0:T(8,128)(2,1)S(1)} %shard_map.79.w_coarse), custom_call_target="tpu_custom_call" | custom-call | flops 452984832 | bytes 2097152 | tf_op jit(solution)/shard_map/pallas_call | solution.py:38
  46.0 0.0 collective-permute-done.4.gl
  46.1 0.0 collective-permute-done.5.gr
  46.1 2.1 %shard_map.81 = f32[16,2,128]{2,1,0:T(2,128)} custom-call(f32[2,32,128]{2,1,0:T(8,128)S(1)} %shard_map.80.mine, f32[16,128]{1,0:T(8,128)S(1)} %collective-permute-done.4.gl, f32[16,128]{1,0:T(8,128)S(1)} %collective-permute-done.5.gr, bf16[512,16]{1,0:T(8,128)(2,1)S(1)} %rev.4.w_lift, bf16[864,512]{1,0:T(8,128)(2,1)S(1)} %shard_map.79.w_coarse, ...), custom_call_target="tpu_custom_call" | custom-call | flops 226492416 | bytes 2097152 | tf_op jit(solution)/shard_map/pallas_call | solution.py:38
  48.2 4.9 %all-to-all-start.1 = ((f32[16,2,128]{2,1,0:T(2,128)}), f32[16,2,128]{2,1,0:T(2,128)S(1)}, u32[]{:S(2)}, u32[]{:S(2)}) async-start(f32[16,2,128]{2,1,0:T(2,128)} %shard_map.81), calls=%async_computation.1 | async-start | bytes 32768 | tf_op jit(solution)/shard_map/all_to_all | solution.py:631
  53.1 0.0 copy-done.1
  53.2 0.5 shard_map.78
  53.6 5.4 %all-to-all-done.1.parts = f32[16,2,128]{2,1,0:T(2,128)S(1)} async-done(((f32[16,2,128]{2,1,0:T(2,128)}), f32[16,2,128]{2,1,0:T(2,128)S(1)}, u32[]{:S(2)}, u32[]{:S(2)}) %all-to-all-start.1) | async-done | bytes 16416 | tf_op jit(solution)/shard_map/all_to_all | solution.py:631
  59.0 1.7 %shard_map.82 = bf16[16,32,16,128]{3,2,1,0:T(8,128)(2,1)} custom-call(bf16[16,256,128]{2,1,0:T(8,128)(2,1)S(1)} %get-tuple-element.39.second.left, bf16[16,256,128]{2,1,0:T(8,128)(2,1)S(1)} %get-tuple-element.40.right, f32[4,256,128]{2,1,0:T(8,128)S(1)} %get-tuple-element.41.ahead, bf16[256,256]{1,0:T(8,128)(2,1)S(1)} %get-tuple-element.42.matrix, ...), custom_call_target="tpu_custom_call" | custom-call | flops 536870912 | bytes 4194304 | tf_op jit(solution)/shard_map/pallas_call | solution.py:505
  (1 shorter events, 0.0 us)
Async XLA Ops:
  0.0 18.1 %copy-start = (bf16[16,512]{1,0:T(8,128)(2,1)S(1)}, bf16[16,512]{1,0:T(8,128)(2,1)}, u32[]{:S(2)}) copy-start(bf16[16,512]{1,0:T(8,128)(2,1)} %param.12) | copy-start | bytes 49156
  0.0 5.0 %copy-start.3 = (bf16[27,16,16]{0,2,1:T(8,128)(2,1)S(1)}, bf16[27,16,16]{0,2,1:T(8,128)(2,1)}, u32[]{:S(2)}) copy-start(bf16[27,16,16]{0,2,1:T(8,128)(2,1)} %param.8) | copy-start | bytes 41476
  0.0 5.0 %copy-start.2 = (bf16[27,16,16]{0,2,1:T(8,128)(2,1)S(1)}, bf16[27,16,16]{0,2,1:T(8,128)(2,1)}, u32[]{:S(2)}) copy-start(bf16[27,16,16]{0,2,1:T(8,128)(2,1)} %param.9) | copy-start | bytes 41476
  2.1 8.5 %collective-permute-start = (bf16[32,32,128]{2,1,0:T(8,128)(2,1)S(1)}, bf16[32,32,128]{2,1,0:T(8,128)(2,1)S(1)}, u32[]{:S(2)}, u32[]{:S(2)}) collective-permute-start(bf16[32,32,128]{2,1,0:T(8,128)(2,1)S(1)} %get-tuple-element.29), channel_id=1, source_target_pairs={{0,1},{1,0},{2,3},{3,2},{4,5},{5,4},{6,7},{7,6},{8,9},{9,8},{10,11... | collective-permute-start | bytes 786440 | tf_op jit(solution)/shard_map/ppermute | solution.py:541
  3.6 8.0 %collective-permute-start.1 = (bf16[32,32,128]{2,1,0:T(8,128)(2,1)S(1)}, bf16[32,32,128]{2,1,0:T(8,128)(2,1)S(1)}, u32[]{:S(2)}, u32[]{:S(2)}) collective-permute-start(bf16[32,32,128]{2,1,0:T(8,128)(2,1)S(1)} %get-tuple-element.30), channel_id=1, source_target_pairs={{0,15},{1,2},{2,1},{3,4},{4,3},{5,6},{6,5},{7,8},{8,7},{9,10},{10,... | collective-permute-start | bytes 786440 | tf_op jit(solution)/shard_map/ppermute | solution.py:542
  5.3 12.8 %copy-start.4 = (bf16[512,16]{0,1:T(8,128)(2,1)S(1)}, bf16[512,16]{0,1:T(8,128)(2,1)}, u32[]{:S(2)}) copy-start(bf16[512,16]{0,1:T(8,128)(2,1)} %param.10) | copy-start | bytes 49156
  12.6 8.8 %collective-permute-start.2 = (bf16[2,320,128]{2,1,0:T(8,128)(2,1)S(1)}, bf16[2,320,128]{2,1,0:T(8,128)(2,1)S(1)}, u32[]{:S(2)}, u32[]{:S(2)}) collective-permute-start(bf16[2,320,128]{2,1,0:T(8,128)(2,1)S(1)} %get-tuple-element.36.send_a), channel_id=1, source_target_pairs={{0,16},{16,0},{32,48},{48,32},{64,80},{80,64},{96,112},{112,96},{1... | collective-permute-start | bytes 491528 | tf_op jit(solution)/shard_map/ppermute | solution.py:577
  15.8 7.9 %collective-permute-start.3 = (bf16[2,320,128]{2,1,0:T(8,128)(2,1)S(1)}, bf16[2,320,128]{2,1,0:T(8,128)(2,1)S(1)}, u32[]{:S(2)}, u32[]{:S(2)}) collective-permute-start(bf16[2,320,128]{2,1,0:T(8,128)(2,1)S(1)} %get-tuple-element.37.send_b), channel_id=1, source_target_pairs={{0,112},{16,32},{32,16},{48,64},{64,48},{80,96},{96,80},{112,0},{1... | collective-permute-start | bytes 491528 | tf_op jit(solution)/shard_map/ppermute | solution.py:578
  25.6 14.3 %all-to-all-start = ((f32[16,2,128]{2,1,0:T(2,128)}), f32[16,2,128]{2,1,0:T(2,128)S(1)}, u32[]{:S(2)}, u32[]{:S(2)}) async-start(f32[16,2,128]{2,1,0:T(2,128)} %get-tuple-element.44.after), calls=%async_computation | async-start | bytes 32768 | tf_op jit(solution)/shard_map/all_to_all | solution.py:605
  34.1 19.0 %copy-start.1 = (bf16[16,32]{1,0:T(8,128)(2,1)S(1)}, bf16[16,32]{1,0:T(8,128)(2,1)}, u32[]{:S(2)}) copy-start(bf16[16,32]{1,0:T(8,128)(2,1)} %w_join.1) | copy-start | bytes 3076
  39.9 6.2 %collective-permute-start.4 = (f32[16,128]{1,0:T(8,128)S(1)}, f32[16,128]{1,0:T(8,128)S(1)}, u32[]{:S(2)}, u32[]{:S(2)}) collective-permute-start(f32[16,128]{1,0:T(8,128)S(1)} %bitcast.13), channel_id=1, source_target_pairs={{0,16},{16,32},{32,48},{48,64},{64,80},{80,96},{96,112},{112,0},{1... | collective-permute-start | bytes 24584 | tf_op jit(solution)/shard_map/ppermute | solution.py:615
  41.9 4.2 %collective-permute-start.5 = (f32[16,128]{1,0:T(8,128)S(1)}, f32[16,128]{1,0:T(8,128)S(1)}, u32[]{:S(2)}, u32[]{:S(2)}) collective-permute-start(f32[16,128]{1,0:T(8,128)S(1)} %bitcast.12), channel_id=1, source_target_pairs={{0,112},{16,0},{32,16},{48,32},{64,48},{80,64},{96,80},{112,96},{1... | collective-permute-start | bytes 24584 | tf_op jit(solution)/shard_map/ppermute | solution.py:616
  48.2 10.8 %all-to-all-start.1 = ((f32[16,2,128]{2,1,0:T(2,128)}), f32[16,2,128]{2,1,0:T(2,128)S(1)}, u32[]{:S(2)}, u32[]{:S(2)}) async-start(f32[16,2,128]{2,1,0:T(2,128)} %shard_map.81), calls=%async_computation.1 | async-start | bytes 32768 | tf_op jit(solution)/shard_map/all_to_all | solution.py:631

commit v3 on v2

--- a/solution.py
+++ b/solution.py
@@ -214,25 +214,25 @@
         put(i).wait()
 
 
-def rim_kernel(rims, faces, gy_a, gy_b, t1, rim_rows, send_a, send_b, halo):
+def face_kernel(faces, gy_a, gy_b, send_a, send_b):
+    last = gy_a.shape[0] - 2
+    left, right = side_flags("gy")
+    even = is_even("gx")
+    for send, side in ((send_a, even), (send_b, 1 - even)):
+        for j in range(2):
+            x = side * last + j
+            send[j, 0:32] = mix(gy_a[x], gy_b[x], left)
+            send[j, 32:288] = faces[side, j]
+            send[j, 288:320] = mix(gy_a[x], gy_b[x], right)
+
+
+def rim_rows_of(rims, gy_a, gy_b, t1, rim_rows, halo):
     size_x = rims.shape[1]
     left, right = side_flags("gy")
     y_left, y_right = left[0] + left[1], right[0] + right[1]
-
-    def fill(x, carry):
+    for x in range(size_x):
         halo[0, x] = mix(gy_a[x], gy_b[x], left)
         halo[1, x] = mix(gy_a[x], gy_b[x], right)
-        return carry
-
-    lax.fori_loop(0, size_x, fill, 0, unroll=4)
-    even = is_even("gx")
-    for send, side in ((send_a, even), (send_b, 1 - even)):
-        for j in range(2):
-            x = side * (size_x - 2) + j
-            send[j, 0:32] = halo[0, x]
-            send[j, 32:288] = faces[side, j]
-            send[j, 288:320] = halo[1, x]
-
     for at in range(0, size_x - 2, 2):
         low = window(lambda x: jnp.concatenate([halo[0, at + x], rims[0, at + x]], axis=0))
         high = window(lambda x: jnp.concatenate([rims[1, at + x], halo[1, at + x]], axis=0))
@@ -249,9 +249,12 @@
     return jnp.sum(value.astype(F32).reshape(4, 16, 128), axis=0)
 
 
-def middle_kernel(low, high_far, rim_rows, t2, second, f1_ends, psum, high, sem):
+def middle_kernel(
+    low, high_far, rims, gy_a, gy_b, t1, t2, second, f1_ends, psum, high, rim_rows, halo, sem
+):
     fetch = pltpu.make_async_copy(high_far, high, sem)
     fetch.start()
+    rim_rows_of(rims, gy_a, gy_b, t1, rim_rows, halo)
     size_x = low.shape[0] + high.shape[0] + 2
 
     def rows(x, j):
@@ -566,23 +569,26 @@
         flops=2 * 192 * 256 * 256 * 70,
         nbytes=4 << 20,
     )
-    rim_rows, send_a, send_b = vmem_call(
-        rim_kernel,
-        [shape(size_x - 2, 64, 128), shape(2, 320, 128), shape(2, 320, 128)],
-        (rims, faces, gy_a, gy_b, t1),
-        scratch=[pltpu.VMEM((2, size_x, 32, 128), BF16)],
-        flops=2 * 192 * 256 * 256 * 15,
-        nbytes=1 << 20,
+    send_a, send_b = vmem_call(
+        face_kernel,
+        [shape(2, 320, 128), shape(2, 320, 128)],
+        (faces, gy_a, gy_b),
+        nbytes=1 << 19,
     )
     got_a = lax.ppermute(send_a, "gx", swap(nx, 0))
     got_b = lax.ppermute(send_b, "gx", swap(nx, 1))
     second, f1_ends, psum = vmem_call(
         middle_kernel,
         [shape(size_x - 4, 256, 128), shape(4, 288, 128), shape(2, 16, 128, dtype=F32)],
-        (low, high, rim_rows, t2),
-        scratch=[pltpu.VMEM((rest, 224, 128), BF16), pltpu.SemaphoreType.DMA],
+        (low, high, rims, gy_a, gy_b, t1, t2),
+        scratch=[
+            pltpu.VMEM((rest, 224, 128), BF16),
+            pltpu.VMEM((size_x - 2, 64, 128), BF16),
+            pltpu.VMEM((2, size_x, 32, 128), BF16),
+            pltpu.SemaphoreType.DMA,
+        ],
         far=(1,),
-        flops=2 * 192 * 256 * 256 * 56,
+        flops=2 * 192 * 256 * 256 * 71,
         nbytes=6 << 20,
     )
     half = shape(size_x // 2, 256, 128)

time: 61.1 us -> 60.2 us (0.985)
  waiting for transfers between devices: 12.6 us -> 11.9 us
    ppermute x1, waiting for transfers between devices: 0.97 us -> 0.2 us  [local(): gy_b = lax.ppermute(gy_b, 'gy', swap(ny, 1))]
  transfers between devices with their start and end apart: 8 -> 8, of which waited for: 4 -> 5; matrix products, arithmetic and copies ran while one was open for 2% -> 2% of each run, Pallas kernels for 19% -> 20%
where the time goes in v3:
time: 60.2 us; the launch traced here: 59.8 us
  starting transfers between devices  27 us (45%)
  Pallas kernels  19.9 us (33%)
  waiting for transfers between devices  11.9 us (20%)
  local copies, waits for them, and re-layouts  0.89 us (1%)
    pallas_call x9, Pallas kernels, vmem_call(): pl.pallas_call(kernel, out_shape=out_shape, in_specs=[pl.BlockSpec(memory...  18.2 us
    all_to_all x1, starting transfers between devices, local(): own = lax.all_to_all(pooled, 'gy', 0, 0)  8.55 us
    all_to_all x1, waiting for transfers between devices, local(): parts = lax.all_to_all(parts, 'gy', 0, 0)  5.38 us
    all_to_all x1, starting transfers between devices, local(): parts = lax.all_to_all(parts, 'gy', 0, 0)  4.91 us
    all_to_all x1, waiting for transfers between devices, local(): own = lax.all_to_all(pooled, 'gy', 0, 0)  3.86 us
    ppermute x1, starting transfers between devices, local(): got_a = lax.ppermute(send_a, 'gx', swap(nx, 0))  3.23 us
    ppermute x1, starting transfers between devices, local(): gr = lax.ppermute(own[:, 0, :], 'gx', ring(nx, -1))  3.18 us
    ppermute x1, waiting for transfers between devices, local(): got_b = lax.ppermute(send_b, 'gx', swap(nx, 1))  2.35 us
  transfers between devices with their start and end apart: 8, of which 5 were waited for; matrix products, arithmetic and copies ran while one was open for 2% of the time, Pallas kernels for 20%

profile of v3, /device:TPU:1, one launch (start us, length us, event | category | flops | bytes accessed | tf_op | source)
XLA Modules:
  0.0 59.8 jit_solution(2026740643922693043)
XLA Ops:
  0.0 0.0 copy-start
  0.0 0.0 copy-start.3
  0.0 0.0 copy-start.2
  0.0 0.0 copy-start.4
  0.0 2.1 %shard_map.74 = (bf16[32,32,128]{2,1,0:T(8,128)(2,1)S(1)}, bf16[32,32,128]{2,1,0:T(8,128)(2,1)S(1)}) custom-call(bf16[16,32,16,128]{3,2,1,0:T(8,128)(2,1)} %far.3), custom_call_target="tpu_custom_call" | custom-call | flops 134217728 | bytes 3145728 | tf_op jit(solution)/shard_map/pallas_call | solution.py:38
  2.1 1.5 %collective-permute-start = (bf16[32,32,128]{2,1,0:T(8,128)(2,1)S(1)}, bf16[32,32,128]{2,1,0:T(8,128)(2,1)S(1)}, u32[]{:S(2)}, u32[]{:S(2)}) collective-permute-start(bf16[32,32,128]{2,1,0:T(8,128)(2,1)S(1)} %get-tuple-element.27), channel_id=1, source_target_pairs={{0,1},{1,0},{2,3},{3,2},{4,5},{5,4},{6,7},{7,6},{8,9},{9,8},{10,11... | collective-permute-start | bytes 786440 | tf_op jit(solution)/shard_map/ppermute | solution.py:544
  3.6 1.4 %collective-permute-start.1 = (bf16[32,32,128]{2,1,0:T(8,128)(2,1)S(1)}, bf16[32,32,128]{2,1,0:T(8,128)(2,1)S(1)}, u32[]{:S(2)}, u32[]{:S(2)}) collective-permute-start(bf16[32,32,128]{2,1,0:T(8,128)(2,1)S(1)} %get-tuple-element.28), channel_id=1, source_target_pairs={{0,15},{1,2},{2,1},{3,4},{4,3},{5,6},{6,5},{7,8},{8,7},{9,10},{10,... | collective-permute-start | bytes 786440 | tf_op jit(solution)/shard_map/ppermute | solution.py:545
  5.0 0.0 copy-done.3
  5.0 0.0 copy-done.2
  5.0 0.1 pad_maximum_fusion
  5.1 0.3 copy.12
  5.4 0.0 copy-done.4
  5.4 0.1 copy.13
  5.5 0.4 rev.4.w_lift
  5.9 0.0 copy-done
  5.9 0.1 constant_dynamic-slice_fusion.w_dec
  6.0 5.4 %shard_map.73 = (bf16[14,224,128]{2,1,0:T(8,128)(2,1)S(1)}, bf16[16,224,128]{2,1,0:T(8,128)(2,1)}, bf16[2,32,32,128]{3,2,1,0:T(8,128)(2,1)S(1)}, bf16[2,2,256,12...) custom-call(bf16[16,32,16,128]{3,2,1,0:T(8,128)(2,1)} %far.3, ...), custom_call_target="tpu_custom_call" | custom-call | flops 1761607680 | bytes 4194304 | tf_op jit(solution)/shard_map/pallas_call | solution.py:38
  11.4 0.0 collective-permute-done.gy_a
  11.4 0.2 collective-permute-done.1.gy_b
  11.7 3.2 %collective-permute-start.2 = (bf16[2,320,128]{2,1,0:T(8,128)(2,1)S(1)}, bf16[2,320,128]{2,1,0:T(8,128)(2,1)S(1)}, u32[]{:S(2)}, u32[]{:S(2)}) collective-permute-start(bf16[2,320,128]{2,1,0:T(8,128)(2,1)S(1)} %get-tuple-element.34.send_a), channel_id=1, source_target_pairs={{0,16},{16,0},{32,48},{48,32},{64,80},{80,64},{96,112},{112,96},{1... | collective-permute-start | bytes 491528 | tf_op jit(solution)/shard_map/ppermute | solution.py:578
  14.9 2.3 %collective-permute-start.3 = (bf16[2,320,128]{2,1,0:T(8,128)(2,1)S(1)}, bf16[2,320,128]{2,1,0:T(8,128)(2,1)S(1)}, u32[]{:S(2)}, u32[]{:S(2)}) collective-permute-start(bf16[2,320,128]{2,1,0:T(8,128)(2,1)S(1)} %get-tuple-element.35.send_b), channel_id=1, source_target_pairs={{0,112},{16,32},{32,16},{48,64},{64,48},{80,96},{96,80},{112,0},{1... | collective-permute-start | bytes 491528 | tf_op jit(solution)/shard_map/ppermute | solution.py:579
  17.2 3.2 %shard_map.75 = (bf16[28,256,128]{2,1,0:T(8,128)(2,1)S(1)}, bf16[4,288,128]{2,1,0:T(8,128)(2,1)S(1)}, f32[2,16,128]{2,1,0:T(8,128)S(1)}) custom-call(bf16[14,224,128]{2,1,0:T(8,128)(2,1)S(1)} %get-tuple-element.24.low, bf16[16,224,128]{2,1,0:T(8,128)(2,1)} %get-tuple-element.25.high_far, bf16[2,32,32,128]{3,2,1,0:T(8,128)(2,1)S(1)} %get-tuple-element.26.rims, ...), custom_call_target="tpu_custom_call" | custom-call | flops 1786773504 | bytes 6291456 | tf_op jit(solution)/shard_map/pallas_call | solution.py:38
  20.4 0.0 collective-permute-done.2.got_a
  20.4 2.3 %collective-permute-done.3.got_b = bf16[2,320,128]{2,1,0:T(8,128)(2,1)S(1)} collective-permute-done((bf16[2,320,128]{2,1,0:T(8,128)(2,1)S(1)}, bf16[2,320,128]{2,1,0:T(8,128)(2,1)S(1)}, u32[]{:S(2)}, u32[]{:S(2)}) %collective-permute-start.3) | collective-permute-done | bytes 163872 | tf_op jit(solution)/shard_map/ppermute | solution.py:579
  22.8 1.9 %shard_map.77 = (bf16[16,256,128]{2,1,0:T(8,128)(2,1)S(1)}, bf16[16,256,128]{2,1,0:T(8,128)(2,1)S(1)}, f32[16,2,128]{2,1,0:T(2,128)}) custom-call(bf16[28,256,128]{2,1,0:T(8,128)(2,1)S(1)} %get-tuple-element.31.inner, bf16[4,288,128]{2,1,0:T(8,128)(2,1)S(1)} %get-tuple-element.32.f1_ends, bf16[2,320,128]{2,1,0:T(8,128)(2,1)S(1)} %get-tuple-element.34.send_a, ...), custom_call_target="tpu_custom_call" | custom-call | flops 427819008 | bytes 1048576 | tf_op jit(solution)/shard_map/pallas_call | solution.py:38
  24.7 8.6 %all-to-all-start = ((f32[16,2,128]{2,1,0:T(2,128)}), f32[16,2,128]{2,1,0:T(2,128)S(1)}, u32[]{:S(2)}, u32[]{:S(2)}) async-start(f32[16,2,128]{2,1,0:T(2,128)} %get-tuple-element.42.after), calls=%async_computation | async-start | bytes 32768 | tf_op jit(solution)/shard_map/all_to_all | solution.py:611
  33.2 0.0 copy-start.1
  33.2 1.9 %shard_map.79.w_coarse = bf16[864,512]{1,0:T(8,128)(2,1)S(1)} custom-call(bf16[864,512]{1,0:T(8,128)(2,1)} %bitcast.11, f32[16,2,128]{2,1,0:T(2,128)} %get-tuple-element.42.after), custom_call_target="tpu_custom_call" | custom-call | flops 268435456 | bytes 4194304 | tf_op jit(solution)/shard_map/pallas_call | solution.py:38
  35.2 3.9 %all-to-all-done.own = f32[16,2,128]{2,1,0:T(2,128)S(1)} async-done(((f32[16,2,128]{2,1,0:T(2,128)}), f32[16,2,128]{2,1,0:T(2,128)S(1)}, u32[]{:S(2)}, u32[]{:S(2)}) %all-to-all-start) | async-done | bytes 16416 | tf_op jit(solution)/shard_map/all_to_all | solution.py:611
  39.0 2.0 %collective-permute-start.4 = (f32[16,128]{1,0:T(8,128)S(1)}, f32[16,128]{1,0:T(8,128)S(1)}, u32[]{:S(2)}, u32[]{:S(2)}) collective-permute-start(f32[16,128]{1,0:T(8,128)S(1)} %bitcast.13), channel_id=1, source_target_pairs={{0,16},{16,32},{32,48},{48,64},{64,80},{80,96},{96,112},{112,0},{1... | collective-permute-start | bytes 24584 | tf_op jit(solution)/shard_map/ppermute | solution.py:621
  41.0 3.2 %collective-permute-start.5 = (f32[16,128]{1,0:T(8,128)S(1)}, f32[16,128]{1,0:T(8,128)S(1)}, u32[]{:S(2)}, u32[]{:S(2)}) collective-permute-start(f32[16,128]{1,0:T(8,128)S(1)} %bitcast.12), channel_id=1, source_target_pairs={{0,112},{16,0},{32,16},{48,32},{64,48},{80,64},{96,80},{112,96},{1... | collective-permute-start | bytes 24584 | tf_op jit(solution)/shard_map/ppermute | solution.py:622
  44.2 1.0 %shard_map.80.mine = f32[2,32,128]{2,1,0:T(8,128)S(1)} custom-call(f32[16,2,128]{2,1,0:T(2,128)S(1)} %all-to-all-done.own, bf16[512,16]{1,0:T(8,128)(2,1)S(1)} %rev.4.w_lift, bf16[864,512]{1,0:T(8,128)(2,1)S(1)} %shard_map.79.w_coarse), custom_call_target="tpu_custom_call" | custom-call | flops 452984832 | bytes 2097152 | tf_op jit(solution)/shard_map/pallas_call | solution.py:38
  45.2 0.1 collective-permute-done.4.gl
  45.2 0.0 collective-permute-done.5.gr
  45.2 2.1 %shard_map.81 = f32[16,2,128]{2,1,0:T(2,128)} custom-call(f32[2,32,128]{2,1,0:T(8,128)S(1)} %shard_map.80.mine, f32[16,128]{1,0:T(8,128)S(1)} %collective-permute-done.4.gl, f32[16,128]{1,0:T(8,128)S(1)} %collective-permute-done.5.gr, bf16[512,16]{1,0:T(8,128)(2,1)S(1)} %rev.4.w_lift, bf16[864,512]{1,0:T(8,128)(2,1)S(1)} %shard_map.79.w_coarse, ...), custom_call_target="tpu_custom_call" | custom-call | flops 226492416 | bytes 2097152 | tf_op jit(solution)/shard_map/pallas_call | solution.py:38
  47.4 4.9 %all-to-all-start.1 = ((f32[16,2,128]{2,1,0:T(2,128)}), f32[16,2,128]{2,1,0:T(2,128)S(1)}, u32[]{:S(2)}, u32[]{:S(2)}) async-start(f32[16,2,128]{2,1,0:T(2,128)} %shard_map.81), calls=%async_computation.1 | async-start | bytes 32768 | tf_op jit(solution)/shard_map/all_to_all | solution.py:637
  52.3 0.0 copy-done.1
  52.3 0.5 shard_map.78
  52.7 5.4 %all-to-all-done.1.parts = f32[16,2,128]{2,1,0:T(2,128)S(1)} async-done(((f32[16,2,128]{2,1,0:T(2,128)}), f32[16,2,128]{2,1,0:T(2,128)S(1)}, u32[]{:S(2)}, u32[]{:S(2)}) %all-to-all-start.1) | async-done | bytes 16416 | tf_op jit(solution)/shard_map/all_to_all | solution.py:637
  58.1 1.7 %shard_map.82 = bf16[16,32,16,128]{3,2,1,0:T(8,128)(2,1)} custom-call(bf16[16,256,128]{2,1,0:T(8,128)(2,1)S(1)} %get-tuple-element.37.second.left, bf16[16,256,128]{2,1,0:T(8,128)(2,1)S(1)} %get-tuple-element.38.right, f32[4,256,128]{2,1,0:T(8,128)S(1)} %get-tuple-element.39.ahead, bf16[256,256]{1,0:T(8,128)(2,1)S(1)} %get-tuple-element.40.matrix, ...), custom_call_target="tpu_custom_call" | custom-call | flops 536870912 | bytes 4194304 | tf_op jit(solution)/shard_map/pallas_call | solution.py:508
  (2 shorter events, 0.0 us)
Async XLA Ops:
  0.0 5.9 %copy-start = (bf16[16,512]{1,0:T(8,128)(2,1)S(1)}, bf16[16,512]{1,0:T(8,128)(2,1)}, u32[]{:S(2)}) copy-start(bf16[16,512]{1,0:T(8,128)(2,1)} %param.12) | copy-start | bytes 49156
  0.0 5.0 %copy-start.3 = (bf16[27,16,16]{0,2,1:T(8,128)(2,1)S(1)}, bf16[27,16,16]{0,2,1:T(8,128)(2,1)}, u32[]{:S(2)}) copy-start(bf16[27,16,16]{0,2,1:T(8,128)(2,1)} %param.8) | copy-start | bytes 41476
  0.0 5.0 %copy-start.2 = (bf16[27,16,16]{0,2,1:T(8,128)(2,1)S(1)}, bf16[27,16,16]{0,2,1:T(8,128)(2,1)}, u32[]{:S(2)}) copy-start(bf16[27,16,16]{0,2,1:T(8,128)(2,1)} %param.9) | copy-start | bytes 41476
  0.0 5.3 %copy-start.4 = (bf16[512,16]{0,1:T(8,128)(2,1)S(1)}, bf16[512,16]{0,1:T(8,128)(2,1)}, u32[]{:S(2)}) copy-start(bf16[512,16]{0,1:T(8,128)(2,1)} %param.10) | copy-start | bytes 49156
  2.1 9.3 %collective-permute-start = (bf16[32,32,128]{2,1,0:T(8,128)(2,1)S(1)}, bf16[32,32,128]{2,1,0:T(8,128)(2,1)S(1)}, u32[]{:S(2)}, u32[]{:S(2)}) collective-permute-start(bf16[32,32,128]{2,1,0:T(8,128)(2,1)S(1)} %get-tuple-element.27), channel_id=1, source_target_pairs={{0,1},{1,0},{2,3},{3,2},{4,5},{5,4},{6,7},{7,6},{8,9},{9,8},{10,11... | collective-permute-start | bytes 786440 | tf_op jit(solution)/shard_map/ppermute | solution.py:544
  3.6 8.0 %collective-permute-start.1 = (bf16[32,32,128]{2,1,0:T(8,128)(2,1)S(1)}, bf16[32,32,128]{2,1,0:T(8,128)(2,1)S(1)}, u32[]{:S(2)}, u32[]{:S(2)}) collective-permute-start(bf16[32,32,128]{2,1,0:T(8,128)(2,1)S(1)} %get-tuple-element.28), channel_id=1, source_target_pairs={{0,15},{1,2},{2,1},{3,4},{4,3},{5,6},{6,5},{7,8},{8,7},{9,10},{10,... | collective-permute-start | bytes 786440 | tf_op jit(solution)/shard_map/ppermute | solution.py:545
  11.7 8.8 %collective-permute-start.2 = (bf16[2,320,128]{2,1,0:T(8,128)(2,1)S(1)}, bf16[2,320,128]{2,1,0:T(8,128)(2,1)S(1)}, u32[]{:S(2)}, u32[]{:S(2)}) collective-permute-start(bf16[2,320,128]{2,1,0:T(8,128)(2,1)S(1)} %get-tuple-element.34.send_a), channel_id=1, source_target_pairs={{0,16},{16,0},{32,48},{48,32},{64,80},{80,64},{96,112},{112,96},{1... | collective-permute-start | bytes 491528 | tf_op jit(solution)/shard_map/ppermute | solution.py:578
  14.9 7.9 %collective-permute-start.3 = (bf16[2,320,128]{2,1,0:T(8,128)(2,1)S(1)}, bf16[2,320,128]{2,1,0:T(8,128)(2,1)S(1)}, u32[]{:S(2)}, u32[]{:S(2)}) collective-permute-start(bf16[2,320,128]{2,1,0:T(8,128)(2,1)S(1)} %get-tuple-element.35.send_b), channel_id=1, source_target_pairs={{0,112},{16,32},{32,16},{48,64},{64,48},{80,96},{96,80},{112,0},{1... | collective-permute-start | bytes 491528 | tf_op jit(solution)/shard_map/ppermute | solution.py:579
  24.7 14.3 %all-to-all-start = ((f32[16,2,128]{2,1,0:T(2,128)}), f32[16,2,128]{2,1,0:T(2,128)S(1)}, u32[]{:S(2)}, u32[]{:S(2)}) async-start(f32[16,2,128]{2,1,0:T(2,128)} %get-tuple-element.42.after), calls=%async_computation | async-start | bytes 32768 | tf_op jit(solution)/shard_map/all_to_all | solution.py:611
  33.2 19.0 %copy-start.1 = (bf16[16,32]{1,0:T(8,128)(2,1)S(1)}, bf16[16,32]{1,0:T(8,128)(2,1)}, u32[]{:S(2)}) copy-start(bf16[16,32]{1,0:T(8,128)(2,1)} %w_join.1) | copy-start | bytes 3076
  39.0 6.2 %collective-permute-start.4 = (f32[16,128]{1,0:T(8,128)S(1)}, f32[16,128]{1,0:T(8,128)S(1)}, u32[]{:S(2)}, u32[]{:S(2)}) collective-permute-start(f32[16,128]{1,0:T(8,128)S(1)} %bitcast.13), channel_id=1, source_target_pairs={{0,16},{16,32},{32,48},{48,64},{64,80},{80,96},{96,112},{112,0},{1... | collective-permute-start | bytes 24584 | tf_op jit(solution)/shard_map/ppermute | solution.py:621
  41.0 4.2 %collective-permute-start.5 = (f32[16,128]{1,0:T(8,128)S(1)}, f32[16,128]{1,0:T(8,128)S(1)}, u32[]{:S(2)}, u32[]{:S(2)}) collective-permute-start(f32[16,128]{1,0:T(8,128)S(1)} %bitcast.12), channel_id=1, source_target_pairs={{0,112},{16,0},{32,16},{48,32},{64,48},{80,64},{96,80},{112,96},{1... | collective-permute-start | bytes 24584 | tf_op jit(solution)/shard_map/ppermute | solution.py:622
  47.4 10.8 %all-to-all-start.1 = ((f32[16,2,128]{2,1,0:T(2,128)}), f32[16,2,128]{2,1,0:T(2,128)S(1)}, u32[]{:S(2)}, u32[]{:S(2)}) async-start(f32[16,2,128]{2,1,0:T(2,128)} %shard_map.81), calls=%async_computation.1 | async-start | bytes 32768 | tf_op jit(solution)/shard_map/all_to_all | solution.py:637

commit v4 on v3

--- a/solution.py
+++ b/solution.py
@@ -350,13 +350,13 @@
             sums[s] = sums[s] + fold_rows(value)
 
     z, lane = iota((128, 128), 0), iota((128, 128), 1)
-    gather = jnp.where((z >> 4) == (lane & 7), 1.0, 0.0).astype(F32)
+    gather = jnp.where((z >> 4) == (lane & 7), 1.0, 0.0).astype(BF16)
     keep = (iota((16, 128), 1) >> 3) == iota((16, 128), 0)
     results = []
+    folded = dot(jnp.concatenate(split3(sums[0]) + split3(sums[1]), axis=0), gather)
     for s in range(2):
-        cells = jnp.dot(
-            sums[s], gather, preferred_element_type=F32, precision=lax.Precision.HIGHEST
-        )
+        first, second, third = (folded[16 * (3 * s + i) : 16 * (3 * s + i) + 16] for i in range(3))
+        cells = first + second + third
         row = jnp.sum(jnp.where(keep, cells, 0.0), axis=0, keepdims=True) * (1.0 / POOL**3)
         results.append(row)
     both = jnp.concatenate(results, axis=0)
@@ -383,9 +383,11 @@
     return total
 
 
-def load_kernel(far, after, out, sem):
+def load_kernel(far, w_lift, after, out, lift, sem):
     fetch = pltpu.make_async_copy(far, out, sem)
     fetch.start()
+    back = (iota((16, 48), 1) & 15) == 15 - iota((16, 48), 0)
+    lift[...] = dot(w_lift[...], jnp.where(back, 1.0, 0.0).astype(BF16)).astype(BF16)
     fetch.wait()
 
 
@@ -394,8 +396,7 @@
     for slab in slabs:
         columns.append(jnp.concatenate(split3(swap_groups(slab)), axis=0))
     stacked = jnp.concatenate(columns, axis=1)
-    lift3 = jnp.concatenate([w_lift] * 3, axis=1)
-    return jnp.maximum(dot(lift3, stacked), 0.0).astype(BF16)
+    return jnp.maximum(dot(w_lift, stacked), 0.0).astype(BF16)
 
 
 def taps(partial, count):
@@ -437,12 +438,15 @@
     m_left = jnp.where(at > 0, 1.0, 0.0).astype(F32)
     m_right = jnp.where(at < last, 1.0, 0.0).astype(F32)
     lifted = lift_slabs([gl[...] * m_left, gr[...] * m_right], w_lift[...])
+    sums = []
     for x in range(2):
         a = 2 * x
         rows = w_coarse[9 * a * count : 9 * (a + 1) * count, :]
-        total = mine[x] + taps(dot(rows, lifted[:, x * 128 : x * 128 + 128]), count)
-        coarse = jnp.maximum(total, 0.0).astype(BF16)
-        rows = swap_groups(dot(w_dec[...], coarse))
+        sums.append(mine[x] + taps(dot(rows, lifted[:, x * 128 : x * 128 + 128]), count))
+    coarse = jnp.maximum(jnp.concatenate(sums, axis=1), 0.0).astype(BF16)
+    decoded = dot(w_dec[...], coarse)
+    for x in range(2):
+        rows = swap_groups(decoded[:, x * 128 : x * 128 + 128])
         for y in range(16):
             out[y, x : x + 1, :] = rows[15 - y : 16 - y, :]
 
@@ -607,12 +611,11 @@
     count = w_coarse.shape[0]
     w_rows = jnp.transpose(w_coarse, (1, 0, 2)).reshape(27 * count, w_coarse.shape[2])
     w_dec = lax.dynamic_slice_in_dim(w_decode, gy * count, count, axis=1)
-    w_lift = jnp.flip(w_lift, axis=1)
     own = lax.all_to_all(pooled, "gy", 0, 0)
-    w_rows = vmem_call(
+    w_rows, w_lift = vmem_call(
         load_kernel,
-        shape(*w_rows.shape),
-        (w_rows, pooled),
+        [shape(*w_rows.shape), shape(w_lift.shape[0], 48)],
+        (w_rows, w_lift, pooled),
         scratch=[pltpu.SemaphoreType.DMA],
         far=(0,),
         flops=1 << 28,

time: 60.2 us -> 60 us (level)
  transfers between devices with their start and end apart: 8 -> 8, of which waited for: 5 -> 6; matrix products, arithmetic and copies ran while one was open for 2% -> 1% of each run, Pallas kernels for 20% -> 20%
where the time goes in v4:
time: 60 us; the launch traced here: 59.6 us
  starting transfers between devices  27 us (45%)
  Pallas kernels  19.5 us (32%)
  waiting for transfers between devices  12.4 us (21%)
    pallas_call x9, Pallas kernels, vmem_call(): pl.pallas_call(kernel, out_shape=out_shape, in_specs=[pl.BlockSpec(memory...  17.8 us
    all_to_all x1, starting transfers between devices, local(): own = lax.all_to_all(pooled, 'gy', 0, 0)  8.69 us
    all_to_all x1, waiting for transfers between devices, local(): parts = lax.all_to_all(parts, 'gy', 0, 0)  5.38 us
    all_to_all x1, starting transfers between devices, local(): parts = lax.all_to_all(parts, 'gy', 0, 0)  4.81 us
    all_to_all x1, waiting for transfers between devices, local(): own = lax.all_to_all(pooled, 'gy', 0, 0)  3.86 us
    ppermute x1, starting transfers between devices, local(): got_a = lax.ppermute(send_a, 'gx', swap(nx, 0))  3.23 us
    ppermute x1, starting transfers between devices, local(): gr = lax.ppermute(own[:, 0, :], 'gx', ring(nx, -1))  3.17 us
    ppermute x1, waiting for transfers between devices, local(): got_b = lax.ppermute(send_b, 'gx', swap(nx, 1))  2.35 us
  transfers between devices with their start and end apart: 8, of which 6 were waited for; matrix products, arithmetic and copies ran while one was open for 1% of the time, Pallas kernels for 20%

profile of v4, /device:TPU:1, one launch (start us, length us, event | category | flops | bytes accessed | tf_op | source)
XLA Modules:
  0.0 59.6 jit_solution(9573877086304160462)
XLA Ops:
  0.0 0.0 copy-start
  0.0 0.0 copy-start.3
  0.0 0.0 copy-start.2
  0.0 0.0 copy-start.4
  0.0 2.1 %shard_map.74 = (bf16[32,32,128]{2,1,0:T(8,128)(2,1)S(1)}, bf16[32,32,128]{2,1,0:T(8,128)(2,1)S(1)}) custom-call(bf16[16,32,16,128]{3,2,1,0:T(8,128)(2,1)} %far.3), custom_call_target="tpu_custom_call" | custom-call | flops 134217728 | bytes 3145728 | tf_op jit(solution)/shard_map/pallas_call | solution.py:38
  2.1 1.5 %collective-permute-start = (bf16[32,32,128]{2,1,0:T(8,128)(2,1)S(1)}, bf16[32,32,128]{2,1,0:T(8,128)(2,1)S(1)}, u32[]{:S(2)}, u32[]{:S(2)}) collective-permute-start(bf16[32,32,128]{2,1,0:T(8,128)(2,1)S(1)} %get-tuple-element.29), channel_id=1, source_target_pairs={{0,1},{1,0},{2,3},{3,2},{4,5},{5,4},{6,7},{7,6},{8,9},{9,8},{10,11... | collective-permute-start | bytes 786440 | tf_op jit(solution)/shard_map/ppermute | solution.py:548
  3.6 1.4 %collective-permute-start.1 = (bf16[32,32,128]{2,1,0:T(8,128)(2,1)S(1)}, bf16[32,32,128]{2,1,0:T(8,128)(2,1)S(1)}, u32[]{:S(2)}, u32[]{:S(2)}) collective-permute-start(bf16[32,32,128]{2,1,0:T(8,128)(2,1)S(1)} %get-tuple-element.30), channel_id=1, source_target_pairs={{0,15},{1,2},{2,1},{3,4},{4,3},{5,6},{6,5},{7,8},{8,7},{9,10},{10,... | collective-permute-start | bytes 786440 | tf_op jit(solution)/shard_map/ppermute | solution.py:549
  5.0 0.0 copy-done.3
  5.0 0.0 copy-done.2
  5.0 0.1 pad_maximum_fusion
  5.1 0.3 copy.12
  5.4 0.0 copy-done.4
  5.4 0.1 copy.13.w_lift
  5.5 0.0 copy-done
  5.5 0.1 constant_dynamic-slice_fusion.w_dec
  5.6 5.4 %shard_map.73 = (bf16[14,224,128]{2,1,0:T(8,128)(2,1)S(1)}, bf16[16,224,128]{2,1,0:T(8,128)(2,1)}, bf16[2,32,32,128]{3,2,1,0:T(8,128)(2,1)S(1)}, bf16[2,2,256,12...) custom-call(bf16[16,32,16,128]{3,2,1,0:T(8,128)(2,1)} %far.3, ...), custom_call_target="tpu_custom_call" | custom-call | flops 1761607680 | bytes 4194304 | tf_op jit(solution)/shard_map/pallas_call | solution.py:38
  11.0 0.0 collective-permute-done.gy_a
  11.0 0.6 %collective-permute-done.1.gy_b = bf16[32,32,128]{2,1,0:T(8,128)(2,1)S(1)} collective-permute-done((bf16[32,32,128]{2,1,0:T(8,128)(2,1)S(1)}, bf16[32,32,128]{2,1,0:T(8,128)(2,1)S(1)}, u32[]{:S(2)}, u32[]{:S(2)}) %collective-permute-start.1) | collective-permute-done | bytes 262176 | tf_op jit(solution)/shard_map/ppermute | solution.py:549
  11.7 3.2 %collective-permute-start.2 = (bf16[2,320,128]{2,1,0:T(8,128)(2,1)S(1)}, bf16[2,320,128]{2,1,0:T(8,128)(2,1)S(1)}, u32[]{:S(2)}, u32[]{:S(2)}) collective-permute-start(bf16[2,320,128]{2,1,0:T(8,128)(2,1)S(1)} %get-tuple-element.36.send_a), channel_id=1, source_target_pairs={{0,16},{16,0},{32,48},{48,32},{64,80},{80,64},{96,112},{112,96},{1... | collective-permute-start | bytes 491528 | tf_op jit(solution)/shard_map/ppermute | solution.py:582
  14.9 2.3 %collective-permute-start.3 = (bf16[2,320,128]{2,1,0:T(8,128)(2,1)S(1)}, bf16[2,320,128]{2,1,0:T(8,128)(2,1)S(1)}, u32[]{:S(2)}, u32[]{:S(2)}) collective-permute-start(bf16[2,320,128]{2,1,0:T(8,128)(2,1)S(1)} %get-tuple-element.37.send_b), channel_id=1, source_target_pairs={{0,112},{16,32},{32,16},{48,64},{64,48},{80,96},{96,80},{112,0},{1... | collective-permute-start | bytes 491528 | tf_op jit(solution)/shard_map/ppermute | solution.py:583
  17.2 3.2 %shard_map.75 = (bf16[28,256,128]{2,1,0:T(8,128)(2,1)S(1)}, bf16[4,288,128]{2,1,0:T(8,128)(2,1)S(1)}, f32[2,16,128]{2,1,0:T(8,128)S(1)}) custom-call(bf16[14,224,128]{2,1,0:T(8,128)(2,1)S(1)} %get-tuple-element.26.low, bf16[16,224,128]{2,1,0:T(8,128)(2,1)} %get-tuple-element.27.high_far, bf16[2,32,32,128]{3,2,1,0:T(8,128)(2,1)S(1)} %get-tuple-element.28.rims, ...), custom_call_target="tpu_custom_call" | custom-call | flops 1786773504 | bytes 6291456 | tf_op jit(solution)/shard_map/pallas_call | solution.py:38
  20.4 0.0 collective-permute-done.2.got_a
  20.4 2.3 %collective-permute-done.3.got_b = bf16[2,320,128]{2,1,0:T(8,128)(2,1)S(1)} collective-permute-done((bf16[2,320,128]{2,1,0:T(8,128)(2,1)S(1)}, bf16[2,320,128]{2,1,0:T(8,128)(2,1)S(1)}, u32[]{:S(2)}, u32[]{:S(2)}) %collective-permute-start.3) | collective-permute-done | bytes 163872 | tf_op jit(solution)/shard_map/ppermute | solution.py:583
  22.8 1.8 %shard_map.77 = (bf16[16,256,128]{2,1,0:T(8,128)(2,1)S(1)}, bf16[16,256,128]{2,1,0:T(8,128)(2,1)S(1)}, f32[16,2,128]{2,1,0:T(2,128)}) custom-call(bf16[28,256,128]{2,1,0:T(8,128)(2,1)S(1)} %get-tuple-element.33.inner, bf16[4,288,128]{2,1,0:T(8,128)(2,1)S(1)} %get-tuple-element.34.f1_ends, bf16[2,320,128]{2,1,0:T(8,128)(2,1)S(1)} %get-tuple-element.36.send_a, ...), custom_call_target="tpu_custom_call" | custom-call | flops 427819008 | bytes 1048576 | tf_op jit(solution)/shard_map/pallas_call | solution.py:38
  24.6 0.0 copy-start.1
  24.6 8.7 %all-to-all-start = ((f32[16,2,128]{2,1,0:T(2,128)}), f32[16,2,128]{2,1,0:T(2,128)S(1)}, u32[]{:S(2)}, u32[]{:S(2)}) async-start(f32[16,2,128]{2,1,0:T(2,128)} %get-tuple-element.44.after), calls=%async_computation | async-start | bytes 32768 | tf_op jit(solution)/shard_map/all_to_all | solution.py:614
  33.3 1.9 %shard_map.79 = (bf16[864,512]{1,0:T(8,128)(2,1)S(1)}, bf16[512,48]{1,0:T(8,128)(2,1)S(1)}) custom-call(bf16[864,512]{1,0:T(8,128)(2,1)} %bitcast.11, bf16[512,16]{1,0:T(8,128)(2,1)S(1)} %copy.13.w_lift, f32[16,2,128]{2,1,0:T(2,128)} %get-tuple-element.44.after), custom_call_target="tpu_custom_call" | custom-call | flops 268435456 | bytes 4194304 | tf_op jit(solution)/shard_map/pallas_call | solution.py:38
  35.2 3.9 %all-to-all-done.own = f32[16,2,128]{2,1,0:T(2,128)S(1)} async-done(((f32[16,2,128]{2,1,0:T(2,128)}), f32[16,2,128]{2,1,0:T(2,128)S(1)}, u32[]{:S(2)}, u32[]{:S(2)}) %all-to-all-start) | async-done | bytes 16416 | tf_op jit(solution)/shard_map/all_to_all | solution.py:614
  39.1 2.0 %collective-permute-start.4 = (f32[16,128]{1,0:T(8,128)S(1)}, f32[16,128]{1,0:T(8,128)S(1)}, u32[]{:S(2)}, u32[]{:S(2)}) collective-permute-start(f32[16,128]{1,0:T(8,128)S(1)} %bitcast.13), channel_id=1, source_target_pairs={{0,16},{16,32},{32,48},{48,64},{64,80},{80,96},{96,112},{112,0},{1... | collective-permute-start | bytes 24584 | tf_op jit(solution)/shard_map/ppermute | solution.py:624
  41.1 3.2 %collective-permute-start.5 = (f32[16,128]{1,0:T(8,128)S(1)}, f32[16,128]{1,0:T(8,128)S(1)}, u32[]{:S(2)}, u32[]{:S(2)}) collective-permute-start(f32[16,128]{1,0:T(8,128)S(1)} %bitcast.12), channel_id=1, source_target_pairs={{0,112},{16,0},{32,16},{48,32},{64,48},{80,64},{96,80},{112,96},{1... | collective-permute-start | bytes 24584 | tf_op jit(solution)/shard_map/ppermute | solution.py:625
  44.2 1.0 %shard_map.80.mine = f32[2,32,128]{2,1,0:T(8,128)S(1)} custom-call(f32[16,2,128]{2,1,0:T(2,128)S(1)} %all-to-all-done.own, bf16[512,48]{1,0:T(8,128)(2,1)S(1)} %get-tuple-element.45.w_lift, bf16[864,512]{1,0:T(8,128)(2,1)S(1)} %get-tuple-element.46.w_coarse), custom_call_target="tpu_custom_call" | custom-call | flops 452984832 | bytes 2097152 | tf_op jit(solution)/shard_map/pallas_call | solution.py:38
  45.2 0.1 collective-permute-done.4.gl
  45.3 0.1 collective-permute-done.5.gr
  45.4 1.8 %shard_map.81 = f32[16,2,128]{2,1,0:T(2,128)} custom-call(f32[2,32,128]{2,1,0:T(8,128)S(1)} %shard_map.80.mine, f32[16,128]{1,0:T(8,128)S(1)} %collective-permute-done.4.gl, f32[16,128]{1,0:T(8,128)S(1)} %collective-permute-done.5.gr, bf16[512,48]{1,0:T(8,128)(2,1)S(1)} %get-tuple-element.45.w_lift, bf16[864,512]{1,0:T(8,128)(2,1)S(1)} %get-tuple-element.46.w_coarse, ...), custom_call_target="tpu_custom_call" | custom-call | flops 226492416 | bytes 2097152 | tf_op jit(solution)/shard_map/pallas_call | solution.py:38
  47.2 4.8 %all-to-all-start.1 = ((f32[16,2,128]{2,1,0:T(2,128)}), f32[16,2,128]{2,1,0:T(2,128)S(1)}, u32[]{:S(2)}, u32[]{:S(2)}) async-start(f32[16,2,128]{2,1,0:T(2,128)} %shard_map.81), calls=%async_computation.1 | async-start | bytes 32768 | tf_op jit(solution)/shard_map/all_to_all | solution.py:640
  52.0 0.0 copy-done.1
  52.0 0.5 shard_map.78
  52.5 5.4 %all-to-all-done.1.parts = f32[16,2,128]{2,1,0:T(2,128)S(1)} async-done(((f32[16,2,128]{2,1,0:T(2,128)}), f32[16,2,128]{2,1,0:T(2,128)S(1)}, u32[]{:S(2)}, u32[]{:S(2)}) %all-to-all-start.1) | async-done | bytes 16416 | tf_op jit(solution)/shard_map/all_to_all | solution.py:640
  57.9 1.7 %shard_map.82 = bf16[16,32,16,128]{3,2,1,0:T(8,128)(2,1)} custom-call(bf16[16,256,128]{2,1,0:T(8,128)(2,1)S(1)} %get-tuple-element.39.second.left, bf16[16,256,128]{2,1,0:T(8,128)(2,1)S(1)} %get-tuple-element.40.right, f32[4,256,128]{2,1,0:T(8,128)S(1)} %get-tuple-element.41.ahead, bf16[256,256]{1,0:T(8,128)(2,1)S(1)} %get-tuple-element.42.matrix, ...), custom_call_target="tpu_custom_call" | custom-call | flops 536870912 | bytes 4194304 | tf_op jit(solution)/shard_map/pallas_call | solution.py:512
  (2 shorter events, 0.0 us)
Async XLA Ops:
  0.0 5.5 %copy-start = (bf16[16,512]{1,0:T(8,128)(2,1)S(1)}, bf16[16,512]{1,0:T(8,128)(2,1)}, u32[]{:S(2)}) copy-start(bf16[16,512]{1,0:T(8,128)(2,1)} %param.12) | copy-start | bytes 49156
  0.0 5.0 %copy-start.3 = (bf16[27,16,16]{0,2,1:T(8,128)(2,1)S(1)}, bf16[27,16,16]{0,2,1:T(8,128)(2,1)}, u32[]{:S(2)}) copy-start(bf16[27,16,16]{0,2,1:T(8,128)(2,1)} %param.8) | copy-start | bytes 41476
  0.0 5.0 %copy-start.2 = (bf16[27,16,16]{0,2,1:T(8,128)(2,1)S(1)}, bf16[27,16,16]{0,2,1:T(8,128)(2,1)}, u32[]{:S(2)}) copy-start(bf16[27,16,16]{0,2,1:T(8,128)(2,1)} %param.9) | copy-start | bytes 41476
  0.0 5.3 %copy-start.4 = (bf16[512,16]{0,1:T(8,128)(2,1)S(1)}, bf16[512,16]{0,1:T(8,128)(2,1)}, u32[]{:S(2)}) copy-start(bf16[512,16]{0,1:T(8,128)(2,1)} %param.10) | copy-start | bytes 49156
  2.1 8.8 %collective-permute-start = (bf16[32,32,128]{2,1,0:T(8,128)(2,1)S(1)}, bf16[32,32,128]{2,1,0:T(8,128)(2,1)S(1)}, u32[]{:S(2)}, u32[]{:S(2)}) collective-permute-start(bf16[32,32,128]{2,1,0:T(8,128)(2,1)S(1)} %get-tuple-element.29), channel_id=1, source_target_pairs={{0,1},{1,0},{2,3},{3,2},{4,5},{5,4},{6,7},{7,6},{8,9},{9,8},{10,11... | collective-permute-start | bytes 786440 | tf_op jit(solution)/shard_map/ppermute | solution.py:548
  3.6 8.0 %collective-permute-start.1 = (bf16[32,32,128]{2,1,0:T(8,128)(2,1)S(1)}, bf16[32,32,128]{2,1,0:T(8,128)(2,1)S(1)}, u32[]{:S(2)}, u32[]{:S(2)}) collective-permute-start(bf16[32,32,128]{2,1,0:T(8,128)(2,1)S(1)} %get-tuple-element.30), channel_id=1, source_target_pairs={{0,15},{1,2},{2,1},{3,4},{4,3},{5,6},{6,5},{7,8},{8,7},{9,10},{10,... | collective-permute-start | bytes 786440 | tf_op jit(solution)/shard_map/ppermute | solution.py:549
  11.7 8.8 %collective-permute-start.2 = (bf16[2,320,128]{2,1,0:T(8,128)(2,1)S(1)}, bf16[2,320,128]{2,1,0:T(8,128)(2,1)S(1)}, u32[]{:S(2)}, u32[]{:S(2)}) collective-permute-start(bf16[2,320,128]{2,1,0:T(8,128)(2,1)S(1)} %get-tuple-element.36.send_a), channel_id=1, source_target_pairs={{0,16},{16,0},{32,48},{48,32},{64,80},{80,64},{96,112},{112,96},{1... | collective-permute-start | bytes 491528 | tf_op jit(solution)/shard_map/ppermute | solution.py:582
  14.9 7.9 %collective-permute-start.3 = (bf16[2,320,128]{2,1,0:T(8,128)(2,1)S(1)}, bf16[2,320,128]{2,1,0:T(8,128)(2,1)S(1)}, u32[]{:S(2)}, u32[]{:S(2)}) collective-permute-start(bf16[2,320,128]{2,1,0:T(8,128)(2,1)S(1)} %get-tuple-element.37.send_b), channel_id=1, source_target_pairs={{0,112},{16,32},{32,16},{48,64},{64,48},{80,96},{96,80},{112,0},{1... | collective-permute-start | bytes 491528 | tf_op jit(solution)/shard_map/ppermute | solution.py:583
  24.6 27.4 %copy-start.1 = (bf16[16,32]{1,0:T(8,128)(2,1)S(1)}, bf16[16,32]{1,0:T(8,128)(2,1)}, u32[]{:S(2)}) copy-start(bf16[16,32]{1,0:T(8,128)(2,1)} %w_join.1) | copy-start | bytes 3076
  24.6 14.5 %all-to-all-start = ((f32[16,2,128]{2,1,0:T(2,128)}), f32[16,2,128]{2,1,0:T(2,128)S(1)}, u32[]{:S(2)}, u32[]{:S(2)}) async-start(f32[16,2,128]{2,1,0:T(2,128)} %get-tuple-element.44.after), calls=%async_computation | async-start | bytes 32768 | tf_op jit(solution)/shard_map/all_to_all | solution.py:614
  39.1 6.2 %collective-permute-start.4 = (f32[16,128]{1,0:T(8,128)S(1)}, f32[16,128]{1,0:T(8,128)S(1)}, u32[]{:S(2)}, u32[]{:S(2)}) collective-permute-start(f32[16,128]{1,0:T(8,128)S(1)} %bitcast.13), channel_id=1, source_target_pairs={{0,16},{16,32},{32,48},{48,64},{64,80},{80,96},{96,112},{112,0},{1... | collective-permute-start | bytes 24584 | tf_op jit(solution)/shard_map/ppermute | solution.py:624
  41.1 4.3 %collective-permute-start.5 = (f32[16,128]{1,0:T(8,128)S(1)}, f32[16,128]{1,0:T(8,128)S(1)}, u32[]{:S(2)}, u32[]{:S(2)}) collective-permute-start(f32[16,128]{1,0:T(8,128)S(1)} %bitcast.12), channel_id=1, source_target_pairs={{0,112},{16,0},{32,16},{48,32},{64,48},{80,64},{96,80},{112,96},{1... | collective-permute-start | bytes 24584 | tf_op jit(solution)/shard_map/ppermute | solution.py:625
  47.2 10.7 %all-to-all-start.1 = ((f32[16,2,128]{2,1,0:T(2,128)}), f32[16,2,128]{2,1,0:T(2,128)S(1)}, u32[]{:S(2)}, u32[]{:S(2)}) async-start(f32[16,2,128]{2,1,0:T(2,128)} %shard_map.81), calls=%async_computation.1 | async-start | bytes 32768 | tf_op jit(solution)/shard_map/all_to_all | solution.py:640

commit v5 on v4

--- a/solution.py
+++ b/solution.py
@@ -55,6 +55,9 @@
     )(*args)
 
 
+RINGS = ('gy',)
+
+
 def side_flags(axis):
     at, count = lax.axis_index(axis), lax.axis_size(axis)
     even = lax.rem(at, 2) == 0
@@ -63,6 +66,8 @@
         return jnp.where(flag, 1.0, 0.0).astype(F32)
 
     inner_left, inner_right = at > 0, at < count - 1
+    if axis in RINGS:
+        return (number(inner_left), 0.0), (0.0, number(inner_right))
     left = number(jnp.logical_not(even)), number(jnp.logical_and(even, inner_left))
     right = number(even), number(jnp.logical_and(jnp.logical_not(even), inner_right))
     return left, right
@@ -77,6 +82,8 @@
 
 
 def is_even(axis):
+    if axis in RINGS:
+        return jnp.int32(1)
     return jnp.where(lax.rem(lax.axis_index(axis), 2) == 0, 1, 0)
 
 
@@ -545,8 +552,8 @@
         flops=2 * 64 * 256 * 128 * size_x,
         nbytes=3 << 20,
     )
-    gy_a = lax.ppermute(gy_a, "gy", swap(ny, 0))
-    gy_b = lax.ppermute(gy_b, "gy", swap(ny, 1))
+    gy_a = lax.ppermute(gy_a, "gy", ring(ny, 1))
+    gy_b = lax.ppermute(gy_b, "gy", ring(ny, -1))
 
     w_fine = jnp.concatenate([w_first, w_second], axis=0).reshape(864, 16)
     near, rest = size_x // 2 - 2, size_x // 2

time: 60 us -> 59.7 us (level)
  starting transfers between devices: 27 us -> 25.4 us
  waiting for transfers between devices: 12.4 us -> 13.6 us
    ppermute x2, waiting for transfers between devices: 0.62 us -> 2.07 us  [the longest x1 2.06 us: local(): gy_b = lax.ppermute(gy_b, 'gy', ring(ny, -1))]
    all_to_all x1, starting transfers between devices: 8.69 us -> 7.45 us  [local(): own = lax.all_to_all(pooled, 'gy', 0, 0)]
    ppermute x1, waiting for transfers between devices: 2.35 us -> 1.34 us  [local(): got_b = lax.ppermute(send_b, 'gx', swap(nx, 1))]
    ppermute x1, waiting for transfers between devices: 0.01 us -> 0.92 us  [local(): got_a = lax.ppermute(send_a, 'gx', swap(nx, 0))]
where the time goes in v5:
time: 59.7 us; the launch traced here: 59.3 us
  starting transfers between devices  25.4 us (43%)
  Pallas kernels  19.5 us (33%)
  waiting for transfers between devices  13.6 us (23%)
    pallas_call x9, Pallas kernels, vmem_call(): pl.pallas_call(kernel, out_shape=out_shape, in_specs=[pl.BlockSpec(memory...  17.8 us
    all_to_all x1, starting transfers between devices, local(): own = lax.all_to_all(pooled, 'gy', 0, 0)  7.45 us
    all_to_all x1, waiting for transfers between devices, local(): parts = lax.all_to_all(parts, 'gy', 0, 0)  5.38 us
    all_to_all x1, starting transfers between devices, local(): parts = lax.all_to_all(parts, 'gy', 0, 0)  4.82 us
    all_to_all x1, waiting for transfers between devices, local(): own = lax.all_to_all(pooled, 'gy', 0, 0)  3.86 us
    ppermute x1, starting transfers between devices, local(): gr = lax.ppermute(own[:, 0, :], 'gx', ring(nx, -1))  3.67 us
    ppermute x1, starting transfers between devices, local(): got_a = lax.ppermute(send_a, 'gx', swap(nx, 0))  2.99 us
    ppermute x1, starting transfers between devices, local(): gy_a = lax.ppermute(gy_a, 'gy', ring(ny, 1))  2.74 us
  transfers between devices with their start and end apart: 8, of which 6 were waited for; matrix products, arithmetic and copies ran while one was open for 1% of the time, Pallas kernels for 20%

profile of v5, /device:TPU:1, one launch (start us, length us, event | category | flops | bytes accessed | tf_op | source)
XLA Modules:
  0.0 59.3 jit_solution(7936093655293882806)
XLA Ops:
  0.0 0.0 copy-start
  0.0 0.0 copy-start.3
  0.0 0.0 copy-start.2
  0.0 0.0 copy-start.4
  0.0 2.1 %shard_map.74 = (bf16[32,32,128]{2,1,0:T(8,128)(2,1)S(1)}, bf16[32,32,128]{2,1,0:T(8,128)(2,1)S(1)}) custom-call(bf16[16,32,16,128]{3,2,1,0:T(8,128)(2,1)} %far.3), custom_call_target="tpu_custom_call" | custom-call | flops 134217728 | bytes 3145728 | tf_op jit(solution)/shard_map/pallas_call | solution.py:38
  2.1 2.7 %collective-permute-start = (bf16[32,32,128]{2,1,0:T(8,128)(2,1)S(1)}, bf16[32,32,128]{2,1,0:T(8,128)(2,1)S(1)}, u32[]{:S(2)}, u32[]{:S(2)}) collective-permute-start(bf16[32,32,128]{2,1,0:T(8,128)(2,1)S(1)} %get-tuple-element.29), channel_id=1, source_target_pairs={{0,1},{1,2},{2,3},{3,4},{4,5},{5,6},{6,7},{7,8},{8,9},{9,10},{10,1... | collective-permute-start | bytes 786440 | tf_op jit(solution)/shard_map/ppermute | solution.py:555
  4.9 0.0 collective-permute-start.1
  4.9 0.0 copy-done.3
  4.9 0.0 copy-done.2
  4.9 0.1 pad_maximum_fusion
  5.0 0.3 copy.12
  5.3 0.0 copy-done.4
  5.3 0.1 copy.13.w_lift
  5.4 0.0 copy-done
  5.4 0.1 constant_dynamic-slice_fusion.w_dec
  5.5 5.4 %shard_map.73 = (bf16[14,224,128]{2,1,0:T(8,128)(2,1)S(1)}, bf16[16,224,128]{2,1,0:T(8,128)(2,1)}, bf16[2,32,32,128]{3,2,1,0:T(8,128)(2,1)S(1)}, bf16[2,2,256,12...) custom-call(bf16[16,32,16,128]{3,2,1,0:T(8,128)(2,1)} %far.3, ...), custom_call_target="tpu_custom_call" | custom-call | flops 1761607680 | bytes 4194304 | tf_op jit(solution)/shard_map/pallas_call | solution.py:38
  10.9 0.0 collective-permute-done.gy_a
  10.9 2.1 %collective-permute-done.1.gy_b = bf16[32,32,128]{2,1,0:T(8,128)(2,1)S(1)} collective-permute-done((bf16[32,32,128]{2,1,0:T(8,128)(2,1)S(1)}, bf16[32,32,128]{2,1,0:T(8,128)(2,1)S(1)}, u32[]{:S(2)}, u32[]{:S(2)}) %collective-permute-start.1) | collective-permute-done | bytes 262176 | tf_op jit(solution)/shard_map/ppermute | solution.py:556
  13.0 3.0 %collective-permute-start.2 = (bf16[2,320,128]{2,1,0:T(8,128)(2,1)S(1)}, bf16[2,320,128]{2,1,0:T(8,128)(2,1)S(1)}, u32[]{:S(2)}, u32[]{:S(2)}) collective-permute-start(bf16[2,320,128]{2,1,0:T(8,128)(2,1)S(1)} %get-tuple-element.36.send_a), channel_id=1, source_target_pairs={{0,16},{16,0},{32,48},{48,32},{64,80},{80,64},{96,112},{112,96},{1... | collective-permute-start | bytes 491528 | tf_op jit(solution)/shard_map/ppermute | solution.py:589
  16.0 2.3 %collective-permute-start.3 = (bf16[2,320,128]{2,1,0:T(8,128)(2,1)S(1)}, bf16[2,320,128]{2,1,0:T(8,128)(2,1)S(1)}, u32[]{:S(2)}, u32[]{:S(2)}) collective-permute-start(bf16[2,320,128]{2,1,0:T(8,128)(2,1)S(1)} %get-tuple-element.37.send_b), channel_id=1, source_target_pairs={{0,112},{16,32},{32,16},{48,64},{64,48},{80,96},{96,80},{112,0},{1... | collective-permute-start | bytes 491528 | tf_op jit(solution)/shard_map/ppermute | solution.py:590
  18.3 3.2 %shard_map.75 = (bf16[28,256,128]{2,1,0:T(8,128)(2,1)S(1)}, bf16[4,288,128]{2,1,0:T(8,128)(2,1)S(1)}, f32[2,16,128]{2,1,0:T(8,128)S(1)}) custom-call(bf16[14,224,128]{2,1,0:T(8,128)(2,1)S(1)} %get-tuple-element.26.low, bf16[16,224,128]{2,1,0:T(8,128)(2,1)} %get-tuple-element.27.high_far, bf16[2,32,32,128]{3,2,1,0:T(8,128)(2,1)S(1)} %get-tuple-element.28.rims, ...), custom_call_target="tpu_custom_call" | custom-call | flops 1786773504 | bytes 6291456 | tf_op jit(solution)/shard_map/pallas_call | solution.py:38
  21.5 0.9 %collective-permute-done.2.got_a = bf16[2,320,128]{2,1,0:T(8,128)(2,1)S(1)} collective-permute-done((bf16[2,320,128]{2,1,0:T(8,128)(2,1)S(1)}, bf16[2,320,128]{2,1,0:T(8,128)(2,1)S(1)}, u32[]{:S(2)}, u32[]{:S(2)}) %collective-permute-start.2) | collective-permute-done | bytes 163872 | tf_op jit(solution)/shard_map/ppermute | solution.py:589
  22.4 1.3 %collective-permute-done.3.got_b = bf16[2,320,128]{2,1,0:T(8,128)(2,1)S(1)} collective-permute-done((bf16[2,320,128]{2,1,0:T(8,128)(2,1)S(1)}, bf16[2,320,128]{2,1,0:T(8,128)(2,1)S(1)}, u32[]{:S(2)}, u32[]{:S(2)}) %collective-permute-start.3) | collective-permute-done | bytes 163872 | tf_op jit(solution)/shard_map/ppermute | solution.py:590
  23.8 1.8 %shard_map.77 = (bf16[16,256,128]{2,1,0:T(8,128)(2,1)S(1)}, bf16[16,256,128]{2,1,0:T(8,128)(2,1)S(1)}, f32[16,2,128]{2,1,0:T(2,128)}) custom-call(bf16[28,256,128]{2,1,0:T(8,128)(2,1)S(1)} %get-tuple-element.33.inner, bf16[4,288,128]{2,1,0:T(8,128)(2,1)S(1)} %get-tuple-element.34.f1_ends, bf16[2,320,128]{2,1,0:T(8,128)(2,1)S(1)} %get-tuple-element.36.send_a, ...), custom_call_target="tpu_custom_call" | custom-call | flops 427819008 | bytes 1048576 | tf_op jit(solution)/shard_map/pallas_call | solution.py:38
  25.6 0.0 copy-start.1
  25.6 7.4 %all-to-all-start = ((f32[16,2,128]{2,1,0:T(2,128)}), f32[16,2,128]{2,1,0:T(2,128)S(1)}, u32[]{:S(2)}, u32[]{:S(2)}) async-start(f32[16,2,128]{2,1,0:T(2,128)} %get-tuple-element.44.after), calls=%async_computation | async-start | bytes 32768 | tf_op jit(solution)/shard_map/all_to_all | solution.py:621
  33.0 1.9 %shard_map.79 = (bf16[864,512]{1,0:T(8,128)(2,1)S(1)}, bf16[512,48]{1,0:T(8,128)(2,1)S(1)}) custom-call(bf16[864,512]{1,0:T(8,128)(2,1)} %bitcast.11, bf16[512,16]{1,0:T(8,128)(2,1)S(1)} %copy.13.w_lift, f32[16,2,128]{2,1,0:T(2,128)} %get-tuple-element.44.after), custom_call_target="tpu_custom_call" | custom-call | flops 268435456 | bytes 4194304 | tf_op jit(solution)/shard_map/pallas_call | solution.py:38
  35.0 3.9 %all-to-all-done.own = f32[16,2,128]{2,1,0:T(2,128)S(1)} async-done(((f32[16,2,128]{2,1,0:T(2,128)}), f32[16,2,128]{2,1,0:T(2,128)S(1)}, u32[]{:S(2)}, u32[]{:S(2)}) %all-to-all-start) | async-done | bytes 16416 | tf_op jit(solution)/shard_map/all_to_all | solution.py:621
  38.9 1.5 %collective-permute-start.4 = (f32[16,128]{1,0:T(8,128)S(1)}, f32[16,128]{1,0:T(8,128)S(1)}, u32[]{:S(2)}, u32[]{:S(2)}) collective-permute-start(f32[16,128]{1,0:T(8,128)S(1)} %bitcast.13), channel_id=1, source_target_pairs={{0,16},{16,32},{32,48},{48,64},{64,80},{80,96},{96,112},{112,0},{1... | collective-permute-start | bytes 24584 | tf_op jit(solution)/shard_map/ppermute | solution.py:631
  40.3 3.7 %collective-permute-start.5 = (f32[16,128]{1,0:T(8,128)S(1)}, f32[16,128]{1,0:T(8,128)S(1)}, u32[]{:S(2)}, u32[]{:S(2)}) collective-permute-start(f32[16,128]{1,0:T(8,128)S(1)} %bitcast.12), channel_id=1, source_target_pairs={{0,112},{16,0},{32,16},{48,32},{64,48},{80,64},{96,80},{112,96},{1... | collective-permute-start | bytes 24584 | tf_op jit(solution)/shard_map/ppermute | solution.py:632
  44.0 1.0 %shard_map.80.mine = f32[2,32,128]{2,1,0:T(8,128)S(1)} custom-call(f32[16,2,128]{2,1,0:T(2,128)S(1)} %all-to-all-done.own, bf16[512,48]{1,0:T(8,128)(2,1)S(1)} %get-tuple-element.45.w_lift, bf16[864,512]{1,0:T(8,128)(2,1)S(1)} %get-tuple-element.46.w_coarse), custom_call_target="tpu_custom_call" | custom-call | flops 452984832 | bytes 2097152 | tf_op jit(solution)/shard_map/pallas_call | solution.py:38
  45.0 0.1 collective-permute-done.4.gl
  45.0 0.0 collective-permute-done.5.gr
  45.0 1.8 %shard_map.81 = f32[16,2,128]{2,1,0:T(2,128)} custom-call(f32[2,32,128]{2,1,0:T(8,128)S(1)} %shard_map.80.mine, f32[16,128]{1,0:T(8,128)S(1)} %collective-permute-done.4.gl, f32[16,128]{1,0:T(8,128)S(1)} %collective-permute-done.5.gr, bf16[512,48]{1,0:T(8,128)(2,1)S(1)} %get-tuple-element.45.w_lift, bf16[864,512]{1,0:T(8,128)(2,1)S(1)} %get-tuple-element.46.w_coarse, ...), custom_call_target="tpu_custom_call" | custom-call | flops 226492416 | bytes 2097152 | tf_op jit(solution)/shard_map/pallas_call | solution.py:38
  46.9 4.8 %all-to-all-start.1 = ((f32[16,2,128]{2,1,0:T(2,128)}), f32[16,2,128]{2,1,0:T(2,128)S(1)}, u32[]{:S(2)}, u32[]{:S(2)}) async-start(f32[16,2,128]{2,1,0:T(2,128)} %shard_map.81), calls=%async_computation.1 | async-start | bytes 32768 | tf_op jit(solution)/shard_map/all_to_all | solution.py:647
  51.7 0.0 copy-done.1
  51.7 0.5 shard_map.78
  52.2 5.4 %all-to-all-done.1.parts = f32[16,2,128]{2,1,0:T(2,128)S(1)} async-done(((f32[16,2,128]{2,1,0:T(2,128)}), f32[16,2,128]{2,1,0:T(2,128)S(1)}, u32[]{:S(2)}, u32[]{:S(2)}) %all-to-all-start.1) | async-done | bytes 16416 | tf_op jit(solution)/shard_map/all_to_all | solution.py:647
  57.5 1.7 %shard_map.82 = bf16[16,32,16,128]{3,2,1,0:T(8,128)(2,1)} custom-call(bf16[16,256,128]{2,1,0:T(8,128)(2,1)S(1)} %get-tuple-element.39.second.left, bf16[16,256,128]{2,1,0:T(8,128)(2,1)S(1)} %get-tuple-element.40.right, f32[4,256,128]{2,1,0:T(8,128)S(1)} %get-tuple-element.41.ahead, bf16[256,256]{1,0:T(8,128)(2,1)S(1)} %get-tuple-element.42.matrix, ...), custom_call_target="tpu_custom_call" | custom-call | flops 536870912 | bytes 4194304 | tf_op jit(solution)/shard_map/pallas_call | solution.py:519
  (2 shorter events, 0.0 us)
Async XLA Ops:
  0.0 5.4 %copy-start = (bf16[16,512]{1,0:T(8,128)(2,1)S(1)}, bf16[16,512]{1,0:T(8,128)(2,1)}, u32[]{:S(2)}) copy-start(bf16[16,512]{1,0:T(8,128)(2,1)} %param.12) | copy-start | bytes 49156
  0.0 4.9 %copy-start.3 = (bf16[27,16,16]{0,2,1:T(8,128)(2,1)S(1)}, bf16[27,16,16]{0,2,1:T(8,128)(2,1)}, u32[]{:S(2)}) copy-start(bf16[27,16,16]{0,2,1:T(8,128)(2,1)} %param.8) | copy-start | bytes 41476
  0.0 4.9 %copy-start.2 = (bf16[27,16,16]{0,2,1:T(8,128)(2,1)S(1)}, bf16[27,16,16]{0,2,1:T(8,128)(2,1)}, u32[]{:S(2)}) copy-start(bf16[27,16,16]{0,2,1:T(8,128)(2,1)} %param.9) | copy-start | bytes 41476
  0.0 5.3 %copy-start.4 = (bf16[512,16]{0,1:T(8,128)(2,1)S(1)}, bf16[512,16]{0,1:T(8,128)(2,1)}, u32[]{:S(2)}) copy-start(bf16[512,16]{0,1:T(8,128)(2,1)} %param.10) | copy-start | bytes 49156
  2.1 8.8 %collective-permute-start = (bf16[32,32,128]{2,1,0:T(8,128)(2,1)S(1)}, bf16[32,32,128]{2,1,0:T(8,128)(2,1)S(1)}, u32[]{:S(2)}, u32[]{:S(2)}) collective-permute-start(bf16[32,32,128]{2,1,0:T(8,128)(2,1)S(1)} %get-tuple-element.29), channel_id=1, source_target_pairs={{0,1},{1,2},{2,3},{3,4},{4,5},{5,6},{6,7},{7,8},{8,9},{9,10},{10,1... | collective-permute-start | bytes 786440 | tf_op jit(solution)/shard_map/ppermute | solution.py:555
  4.9 8.1 %collective-permute-start.1 = (bf16[32,32,128]{2,1,0:T(8,128)(2,1)S(1)}, bf16[32,32,128]{2,1,0:T(8,128)(2,1)S(1)}, u32[]{:S(2)}, u32[]{:S(2)}) collective-permute-start(bf16[32,32,128]{2,1,0:T(8,128)(2,1)S(1)} %get-tuple-element.30), channel_id=1, source_target_pairs={{0,15},{1,0},{2,1},{3,2},{4,3},{5,4},{6,5},{7,6},{8,7},{9,8},{10,9... | collective-permute-start | bytes 786440 | tf_op jit(solution)/shard_map/ppermute | solution.py:556
  13.0 9.4 %collective-permute-start.2 = (bf16[2,320,128]{2,1,0:T(8,128)(2,1)S(1)}, bf16[2,320,128]{2,1,0:T(8,128)(2,1)S(1)}, u32[]{:S(2)}, u32[]{:S(2)}) collective-permute-start(bf16[2,320,128]{2,1,0:T(8,128)(2,1)S(1)} %get-tuple-element.36.send_a), channel_id=1, source_target_pairs={{0,16},{16,0},{32,48},{48,32},{64,80},{80,64},{96,112},{112,96},{1... | collective-permute-start | bytes 491528 | tf_op jit(solution)/shard_map/ppermute | solution.py:589
  16.0 7.8 %collective-permute-start.3 = (bf16[2,320,128]{2,1,0:T(8,128)(2,1)S(1)}, bf16[2,320,128]{2,1,0:T(8,128)(2,1)S(1)}, u32[]{:S(2)}, u32[]{:S(2)}) collective-permute-start(bf16[2,320,128]{2,1,0:T(8,128)(2,1)S(1)} %get-tuple-element.37.send_b), channel_id=1, source_target_pairs={{0,112},{16,32},{32,16},{48,64},{64,48},{80,96},{96,80},{112,0},{1... | collective-permute-start | bytes 491528 | tf_op jit(solution)/shard_map/ppermute | solution.py:590
  25.6 26.1 %copy-start.1 = (bf16[16,32]{1,0:T(8,128)(2,1)S(1)}, bf16[16,32]{1,0:T(8,128)(2,1)}, u32[]{:S(2)}) copy-start(bf16[16,32]{1,0:T(8,128)(2,1)} %w_join.1) | copy-start | bytes 3076
  25.6 13.2 %all-to-all-start = ((f32[16,2,128]{2,1,0:T(2,128)}), f32[16,2,128]{2,1,0:T(2,128)S(1)}, u32[]{:S(2)}, u32[]{:S(2)}) async-start(f32[16,2,128]{2,1,0:T(2,128)} %get-tuple-element.44.after), calls=%async_computation | async-start | bytes 32768 | tf_op jit(solution)/shard_map/all_to_all | solution.py:621
  38.9 6.2 %collective-permute-start.4 = (f32[16,128]{1,0:T(8,128)S(1)}, f32[16,128]{1,0:T(8,128)S(1)}, u32[]{:S(2)}, u32[]{:S(2)}) collective-permute-start(f32[16,128]{1,0:T(8,128)S(1)} %bitcast.13), channel_id=1, source_target_pairs={{0,16},{16,32},{32,48},{48,64},{64,80},{80,96},{96,112},{112,0},{1... | collective-permute-start | bytes 24584 | tf_op jit(solution)/shard_map/ppermute | solution.py:631
  40.3 4.7 %collective-permute-start.5 = (f32[16,128]{1,0:T(8,128)S(1)}, f32[16,128]{1,0:T(8,128)S(1)}, u32[]{:S(2)}, u32[]{:S(2)}) collective-permute-start(f32[16,128]{1,0:T(8,128)S(1)} %bitcast.12), channel_id=1, source_target_pairs={{0,112},{16,0},{32,16},{48,32},{64,48},{80,64},{96,80},{112,96},{1... | collective-permute-start | bytes 24584 | tf_op jit(solution)/shard_map/ppermute | solution.py:632
  46.9 10.7 %all-to-all-start.1 = ((f32[16,2,128]{2,1,0:T(2,128)}), f32[16,2,128]{2,1,0:T(2,128)S(1)}, u32[]{:S(2)}, u32[]{:S(2)}) async-start(f32[16,2,128]{2,1,0:T(2,128)} %shard_map.81), calls=%async_computation.1 | async-start | bytes 32768 | tf_op jit(solution)/shard_map/all_to_all | solution.py:647

commit v6 on v5

--- a/solution.py
+++ b/solution.py
@@ -74,6 +74,9 @@
 
 
 def mix(a, b, flags):
+    for value, flag, other in ((a, *flags), (b, *flags[::-1])):
+        if isinstance(other, float) and other == 0.0:
+            return scaled(value, flag)
     return (a.astype(F32) * flags[0] + b.astype(F32) * flags[1]).astype(BF16)
 
 

time: 59.7 us -> 59.7 us (level)
  transfers between devices with their start and end apart: 8 -> 8, of which waited for: 6 -> 5; matrix products, arithmetic and copies ran while one was open for 1% -> 1% of each run, Pallas kernels for 20% -> 20%
where the time goes in v6:
time: 59.7 us; the launch traced here: 59.3 us
  starting transfers between devices  25.4 us (43%)
  Pallas kernels  19.5 us (33%)
  waiting for transfers between devices  13.7 us (23%)
    pallas_call x9, Pallas kernels, vmem_call(): pl.pallas_call(kernel, out_shape=out_shape, in_specs=[pl.BlockSpec(memory...  17.8 us
    all_to_all x1, starting transfers between devices, local(): own = lax.all_to_all(pooled, 'gy', 0, 0)  7.44 us
    all_to_all x1, waiting for transfers between devices, local(): parts = lax.all_to_all(parts, 'gy', 0, 0)  5.38 us
    all_to_all x1, starting transfers between devices, local(): parts = lax.all_to_all(parts, 'gy', 0, 0)  4.83 us
    all_to_all x1, waiting for transfers between devices, local(): own = lax.all_to_all(pooled, 'gy', 0, 0)  3.86 us
    ppermute x1, starting transfers between devices, local(): gr = lax.ppermute(own[:, 0, :], 'gx', ring(nx, -1))  3.67 us
    ppermute x1, starting transfers between devices, local(): got_a = lax.ppermute(send_a, 'gx', swap(nx, 0))  2.99 us
    ppermute x1, starting transfers between devices, local(): gy_a = lax.ppermute(gy_a, 'gy', ring(ny, 1))  2.74 us
  transfers between devices with their start and end apart: 8, of which 5 were waited for; matrix products, arithmetic and copies ran while one was open for 1% of the time, Pallas kernels for 20%

profile of v6, /device:TPU:1, one launch (start us, length us, event | category | flops | bytes accessed | tf_op | source)
XLA Modules:
  0.0 59.3 jit_solution(2357306902183759990)
XLA Ops:
  0.0 0.0 copy-start
  0.0 0.0 copy-start.3
  0.0 0.0 copy-start.2
  0.0 0.0 copy-start.4
  0.0 2.1 %shard_map.74 = (bf16[32,32,128]{2,1,0:T(8,128)(2,1)S(1)}, bf16[32,32,128]{2,1,0:T(8,128)(2,1)S(1)}) custom-call(bf16[16,32,16,128]{3,2,1,0:T(8,128)(2,1)} %far.3), custom_call_target="tpu_custom_call" | custom-call | flops 134217728 | bytes 3145728 | tf_op jit(solution)/shard_map/pallas_call | solution.py:38
  2.1 2.7 %collective-permute-start = (bf16[32,32,128]{2,1,0:T(8,128)(2,1)S(1)}, bf16[32,32,128]{2,1,0:T(8,128)(2,1)S(1)}, u32[]{:S(2)}, u32[]{:S(2)}) collective-permute-start(bf16[32,32,128]{2,1,0:T(8,128)(2,1)S(1)} %get-tuple-element.29), channel_id=1, source_target_pairs={{0,1},{1,2},{2,3},{3,4},{4,5},{5,6},{6,7},{7,8},{8,9},{9,10},{10,1... | collective-permute-start | bytes 786440 | tf_op jit(solution)/shard_map/ppermute | solution.py:558
  4.9 0.0 collective-permute-start.1
  4.9 0.0 copy-done.3
  4.9 0.0 copy-done.2
  4.9 0.1 pad_maximum_fusion
  5.0 0.3 copy.12
  5.3 0.0 copy-done.4
  5.3 0.1 copy.13.w_lift
  5.4 0.0 copy-done
  5.4 0.1 constant_dynamic-slice_fusion.w_dec
  5.5 5.4 %shard_map.73 = (bf16[14,224,128]{2,1,0:T(8,128)(2,1)S(1)}, bf16[16,224,128]{2,1,0:T(8,128)(2,1)}, bf16[2,32,32,128]{3,2,1,0:T(8,128)(2,1)S(1)}, bf16[2,2,256,12...) custom-call(bf16[16,32,16,128]{3,2,1,0:T(8,128)(2,1)} %far.3, ...), custom_call_target="tpu_custom_call" | custom-call | flops 1761607680 | bytes 4194304 | tf_op jit(solution)/shard_map/pallas_call | solution.py:38
  10.9 0.0 collective-permute-done.gy_a
  10.9 2.1 %collective-permute-done.1.gy_b = bf16[32,32,128]{2,1,0:T(8,128)(2,1)S(1)} collective-permute-done((bf16[32,32,128]{2,1,0:T(8,128)(2,1)S(1)}, bf16[32,32,128]{2,1,0:T(8,128)(2,1)S(1)}, u32[]{:S(2)}, u32[]{:S(2)}) %collective-permute-start.1) | collective-permute-done | bytes 262176 | tf_op jit(solution)/shard_map/ppermute | solution.py:559
  13.0 3.0 %collective-permute-start.2 = (bf16[2,320,128]{2,1,0:T(8,128)(2,1)S(1)}, bf16[2,320,128]{2,1,0:T(8,128)(2,1)S(1)}, u32[]{:S(2)}, u32[]{:S(2)}) collective-permute-start(bf16[2,320,128]{2,1,0:T(8,128)(2,1)S(1)} %get-tuple-element.36.send_a), channel_id=1, source_target_pairs={{0,16},{16,0},{32,48},{48,32},{64,80},{80,64},{96,112},{112,96},{1... | collective-permute-start | bytes 491528 | tf_op jit(solution)/shard_map/ppermute | solution.py:592
  16.0 2.3 %collective-permute-start.3 = (bf16[2,320,128]{2,1,0:T(8,128)(2,1)S(1)}, bf16[2,320,128]{2,1,0:T(8,128)(2,1)S(1)}, u32[]{:S(2)}, u32[]{:S(2)}) collective-permute-start(bf16[2,320,128]{2,1,0:T(8,128)(2,1)S(1)} %get-tuple-element.37.send_b), channel_id=1, source_target_pairs={{0,112},{16,32},{32,16},{48,64},{64,48},{80,96},{96,80},{112,0},{1... | collective-permute-start | bytes 491528 | tf_op jit(solution)/shard_map/ppermute | solution.py:593
  18.3 3.2 %shard_map.75 = (bf16[28,256,128]{2,1,0:T(8,128)(2,1)S(1)}, bf16[4,288,128]{2,1,0:T(8,128)(2,1)S(1)}, f32[2,16,128]{2,1,0:T(8,128)S(1)}) custom-call(bf16[14,224,128]{2,1,0:T(8,128)(2,1)S(1)} %get-tuple-element.26.low, bf16[16,224,128]{2,1,0:T(8,128)(2,1)} %get-tuple-element.27.high_far, bf16[2,32,32,128]{3,2,1,0:T(8,128)(2,1)S(1)} %get-tuple-element.28.rims, ...), custom_call_target="tpu_custom_call" | custom-call | flops 1786773504 | bytes 6291456 | tf_op jit(solution)/shard_map/pallas_call | solution.py:38
  21.5 1.0 %collective-permute-done.2.got_a = bf16[2,320,128]{2,1,0:T(8,128)(2,1)S(1)} collective-permute-done((bf16[2,320,128]{2,1,0:T(8,128)(2,1)S(1)}, bf16[2,320,128]{2,1,0:T(8,128)(2,1)S(1)}, u32[]{:S(2)}, u32[]{:S(2)}) %collective-permute-start.2) | collective-permute-done | bytes 163872 | tf_op jit(solution)/shard_map/ppermute | solution.py:592
  22.4 1.3 %collective-permute-done.3.got_b = bf16[2,320,128]{2,1,0:T(8,128)(2,1)S(1)} collective-permute-done((bf16[2,320,128]{2,1,0:T(8,128)(2,1)S(1)}, bf16[2,320,128]{2,1,0:T(8,128)(2,1)S(1)}, u32[]{:S(2)}, u32[]{:S(2)}) %collective-permute-start.3) | collective-permute-done | bytes 163872 | tf_op jit(solution)/shard_map/ppermute | solution.py:593
  23.8 1.8 %shard_map.77 = (bf16[16,256,128]{2,1,0:T(8,128)(2,1)S(1)}, bf16[16,256,128]{2,1,0:T(8,128)(2,1)S(1)}, f32[16,2,128]{2,1,0:T(2,128)}) custom-call(bf16[28,256,128]{2,1,0:T(8,128)(2,1)S(1)} %get-tuple-element.33.inner, bf16[4,288,128]{2,1,0:T(8,128)(2,1)S(1)} %get-tuple-element.34.f1_ends, bf16[2,320,128]{2,1,0:T(8,128)(2,1)S(1)} %get-tuple-element.36.send_a, ...), custom_call_target="tpu_custom_call" | custom-call | flops 427819008 | bytes 1048576 | tf_op jit(solution)/shard_map/pallas_call | solution.py:38
  25.6 0.0 copy-start.1
  25.6 7.4 %all-to-all-start = ((f32[16,2,128]{2,1,0:T(2,128)}), f32[16,2,128]{2,1,0:T(2,128)S(1)}, u32[]{:S(2)}, u32[]{:S(2)}) async-start(f32[16,2,128]{2,1,0:T(2,128)} %get-tuple-element.44.after), calls=%async_computation | async-start | bytes 32768 | tf_op jit(solution)/shard_map/all_to_all | solution.py:624
  33.0 1.9 %shard_map.79 = (bf16[864,512]{1,0:T(8,128)(2,1)S(1)}, bf16[512,48]{1,0:T(8,128)(2,1)S(1)}) custom-call(bf16[864,512]{1,0:T(8,128)(2,1)} %bitcast.11, bf16[512,16]{1,0:T(8,128)(2,1)S(1)} %copy.13.w_lift, f32[16,2,128]{2,1,0:T(2,128)} %get-tuple-element.44.after), custom_call_target="tpu_custom_call" | custom-call | flops 268435456 | bytes 4194304 | tf_op jit(solution)/shard_map/pallas_call | solution.py:38
  35.0 3.9 %all-to-all-done.own = f32[16,2,128]{2,1,0:T(2,128)S(1)} async-done(((f32[16,2,128]{2,1,0:T(2,128)}), f32[16,2,128]{2,1,0:T(2,128)S(1)}, u32[]{:S(2)}, u32[]{:S(2)}) %all-to-all-start) | async-done | bytes 16416 | tf_op jit(solution)/shard_map/all_to_all | solution.py:624
  38.9 1.5 %collective-permute-start.4 = (f32[16,128]{1,0:T(8,128)S(1)}, f32[16,128]{1,0:T(8,128)S(1)}, u32[]{:S(2)}, u32[]{:S(2)}) collective-permute-start(f32[16,128]{1,0:T(8,128)S(1)} %bitcast.13), channel_id=1, source_target_pairs={{0,16},{16,32},{32,48},{48,64},{64,80},{80,96},{96,112},{112,0},{1... | collective-permute-start | bytes 24584 | tf_op jit(solution)/shard_map/ppermute | solution.py:634
  40.3 3.7 %collective-permute-start.5 = (f32[16,128]{1,0:T(8,128)S(1)}, f32[16,128]{1,0:T(8,128)S(1)}, u32[]{:S(2)}, u32[]{:S(2)}) collective-permute-start(f32[16,128]{1,0:T(8,128)S(1)} %bitcast.12), channel_id=1, source_target_pairs={{0,112},{16,0},{32,16},{48,32},{64,48},{80,64},{96,80},{112,96},{1... | collective-permute-start | bytes 24584 | tf_op jit(solution)/shard_map/ppermute | solution.py:635
  44.0 1.0 %shard_map.80.mine = f32[2,32,128]{2,1,0:T(8,128)S(1)} custom-call(f32[16,2,128]{2,1,0:T(2,128)S(1)} %all-to-all-done.own, bf16[512,48]{1,0:T(8,128)(2,1)S(1)} %get-tuple-element.45.w_lift, bf16[864,512]{1,0:T(8,128)(2,1)S(1)} %get-tuple-element.46.w_coarse), custom_call_target="tpu_custom_call" | custom-call | flops 452984832 | bytes 2097152 | tf_op jit(solution)/shard_map/pallas_call | solution.py:38
  45.0 0.0 collective-permute-done.4.gl
  45.0 0.0 collective-permute-done.5.gr
  45.0 1.8 %shard_map.81 = f32[16,2,128]{2,1,0:T(2,128)} custom-call(f32[2,32,128]{2,1,0:T(8,128)S(1)} %shard_map.80.mine, f32[16,128]{1,0:T(8,128)S(1)} %collective-permute-done.4.gl, f32[16,128]{1,0:T(8,128)S(1)} %collective-permute-done.5.gr, bf16[512,48]{1,0:T(8,128)(2,1)S(1)} %get-tuple-element.45.w_lift, bf16[864,512]{1,0:T(8,128)(2,1)S(1)} %get-tuple-element.46.w_coarse, ...), custom_call_target="tpu_custom_call" | custom-call | flops 226492416 | bytes 2097152 | tf_op jit(solution)/shard_map/pallas_call | solution.py:38
  46.9 4.8 %all-to-all-start.1 = ((f32[16,2,128]{2,1,0:T(2,128)}), f32[16,2,128]{2,1,0:T(2,128)S(1)}, u32[]{:S(2)}, u32[]{:S(2)}) async-start(f32[16,2,128]{2,1,0:T(2,128)} %shard_map.81), calls=%async_computation.1 | async-start | bytes 32768 | tf_op jit(solution)/shard_map/all_to_all | solution.py:650
  51.7 0.0 copy-done.1
  51.7 0.5 shard_map.78
  52.2 5.4 %all-to-all-done.1.parts = f32[16,2,128]{2,1,0:T(2,128)S(1)} async-done(((f32[16,2,128]{2,1,0:T(2,128)}), f32[16,2,128]{2,1,0:T(2,128)S(1)}, u32[]{:S(2)}, u32[]{:S(2)}) %all-to-all-start.1) | async-done | bytes 16416 | tf_op jit(solution)/shard_map/all_to_all | solution.py:650
  57.6 1.7 %shard_map.82 = bf16[16,32,16,128]{3,2,1,0:T(8,128)(2,1)} custom-call(bf16[16,256,128]{2,1,0:T(8,128)(2,1)S(1)} %get-tuple-element.39.second.left, bf16[16,256,128]{2,1,0:T(8,128)(2,1)S(1)} %get-tuple-element.40.right, f32[4,256,128]{2,1,0:T(8,128)S(1)} %get-tuple-element.41.ahead, bf16[256,256]{1,0:T(8,128)(2,1)S(1)} %get-tuple-element.42.matrix, ...), custom_call_target="tpu_custom_call" | custom-call | flops 536870912 | bytes 4194304 | tf_op jit(solution)/shard_map/pallas_call | solution.py:522
  (2 shorter events, 0.0 us)
Async XLA Ops:
  0.0 5.4 %copy-start = (bf16[16,512]{1,0:T(8,128)(2,1)S(1)}, bf16[16,512]{1,0:T(8,128)(2,1)}, u32[]{:S(2)}) copy-start(bf16[16,512]{1,0:T(8,128)(2,1)} %param.12) | copy-start | bytes 49156
  0.0 4.9 %copy-start.3 = (bf16[27,16,16]{0,2,1:T(8,128)(2,1)S(1)}, bf16[27,16,16]{0,2,1:T(8,128)(2,1)}, u32[]{:S(2)}) copy-start(bf16[27,16,16]{0,2,1:T(8,128)(2,1)} %param.8) | copy-start | bytes 41476
  0.0 4.9 %copy-start.2 = (bf16[27,16,16]{0,2,1:T(8,128)(2,1)S(1)}, bf16[27,16,16]{0,2,1:T(8,128)(2,1)}, u32[]{:S(2)}) copy-start(bf16[27,16,16]{0,2,1:T(8,128)(2,1)} %param.9) | copy-start | bytes 41476
  0.0 5.3 %copy-start.4 = (bf16[512,16]{0,1:T(8,128)(2,1)S(1)}, bf16[512,16]{0,1:T(8,128)(2,1)}, u32[]{:S(2)}) copy-start(bf16[512,16]{0,1:T(8,128)(2,1)} %param.10) | copy-start | bytes 49156
  2.1 8.8 %collective-permute-start = (bf16[32,32,128]{2,1,0:T(8,128)(2,1)S(1)}, bf16[32,32,128]{2,1,0:T(8,128)(2,1)S(1)}, u32[]{:S(2)}, u32[]{:S(2)}) collective-permute-start(bf16[32,32,128]{2,1,0:T(8,128)(2,1)S(1)} %get-tuple-element.29), channel_id=1, source_target_pairs={{0,1},{1,2},{2,3},{3,4},{4,5},{5,6},{6,7},{7,8},{8,9},{9,10},{10,1... | collective-permute-start | bytes 786440 | tf_op jit(solution)/shard_map/ppermute | solution.py:558
  4.9 8.1 %collective-permute-start.1 = (bf16[32,32,128]{2,1,0:T(8,128)(2,1)S(1)}, bf16[32,32,128]{2,1,0:T(8,128)(2,1)S(1)}, u32[]{:S(2)}, u32[]{:S(2)}) collective-permute-start(bf16[32,32,128]{2,1,0:T(8,128)(2,1)S(1)} %get-tuple-element.30), channel_id=1, source_target_pairs={{0,15},{1,0},{2,1},{3,2},{4,3},{5,4},{6,5},{7,6},{8,7},{9,8},{10,9... | collective-permute-start | bytes 786440 | tf_op jit(solution)/shard_map/ppermute | solution.py:559
  13.0 9.4 %collective-permute-start.2 = (bf16[2,320,128]{2,1,0:T(8,128)(2,1)S(1)}, bf16[2,320,128]{2,1,0:T(8,128)(2,1)S(1)}, u32[]{:S(2)}, u32[]{:S(2)}) collective-permute-start(bf16[2,320,128]{2,1,0:T(8,128)(2,1)S(1)} %get-tuple-element.36.send_a), channel_id=1, source_target_pairs={{0,16},{16,0},{32,48},{48,32},{64,80},{80,64},{96,112},{112,96},{1... | collective-permute-start | bytes 491528 | tf_op jit(solution)/shard_map/ppermute | solution.py:592
  16.0 7.8 %collective-permute-start.3 = (bf16[2,320,128]{2,1,0:T(8,128)(2,1)S(1)}, bf16[2,320,128]{2,1,0:T(8,128)(2,1)S(1)}, u32[]{:S(2)}, u32[]{:S(2)}) collective-permute-start(bf16[2,320,128]{2,1,0:T(8,128)(2,1)S(1)} %get-tuple-element.37.send_b), channel_id=1, source_target_pairs={{0,112},{16,32},{32,16},{48,64},{64,48},{80,96},{96,80},{112,0},{1... | collective-permute-start | bytes 491528 | tf_op jit(solution)/shard_map/ppermute | solution.py:593
  25.6 26.1 %copy-start.1 = (bf16[16,32]{1,0:T(8,128)(2,1)S(1)}, bf16[16,32]{1,0:T(8,128)(2,1)}, u32[]{:S(2)}) copy-start(bf16[16,32]{1,0:T(8,128)(2,1)} %w_join.1) | copy-start | bytes 3076
  25.6 13.2 %all-to-all-start = ((f32[16,2,128]{2,1,0:T(2,128)}), f32[16,2,128]{2,1,0:T(2,128)S(1)}, u32[]{:S(2)}, u32[]{:S(2)}) async-start(f32[16,2,128]{2,1,0:T(2,128)} %get-tuple-element.44.after), calls=%async_computation | async-start | bytes 32768 | tf_op jit(solution)/shard_map/all_to_all | solution.py:624
  38.9 6.2 %collective-permute-start.4 = (f32[16,128]{1,0:T(8,128)S(1)}, f32[16,128]{1,0:T(8,128)S(1)}, u32[]{:S(2)}, u32[]{:S(2)}) collective-permute-start(f32[16,128]{1,0:T(8,128)S(1)} %bitcast.13), channel_id=1, source_target_pairs={{0,16},{16,32},{32,48},{48,64},{64,80},{80,96},{96,112},{112,0},{1... | collective-permute-start | bytes 24584 | tf_op jit(solution)/shard_map/ppermute | solution.py:634
  40.3 4.7 %collective-permute-start.5 = (f32[16,128]{1,0:T(8,128)S(1)}, f32[16,128]{1,0:T(8,128)S(1)}, u32[]{:S(2)}, u32[]{:S(2)}) collective-permute-start(f32[16,128]{1,0:T(8,128)S(1)} %bitcast.12), channel_id=1, source_target_pairs={{0,112},{16,0},{32,16},{48,32},{64,48},{80,64},{96,80},{112,96},{1... | collective-permute-start | bytes 24584 | tf_op jit(solution)/shard_map/ppermute | solution.py:635
  46.9 10.7 %all-to-all-start.1 = ((f32[16,2,128]{2,1,0:T(2,128)}), f32[16,2,128]{2,1,0:T(2,128)S(1)}, u32[]{:S(2)}, u32[]{:S(2)}) async-start(f32[16,2,128]{2,1,0:T(2,128)} %shard_map.81), calls=%async_computation.1 | async-start | bytes 32768 | tf_op jit(solution)/shard_map/all_to_all | solution.py:650
